TPU v7x, 32 devices: a whole 2x2x4 slice. The times are simulated.
32 devices in a mesh: row: 8 (over z, y), col: 4 (over x, core).
Axes of the slice: x: 2, y: 2, z: 4, core: 2. Of those that a mesh axis runs over, the one named last changes fastest.
Arguments:
- hidden_in: bfloat16 [16384, 1024], P(('row', 'col')), may hold values from -6 to 6
- teacher: float32 [16384, 1024], P(('row', 'col')), may hold values from -6 to 6
- valid_mask: int32 [16384], replicated, may hold values from 0 to 1, as said below
- first_gain: float32 [1024], replicated, may hold values from 0.1 to 1.9
- second_gain: float32 [1024], replicated, may hold values from 0.1 to 1.9
- attention_in: bfloat16 [3, 1024, 1024], P(None, 'col', 'row'), may hold values from -0.1875 to 0.1875
- attention_out: bfloat16 [1024, 1024], P('row', 'col'), may hold values from -6 to 6
- feed_in: bfloat16 [2, 2624, 1024], P(None, 'col', 'row'), may hold values from -0.1875 to 0.1875
- feed_out: bfloat16 [1024, 2624], P('row', 'col'), may hold values from -0.125 to 0.125
Outputs:
- layer_out: bfloat16 [16384, 1024], P(('row', 'col'))
- loss: float32 [], replicated
- grad_input: float32 [16384, 1024], P(('row', 'col'))
- grad_first_gain: float32 [1024], replicated
- grad_second_gain: float32 [1024], replicated
- grad_attention_in: float32 [3, 1024, 1024], P(None, 'col', 'row')
- grad_attention_out: float32 [1024, 1024], P('row', 'col')
- grad_feed_in: float32 [2, 2624, 1024], P(None, 'col', 'row')
- grad_feed_out: float32 [1024, 2624], P('row', 'col')
Inputs may be any that keep to these rules, and one draw needn't show every extreme that they name: `valid_mask`: 1 marks a token that serves as a key and counts in the loss; the first token of every sequence of 2048 is 1.
All inputs are finite; a program needn't handle non-finite values.
Results may differ from a plain program's by a relative error of at most 0.012.
Values may be sent and summed in bfloat16 or wider, within the bound.
No kernel may reach another device: no remote copies, remote signals or barrier semaphores. Data moves between devices by JAX's collectives and lax.ppermute only.
A program may use at most 256 MiB of HBM per device.

v0:
```python
import functools

import jax
import jax.numpy as jnp
from jax import lax
from jax.experimental import pallas as pl
from jax.experimental.pallas import tpu as pltpu
from jax.sharding import PartitionSpec as P

D = 1024
HD = 64
SEQ_LEN = 2048


EPSILON = 1e-05
ROPE_BASE = 160000.0
FLOOR_SCORE = -1e30


def layer_norm(values, gain):
    center = values - jnp.mean(values, axis=1, keepdims=True)
    inverse = lax.rsqrt(jnp.mean(center * center, axis=1, keepdims=True) + EPSILON)
    normed = center * inverse
    return (normed, inverse, (normed * gain).astype(jnp.bfloat16))


def norm_back(grad_low, normed, inverse, gain):
    scaled = grad_low * gain
    inner = jnp.mean(scaled * normed, axis=1, keepdims=True)
    centered = scaled - jnp.mean(scaled, axis=1, keepdims=True)
    return (inverse * (centered - normed * inner), jnp.sum(grad_low * normed, axis=0))


def rotary_tables(rows, width):
    half = width // 2
    frequency = ROPE_BASE ** (-(jnp.arange(half, dtype=jnp.float32) * 2.0) / width)
    place = (jnp.arange(rows, dtype=jnp.int32) % SEQ_LEN).astype(jnp.float32)
    angle = place[:, None] * frequency[None, :]
    angle = jnp.concatenate([angle, angle], axis=1)
    return (jnp.cos(angle), jnp.sin(angle))


def rotate(values, cosine, sine):
    half = values.shape[-1] // 2
    turned = jnp.concatenate([-values[..., half:], values[..., :half]], axis=-1)
    return values * cosine[:, None, :] + turned * sine[:, None, :]


def rotate_back(grads, cosine, sine):
    half = grads.shape[-1] // 2
    moved = grads * sine[:, None, :]
    turned = jnp.concatenate([moved[..., half:], -moved[..., :half]], axis=-1)
    return grads * cosine[:, None, :] + turned


def block_scores(query, keys, live, start, block):
    base = start // SEQ_LEN * SEQ_LEN
    picked = lax.dynamic_slice_in_dim(query, start, block, 0)
    window = lax.dynamic_slice_in_dim(keys, base, SEQ_LEN, 0)
    allowed = lax.dynamic_slice_in_dim(live, base, SEQ_LEN, 0)
    scores = jnp.einsum(
        "qhd,khd->hqk", picked, window, preferred_element_type=jnp.float32
    ) * query.shape[2] ** (-0.5)
    return (jnp.where(allowed[None, None, :] > 0, scores, FLOOR_SCORE), picked, window, base)


def attend(query, keys, values, live):
    rows, heads, width = query.shape
    block = min(512, SEQ_LEN)

    def one_block(index):
        start = index * block
        scores, _, _, base = block_scores(query, keys, live, start, block)
        seq_values = lax.dynamic_slice_in_dim(values, base, SEQ_LEN, 0)
        top = jnp.max(scores, axis=2, keepdims=True)
        weights = jnp.exp(scores - top)
        total = jnp.sum(weights, axis=2, keepdims=True)
        probs = (weights / total).astype(jnp.bfloat16)
        mixed = jnp.einsum("hqk,khd->qhd", probs, seq_values, preferred_element_type=jnp.float32)
        return (mixed.astype(jnp.bfloat16), (top + jnp.log(total))[:, :, 0])

    mixed, log_total = lax.map(one_block, jnp.arange(rows // block, dtype=jnp.int32))
    return (mixed.reshape(rows, heads * width), log_total)


def attend_back(query, keys, values, live, log_total, grad_mixed):
    rows, heads, width = query.shape
    block = min(512, SEQ_LEN)
    scale = width ** (-0.5)
    zeros = jnp.zeros((rows, heads, width), jnp.float32)

    def one_block(index, carry):
        grad_query, grad_keys, grad_values = carry
        start = index * block
        scores, picked, window, base = block_scores(query, keys, live, start, block)
        probs = jnp.exp(scores - log_total[index][:, :, None])
        seq_values = lax.dynamic_slice_in_dim(values, base, SEQ_LEN, 0)
        grad_block = lax.dynamic_slice_in_dim(grad_mixed, start, block, 0)
        grad_probs = jnp.einsum(
            "qhd,khd->hqk", grad_block, seq_values, preferred_element_type=jnp.float32
        )
        inner = jnp.sum(probs * grad_probs, axis=2, keepdims=True)
        grad_scores = (probs * (grad_probs - inner)).astype(jnp.bfloat16)
        part_query = (
            jnp.einsum("hqk,khd->qhd", grad_scores, window, preferred_element_type=jnp.float32)
            * scale
        )
        part_keys = (
            jnp.einsum("hqk,qhd->khd", grad_scores, picked, preferred_element_type=jnp.float32)
            * scale
        )
        part_values = jnp.einsum(
            "hqk,qhd->khd",
            probs.astype(jnp.bfloat16),
            grad_block,
            preferred_element_type=jnp.float32,
        )
        grad_query = lax.dynamic_update_slice_in_dim(grad_query, part_query, start, 0)
        grad_keys = lax.dynamic_update_slice_in_dim(
            grad_keys, lax.dynamic_slice_in_dim(grad_keys, base, SEQ_LEN, 0) + part_keys, base, 0
        )
        grad_values = lax.dynamic_update_slice_in_dim(
            grad_values,
            lax.dynamic_slice_in_dim(grad_values, base, SEQ_LEN, 0) + part_values,
            base,
            0,
        )
        return (grad_query, grad_keys, grad_values)

    return lax.fori_loop(0, rows // block, one_block, (zeros, zeros, zeros))


def general_shards(
    hidden_in,
    teacher,
    valid_mask,
    first_gain,
    second_gain,
    attention_in,
    attention_out,
    feed_in,
    feed_out,
):
    columns = lax.axis_size("col")
    own_rows = hidden_in.shape[0]
    group = own_rows * columns
    own_start = lax.axis_index("col") * own_rows
    group_start = lax.axis_index("row") * group
    total_tokens = group * lax.axis_size("row")
    live_group = lax.dynamic_slice_in_dim(valid_mask, group_start, group, 0)
    live_own = lax.dynamic_slice_in_dim(live_group, own_start, own_rows, 0).astype(jnp.float32)
    valid_total = jnp.sum(valid_mask.astype(jnp.float32))
    joint_rows, attention_rows, feed_in_rows, feed_out_rows = (
        lax.all_gather(attention_in, "row", axis=2, tiled=True),
        lax.all_gather(attention_out, "row", axis=0, tiled=True),
        lax.all_gather(feed_in, "row", axis=2, tiled=True),
        lax.all_gather(feed_out, "row", axis=0, tiled=True),
    )
    inputs = hidden_in.astype(jnp.float32)
    normed_one, inverse_one, low_one = layer_norm(inputs, first_gain)
    joint = jnp.einsum(
        "rd,icd->ric",
        lax.all_gather(low_one, "col", axis=0, tiled=True),
        joint_rows,
        preferred_element_type=jnp.float32,
    )
    local_width = joint.shape[2]
    split = (group, local_width // HD, HD)
    cosine, sine = rotary_tables(group, HD)
    query = rotate(joint[:, 0].reshape(split), cosine, sine).astype(jnp.bfloat16)
    keys = rotate(joint[:, 1].reshape(split), cosine, sine).astype(jnp.bfloat16)
    values = joint[:, 2].reshape(split).astype(jnp.bfloat16)
    mixed, log_total = attend(query, keys, values, live_group)
    part = mixed
    branch = lax.psum_scatter(
        jnp.einsum("rc,oc->ro", part, attention_rows, preferred_element_type=jnp.float32),
        "col",
        scatter_dimension=0,
        tiled=True,
    )
    middle = inputs + branch
    normed_two, inverse_two, low_two = layer_norm(middle, second_gain)
    projected = jnp.einsum(
        "rd,ifd->rif",
        lax.all_gather(low_two, "col", axis=0, tiled=True),
        feed_in_rows,
        preferred_element_type=jnp.float32,
    )
    gate = projected[:, 0]
    upper = projected[:, 1]
    activated = (jax.nn.gelu(gate, approximate=False) * upper).astype(jnp.bfloat16)
    part = activated
    feed_branch = lax.psum_scatter(
        jnp.einsum("rf,of->ro", part, feed_out_rows, preferred_element_type=jnp.float32),
        "col",
        scatter_dimension=0,
        tiled=True,
    )
    result = middle + feed_branch
    error_term = result - teacher
    squares = jnp.sum(live_own * jnp.sum(error_term * error_term, axis=1))
    grad_result = (total_tokens * live_own)[:, None] * error_term / valid_total
    grad_low = grad_result.astype(jnp.bfloat16)
    piece = lax.all_gather(grad_low, "col", axis=0, tiled=True)
    part = activated
    grad_out = jnp.einsum("ro,rf->of", piece, part, preferred_element_type=jnp.float32)
    rows_grad = jnp.einsum("ro,of->rf", piece, feed_out_rows, preferred_element_type=jnp.float32)
    grad_act = rows_grad

    def geglu(first, second):
        return jax.nn.gelu(first, approximate=False) * second

    _, pull = jax.vjp(geglu, gate, upper)
    grad_gate, grad_upper = pull(grad_act)
    grad_projected = jnp.stack([grad_gate, grad_upper], axis=1).astype(jnp.bfloat16)
    part = grad_projected
    grad_low_two = lax.psum_scatter(
        jnp.einsum("rif,ifd->rd", part, feed_in_rows, preferred_element_type=jnp.float32),
        "col",
        scatter_dimension=0,
        tiled=True,
    )
    grad_middle_norm, grad_second = norm_back(grad_low_two, normed_two, inverse_two, second_gain)
    grad_middle = grad_result + grad_middle_norm
    grad_branch = grad_middle.astype(jnp.bfloat16)
    piece = lax.all_gather(grad_branch, "col", axis=0, tiled=True)
    part = mixed
    grad_weight = jnp.einsum("ro,rc->oc", piece, part, preferred_element_type=jnp.float32)
    rows_grad = jnp.einsum("ro,oc->rc", piece, attention_rows, preferred_element_type=jnp.float32)
    grad_heads = rows_grad
    grad_attention_rows, grad_heads = (grad_weight, grad_heads)
    grad_mixed = grad_heads.astype(jnp.bfloat16)
    grad_query, grad_keys, grad_values = attend_back(
        query, keys, values, live_group, log_total, grad_mixed.reshape(split)
    )
    grad_joint = jnp.stack(
        [rotate_back(grad_query, cosine, sine), rotate_back(grad_keys, cosine, sine), grad_values],
        axis=1,
    )
    grad_joint = grad_joint.astype(jnp.bfloat16).reshape(group, 3, local_width)
    part = grad_joint
    grad_low_one = lax.psum_scatter(
        jnp.einsum("ric,icd->rd", part, joint_rows, preferred_element_type=jnp.float32).astype(
            jnp.bfloat16
        ),
        "col",
        scatter_dimension=0,
        tiled=True,
    ).astype(jnp.float32)
    grad_input_norm, grad_first = norm_back(grad_low_one, normed_one, inverse_one, first_gain)
    grad_input = grad_middle + grad_input_norm
    grad_joint_weight = jnp.einsum(
        "ric,rd->icd",
        grad_joint,
        lax.all_gather(low_one, "col", axis=0, tiled=True),
        preferred_element_type=jnp.float32,
    )
    grad_feed_weight = jnp.einsum(
        "rif,rd->ifd",
        grad_projected,
        lax.all_gather(low_two, "col", axis=0, tiled=True),
        preferred_element_type=jnp.float32,
    )
    grads = (
        lax.psum_scatter(
            grad_joint_weight.astype(jnp.bfloat16), "row", scatter_dimension=2, tiled=True
        ).astype(jnp.float32),
        lax.psum_scatter(
            grad_attention_rows.astype(jnp.bfloat16), "row", scatter_dimension=0, tiled=True
        ).astype(jnp.float32),
        lax.psum_scatter(
            grad_feed_weight.astype(jnp.bfloat16), "row", scatter_dimension=2, tiled=True
        ).astype(jnp.float32),
        lax.psum_scatter(
            grad_out.astype(jnp.bfloat16), "row", scatter_dimension=0, tiled=True
        ).astype(jnp.float32),
    )
    totals = lax.psum((grad_first, grad_second, squares), ("row", "col"))
    loss = totals[2] / (D * valid_total)
    return (
        result.astype(jnp.bfloat16),
        loss,
        grad_input,
        totals[0],
        totals[1],
        grads[0],
        grads[1],
        grads[2],
        grads[3],
    )


BF = jnp.bfloat16
F32 = jnp.float32
MASKED = -1e30
ROW_DIMS = (((1,), (1,)), ((), ()))
HEAD_DIMS = (((0,), (0,)), ((), ()))
PLAIN_DIMS = (((1,), (0,)), ((), ()))


def swap(values, axis, flip):
    size = lax.axis_size(axis)
    return lax.ppermute(values, axis, [(place, place ^ flip) for place in range(size)])


def row_blocks(block):
    parts = [block] + [swap(block, "row", 2 * step) for step in range(1, 4)]
    blocks = []
    for part in parts:
        blocks += [part, swap(part, "row", 1)]
    return blocks, parts


def dot(left, right, dims):
    return lax.dot_general(left, right, dims, preferred_element_type=F32)


def turn(values, cosine, sine):
    lane = lax.broadcasted_iota(jnp.int32, values.shape, 1)
    swapped = jnp.where(
        lane % HD < HD // 2, pltpu.roll(values, 2 * HD - HD // 2, 1), pltpu.roll(values, HD // 2, 1)
    )
    return values * cosine + swapped * sine


def tables(inner, outer, start):
    cos_in, sin_in = inner[0], inner[1]
    cos_out = outer[0, pl.ds(start, 1)]
    sin_out = outer[1, pl.ds(start, 1)]
    lane = lax.broadcasted_iota(jnp.int32, cos_in.shape, 1)
    sign = jnp.where(lane % HD < HD // 2, -1.0, 1.0)
    cosine = cos_in * cos_out - sin_in * sin_out
    return cosine, (sin_in * cos_out + cos_in * sin_out) * sign


def project_kernel(row_ref, x0, x1, x2, x3, *rest):
    weights = rest[:8]
    inner, outer, bias_ref, tokens, joint, query, keys, values = rest[8:]
    step = pl.program_id(0)
    row = row_ref[0]
    pairs = joint.shape[0] // 384

    @pl.when(step == 0)
    def _():
        for index, weight in enumerate(weights):
            start = pl.multiple_of((row ^ index) * 128, 128)
            for pair in range(pairs):
                for kind in range(3):
                    at = (3 * pair + kind) * 128
                    old = (kind * pairs + pair) * 128
                    joint[at : at + 128, pl.ds(start, 128)] = weight[old : old + 128]

    for index, source in enumerate((x0, x1, x2, x3)):

        @pl.when(step == index)
        def _(source=source):
            tokens[...] = source[...]

    result = dot(tokens[...], joint[...], ROW_DIMS)
    cosine, sine = tables(inner, outer, step)
    rows = result.shape[0]
    lane = lax.broadcasted_iota(jnp.int32, (rows, 128), 1)
    spare = lane % HD
    one = jnp.ones((rows, 128), F32)
    zero = jnp.zeros((rows, 128), F32)
    key_spare = jnp.where(spare == 0, bias_ref[...] * one, jnp.where(spare <= 3, one, zero))
    query_spare = jnp.where(spare == 0, one, zero)
    for pair in range(pairs):
        at = pair * 384
        q = turn(result[:, at : at + 128], cosine, sine) * HD**-0.5
        k = turn(result[:, at + 128 : at + 256], cosine, sine)
        v = result[:, at + 256 : at + 384]
        for side in range(2):
            mine = (lane < HD) if side == 0 else (lane >= HD)
            query[2 * pair + side] = jnp.where(mine, q, query_spare).astype(BF)
            keys[2 * pair + side] = jnp.where(mine, k, key_spare).astype(BF)
            values[2 * pair + side] = jnp.where(mine, v, one).astype(BF)


def project(row, tokens, weights, inner, outer, bias):
    rows = tokens[0].shape[0]
    total = rows * len(tokens)
    width = weights[0].shape[0]
    heads = width // 3 // HD
    whole = lambda array: pl.BlockSpec(array.shape, lambda i, r: (0,) * array.ndim)
    wide = pl.BlockSpec((heads, rows, 128), lambda i, r: (0, i, 0))
    joint_shape = jax.ShapeDtypeStruct((width, D), BF)
    head_shape = jax.ShapeDtypeStruct((heads, total, 128), BF)
    return pl.pallas_call(
        project_kernel,
        out_shape=(
            jax.ShapeDtypeStruct((total, D), BF),
            joint_shape,
            head_shape,
            head_shape,
            head_shape,
        ),
        grid_spec=pltpu.PrefetchScalarGridSpec(
            num_scalar_prefetch=1,
            grid=(len(tokens),),
            in_specs=[whole(t) for t in tokens]
            + [whole(w) for w in weights]
            + [whole(inner), whole(outer), pl.BlockSpec((rows, 1), lambda i, r: (i, 0))],
            out_specs=(
                pl.BlockSpec((rows, D), lambda i, r: (i, 0)),
                pl.BlockSpec((width, D), lambda i, r: (0, 0)),
                wide,
                wide,
                wide,
            ),
        ),
        cost_estimate=pl.CostEstimate(
            flops=2 * total * width * D, transcendentals=0, bytes_accessed=8 * total * D
        ),
        name="project",
    )(row, *tokens, *weights, inner, outer, bias)


def split_three(column):
    high = column.astype(BF).astype(F32)
    rest = column - high
    middle = rest.astype(BF).astype(F32)
    return high, middle, rest - middle


def attend_kernel(query, keys, values, mixed, exact, query_back):
    rows = mixed.shape[0]
    lane = lax.broadcasted_iota(jnp.int32, (rows, 128), 1)
    spare = lane % HD
    outs = []
    for side in range(2):
        q = query[side]
        scores = dot(q, keys[side], ROW_DIMS)
        top = jnp.max(scores, axis=1, keepdims=True)
        weights = jnp.exp(scores - top).astype(BF)
        out = dot(weights, values[side], PLAIN_DIMS)
        at = HD if side == 0 else 0
        total = out[:, at : at + 1]
        outs.append(out / total)
        high, middle, low = split_three(top + jnp.log(total))
        mine = (lane < HD) if side == 0 else (lane >= HD)
        extra = jnp.where(spare == 1, -high, jnp.where(spare == 2, -middle, -low))
        keep = jnp.logical_or(mine, jnp.logical_or(spare == 0, spare > 3))
        query_back[side] = jnp.where(keep, q.astype(F32), extra).astype(BF)
    both = jnp.where(lane < HD, outs[0], outs[1])
    exact[...] = both
    mixed[...] = both.astype(BF)


def attend_pair(pair, query, keys, values, block):
    _, rows, _ = query.shape
    part = pl.BlockSpec((2, block, 128), lambda i: (pair, i, 0))
    whole = pl.BlockSpec((2, rows, 128), lambda i: (pair, 0, 0))
    out = pl.BlockSpec((block, 128), lambda i: (i, 0))
    return pl.pallas_call(
        attend_kernel,
        out_shape=(
            jax.ShapeDtypeStruct((rows, 128), BF),
            jax.ShapeDtypeStruct((rows, 128), F32),
            jax.ShapeDtypeStruct((2, rows, 128), BF),
        ),
        grid=(rows // block,),
        in_specs=[part, whole, whole],
        out_specs=(out, out, pl.BlockSpec((2, block, 128), lambda i: (0, i, 0))),
        cost_estimate=pl.CostEstimate(
            flops=16 * rows * rows * 128, transcendentals=0, bytes_accessed=8 * rows * 128
        ),
        name="attend",
    )(query, keys, values)


def attend_back_kernel(query, grad, exact, keys, values, inner, outer, *refs):
    out, grad_keys, grad_values = refs[-3:]
    step = pl.program_id(0)
    rows = grad.shape[0]
    total = keys.shape[1]
    lane = lax.broadcasted_iota(jnp.int32, (rows, 128), 1)
    spare = lane % HD

    @pl.when(step == 0)
    def _():
        grad_keys[...] = jnp.zeros_like(grad_keys)
        grad_values[...] = jnp.zeros_like(grad_values)

    product = grad[...].astype(F32) * exact[...]
    sides = []
    for side in range(2):
        q = query[side]
        mine = (lane < HD) if side == 0 else (lane >= HD)
        total_grad = jnp.sum(jnp.where(mine, product, 0.0), axis=1, keepdims=True)
        high, middle, low = split_three(total_grad)
        extra = jnp.where(
            spare == 0, -high, jnp.where(spare == 1, -middle, jnp.where(spare == 2, -low, 0.0))
        )
        g = jnp.where(mine, grad[...].astype(F32), extra).astype(BF)
        grad_query = jnp.zeros((128, rows), F32)
        for start in range(0, total, rows):
            k = keys[side, start : start + rows]
            v = values[side, start : start + rows]
            probs = jnp.exp(dot(k, q, ROW_DIMS))
            slope = (probs * dot(v, g, ROW_DIMS)).astype(BF)
            grad_values[side, start : start + rows] += dot(probs.astype(BF), g, PLAIN_DIMS)
            grad_keys[side, start : start + rows] += dot(slope, q, PLAIN_DIMS)
            grad_query += dot(k, slope, HEAD_DIMS)
        sides.append(grad_query)
    row = lax.broadcasted_iota(jnp.int32, (128, rows), 0)
    both = jnp.where(row < HD, sides[0], sides[1]).T * HD**-0.5
    cosine, sine = tables(inner, outer, step)
    from_row = pl.multiple_of(step * rows, rows)
    out[pl.ds(from_row, rows), :128] = turn(both, cosine, -sine).astype(BF)

    @pl.when(step == pl.num_programs(0) - 1)
    def _():
        for block in range(total // rows):
            here = slice(block * rows, (block + 1) * rows)
            k = jnp.where(lane < HD, grad_keys[0, here], grad_keys[1, here])
            v = jnp.where(lane < HD, grad_values[0, here], grad_values[1, here])
            cosine, sine = tables(inner, outer, block)
            out[here, 128:256] = turn(k, cosine, -sine).astype(BF)
            out[here, 256:] = v.astype(BF)


def attend_back_pair(pair, query, grad, exact, keys, values, inner, outer, held):
    heads, rows, _ = keys.shape
    block = inner.shape[1]
    part = pl.BlockSpec((2, block, 128), lambda i: (0, i, 0))
    whole = pl.BlockSpec((2, rows, 128), lambda i: (pair, 0, 0))
    fixed = lambda array: pl.BlockSpec(array.shape, lambda i: (0,) * array.ndim)
    return pl.pallas_call(
        attend_back_kernel,
        out_shape=jax.ShapeDtypeStruct((rows, 3 * heads * HD), BF),
        grid=(rows // block,),
        in_specs=[
            part,
            pl.BlockSpec((block, 128), lambda i: (i, pair)),
            pl.BlockSpec((block, 128), lambda i: (i, 0)),
            whole,
            whole,
            fixed(inner),
            fixed(outer),
        ]
        + [pl.BlockSpec(memory_space=pl.ANY)] * len(held),
        out_specs=pl.BlockSpec((rows, 3 * 128), lambda i: (0, pair)),
        scratch_shapes=[pltpu.VMEM((2, rows, 128), F32), pltpu.VMEM((2, rows, 128), F32)],
        input_output_aliases={7 + i: i for i in range(len(held))},
        cost_estimate=pl.CostEstimate(
            flops=48 * rows * rows * HD, transcendentals=0, bytes_accessed=8 * rows * HD
        ),
        name="attend_back",
    )(query, grad, exact, keys, values, inner, outer, *held)


def pick(step, sources, target):
    for index, source in enumerate(sources):

        @pl.when(step == index)
        def _(source=source):
            target[...] = source[...]


def share(step, part, keep, send):
    @pl.when(step % 2 == 0)
    def _():
        keep[...] = part

    @pl.when(step % 2 == 1)
    def _():
        send[...] = part.astype(BF)


def feed_kernel(row_ref, *refs, count, blocks, held):
    sources, second = refs[:count], refs[count]
    firsts = refs[count + 1 : count + 1 + blocks]
    tokens, act, slope, gelu_out, keep, send = refs[count + 1 + blocks + held :][:6]
    step = pl.program_id(0)
    first = firsts[0] if blocks == 1 else refs[-1]
    if blocks > 1:

        @pl.when(step == 0)
        def _():
            for index, block in enumerate(firsts):
                start = pl.multiple_of((row_ref[0] ^ index) * 128, 128)
                first[:, pl.ds(start, 128)] = block[...]

    hidden = first.shape[0] // 2
    pick(step, sources, tokens)
    x = tokens[...]
    gate = dot(x, first[:hidden], ROW_DIMS)
    upper = dot(x, first[hidden:], ROW_DIMS)
    phi = 0.5 * (1.0 + lax.erf(gate * 2**-0.5))
    gelu = gate * phi
    low = (gelu * upper).astype(BF)
    density = jnp.exp(-0.5 * gate * gate) * 0.3989422804014327
    act[...] = low
    slope[...] = (upper * (phi + gate * density)).astype(BF)
    gelu_out[...] = gelu.astype(BF)
    share(step, dot(low, second[...], ROW_DIMS), keep, send)


def feed(row, tokens, firsts, second, total, start, held):
    count = len(tokens)
    blocks = len(firsts)
    rows = tokens[0].shape[0]
    hidden = second.shape[1]
    fixed = lambda array: pl.BlockSpec(array.shape, lambda i, r: (0,) * array.ndim)
    tall = pl.BlockSpec((rows, hidden), lambda i, r: (i + start, 0))
    wide = pl.BlockSpec((rows, D), lambda i, r: (i + start, 0))
    half = pl.BlockSpec((rows, D), lambda i, r: (i // 2, 0))
    hidden_shape = jax.ShapeDtypeStruct((total, hidden), BF)
    size = rows * count
    first_shape = [jax.ShapeDtypeStruct((2 * hidden, D), BF)] * (blocks > 1)
    return pl.pallas_call(
        functools.partial(feed_kernel, count=count, blocks=blocks, held=len(held)),
        out_shape=(
            jax.ShapeDtypeStruct((total, D), BF),
            hidden_shape,
            hidden_shape,
            hidden_shape,
            jax.ShapeDtypeStruct((size // 2, D), F32),
            jax.ShapeDtypeStruct((size // 2, D), BF),
            *first_shape,
        ),
        grid_spec=pltpu.PrefetchScalarGridSpec(
            num_scalar_prefetch=1,
            grid=(count,),
            in_specs=[fixed(t) for t in tokens]
            + [fixed(second)]
            + [fixed(f) for f in firsts]
            + [pl.BlockSpec(memory_space=pl.ANY)] * len(held),
            out_specs=(wide, tall, tall, tall, half, half, *map(fixed, first_shape)),
        ),
        input_output_aliases={count + 2 + blocks + i: i for i in range(len(held))},
        cost_estimate=pl.CostEstimate(
            flops=6 * size * hidden * D, transcendentals=0, bytes_accessed=6 * hidden * D
        ),
        name="feed",
    )(row, *tokens, second, *firsts, *held)


def feed_back_kernel(*refs, count, held):
    sources, (slope, gelu, first, second) = refs[:count], refs[count : count + 4]
    grads, out, keep, send = refs[count + 4 + held :]
    step = pl.program_id(0)
    pick(step, sources, grads)
    grad_act = dot(grads[...], second[...], PLAIN_DIMS)
    gate = (grad_act * slope[...].astype(F32)).astype(BF)
    upper = (grad_act * gelu[...].astype(F32)).astype(BF)
    out[0] = gate
    out[1] = upper
    hidden = first.shape[0] // 2
    part = dot(gate, first[:hidden], PLAIN_DIMS) + dot(upper, first[hidden:], PLAIN_DIMS)
    share(step, part, keep, send)


def feed_back(grads, slope, gelu, first, second, start, held):
    count = len(grads)
    rows = grads[0].shape[0]
    total, hidden = slope.shape
    fixed = lambda array: pl.BlockSpec(array.shape, lambda i: (0,) * array.ndim)
    tall = pl.BlockSpec((rows, hidden), lambda i: (i + start, 0))
    wide = pl.BlockSpec((rows, D), lambda i: (i + start, 0))
    half = pl.BlockSpec((rows, D), lambda i: (i // 2, 0))
    size = rows * count
    return pl.pallas_call(
        functools.partial(feed_back_kernel, count=count, held=len(held)),
        out_shape=(
            jax.ShapeDtypeStruct((total, D), BF),
            jax.ShapeDtypeStruct((2, total, hidden), BF),
            jax.ShapeDtypeStruct((size // 2, D), F32),
            jax.ShapeDtypeStruct((size // 2, D), BF),
        ),
        grid=(count,),
        in_specs=[fixed(t) for t in grads]
        + [tall, tall, fixed(first), fixed(second)]
        + [pl.BlockSpec(memory_space=pl.ANY)] * len(held),
        out_specs=(wide, pl.BlockSpec((2, rows, hidden), lambda i: (0, i + start, 0)), half, half),
        input_output_aliases={count + 4 + i: i for i in range(len(held))},
        cost_estimate=pl.CostEstimate(
            flops=6 * size * hidden * D, transcendentals=0, bytes_accessed=6 * hidden * D
        ),
        name="feed_back",
    )(*grads, slope, gelu, first, second, *held)


def pack_kernel(row_ref, *refs):
    half = len(refs) // 2
    for source, target in zip(refs[:half], refs[half:]):
        target[0] = source[...]


def pack(row, tall, wide):
    ins, in_specs, shapes, out_specs = [], [], [], []
    for array, is_tall in [(a, True) for a in tall] + [(a, False) for a in wide]:
        block = (128, array.shape[1]) if is_tall else (array.shape[0], 128)
        for odd in range(2):
            if is_tall:
                index = lambda j, r, odd=odd: ((2 * j + odd) ^ r[0], 0)
            else:
                index = lambda j, r, odd=odd: (0, (2 * j + odd) ^ r[0])
            ins.append(array)
            in_specs.append(pl.BlockSpec(block, index))
            shapes.append(jax.ShapeDtypeStruct((4, *block), BF))
            out_specs.append(pl.BlockSpec((1, *block), lambda j, r: (j, 0, 0)))
    return pl.pallas_call(
        pack_kernel,
        out_shape=shapes,
        grid_spec=pltpu.PrefetchScalarGridSpec(
            num_scalar_prefetch=1, grid=(4,), in_specs=in_specs, out_specs=out_specs
        ),
        name="pack",
    )(row, *ins)


def stack_kernel(source, target):
    target[0] = source[...]


def stack_wide(array):
    rows, columns = array.shape
    return pl.pallas_call(
        stack_kernel,
        out_shape=jax.ShapeDtypeStruct((columns // 128, rows, 128), array.dtype),
        grid=(columns // 128,),
        in_specs=[pl.BlockSpec((rows, 128), lambda k: (0, k))],
        out_specs=pl.BlockSpec((1, rows, 128), lambda k: (k, 0, 0)),
        name="stack",
    )(array)


def sum_far(near):
    total = near[0]
    for step in range(1, 4):
        total = total + swap(near[step].astype(BF), "row", 2 * step).astype(F32)
    return total


def add_all(values):
    for axis in ("col", "row"):
        flip = 1
        while flip < lax.axis_size(axis):
            values = values + swap(values, axis, flip)
            flip *= 2
    return values


def group_shards(
    hidden_in,
    teacher,
    valid_mask,
    first_gain,
    second_gain,
    attention_in,
    attention_out,
    feed_in,
    feed_out,
):
    own = hidden_in.shape[0]
    column = lax.axis_index("col")
    row = lax.axis_index("row")
    group = own * 4
    group_start = row * group
    total_tokens = group * lax.axis_size("row")
    valid_total = jnp.sum(valid_mask.astype(F32))
    live_group = lax.dynamic_slice_in_dim(valid_mask, group_start, group, 0)
    live_own = lax.dynamic_slice_in_dim(live_group, column * own, own, 0).astype(F32)
    order = jnp.arange(4, dtype=jnp.int32) ^ column
    live = jnp.take(live_group.reshape(4, own), order, axis=0).reshape(group, 1)
    bias = jnp.where(live > 0, 0.0, MASKED).astype(F32)
    half = HD // 2
    frequency = ROPE_BASE ** (-(jnp.arange(half, dtype=F32) * 2.0) / HD)
    frequency = jnp.tile(frequency, 4)[None, :]
    inner = jnp.arange(own, dtype=F32)[:, None] * frequency
    inner = jnp.stack([jnp.cos(inner), jnp.sin(inner)])
    outer = (order * own).astype(F32)[:, None] * frequency
    outer = jnp.stack([jnp.cos(outer), jnp.sin(outer)])

    inputs = hidden_in.astype(F32)
    normed_one, inverse_one, low_one = layer_norm(inputs, first_gain)
    width = attention_in.shape[1]
    joint_blocks, joint_parts = row_blocks(attention_in.reshape(3 * width, attention_in.shape[2]))
    far = swap(low_one, "col", 2)
    near = swap(low_one, "col", 1)
    out_twin = swap(attention_out, "col", 2)
    hidden = feed_in.shape[1]
    index = row.reshape(1)
    feed_in, feed_out, attention_out, out_twin, *_ = lax.optimization_barrier(
        (feed_in, feed_out, attention_out, out_twin, *joint_parts)
    )
    tokens = [low_one, near, far, swap(far, "col", 1)]
    out_rows = lax.all_gather(
        jnp.concatenate([attention_out, out_twin, feed_out], axis=1), "row", axis=0, tiled=True
    )
    feed_in_blocks, _ = row_blocks(feed_in.reshape(2 * hidden, 128))
    all_low_one, joint, query, keys, values = project(
        index, tokens, joint_blocks, inner, outer, bias
    )
    mixed, exact, query_back, mixed_twin = [], [], [], []
    for pair in range(width // 128):
        pair_mixed, pair_exact, pair_query = attend_pair(pair, query, keys, values, 512)
        mixed.append(pair_mixed)
        exact.append(pair_exact)
        query_back.append(pair_query)
        mixed_twin.append(swap(pair_mixed[2 * own :], "col", 2))
    mixed = jnp.concatenate([m[: 2 * own] for m in mixed], axis=1)
    mixed_twin = jnp.concatenate(mixed_twin, axis=1)
    attention_rows = out_rows[:, :width]
    attention_twin = out_rows[:, width : 2 * width]
    feed_out_rows = out_rows[:, 2 * width :]
    mixed_own = mixed[: 2 * own]
    near = dot(mixed_own[own:], attention_rows, ROW_DIMS) + dot(
        mixed_twin[own:], attention_twin, ROW_DIMS
    )
    near = swap(near, "col", 1)
    branch = (
        dot(mixed_own[:own], attention_rows, ROW_DIMS)
        + dot(mixed_twin[:own], attention_twin, ROW_DIMS)
        + near
    )
    middle = inputs + branch
    normed_two, inverse_two, low_two = layer_norm(middle, second_gain)

    chunks = 2
    size = own // chunks
    parts = [slice(i * size, (i + 1) * size) for i in range(chunks)]
    far = [swap(low_two[here], "col", 2) for here in parts]
    near = []
    for here in parts:
        near += [low_two[here], swap(low_two[here], "col", 1)]
    *kept, keep_near, send_near, feed_in_rows = feed(
        index, near, feed_in_blocks, feed_out_rows, group, 0, []
    )
    far[0], kept[0] = lax.optimization_barrier((far[0], kept[0]))
    got_near = swap(send_near, "col", 1)
    sums = []
    gate_to = None
    for i in range(chunks):
        there = far[i]
        if gate_to is not None:
            there, gate_to = lax.optimization_barrier((there, gate_to))
            sums[-1] = gate_to
        there = [there, swap(there, "col", 1)]
        *kept, keep, send = feed(
            index, there, [feed_in_rows], feed_out_rows, group, 2 * chunks + 2 * i, kept
        )
        gate_to = (keep + swap(send, "col", 1).astype(F32)).astype(BF)
        sums.append(gate_to)
    all_low_two, act, slope, gelu = kept
    squares = jnp.float32(0.0)
    results, grad_results, far, held, nears = [], [], [], [], []
    for i, here in enumerate(parts):
        got_far = swap(sums[i], "col", 2)
        if held:
            got_far, held[0] = lax.optimization_barrier((got_far, held[0]))
        result = (
            middle[here]
            + keep_near[here]
            + got_near[here].astype(F32)
            + got_far.astype(F32)
        )
        results.append(result)
        error_term = result - teacher[here]
        live_here = live_own[here]
        squares = squares + jnp.sum(live_here * jnp.sum(error_term * error_term, axis=1))
        grad_result = (total_tokens * live_here)[:, None] * error_term / valid_total
        grad_results.append(grad_result)
        low = grad_result.astype(BF)
        far.append(swap(low, "col", 2))
        low = [low, swap(low, "col", 1)]
        *held, keep, send = feed_back(low, slope, gelu, feed_in_rows, feed_out_rows, 2 * i, held)
        nears.append(keep + swap(send, "col", 1).astype(F32))
    sums = []
    gate_to = None
    for i in range(chunks):
        there = far[i]
        if gate_to is not None:
            there, gate_to = lax.optimization_barrier((there, gate_to))
            sums[-1] = gate_to
        there = [there, swap(there, "col", 1)]
        *held, keep, send = feed_back(
            there,
            slope,
            gelu,
            feed_in_rows,
            feed_out_rows,
            2 * chunks + 2 * i,
            held,
        )
        gate_to = (keep + swap(send, "col", 1).astype(F32)).astype(BF)
        sums.append(gate_to)
    all_grads, grad_hidden = held
    all_grads, grad_hidden, gate_to = lax.optimization_barrier((all_grads, grad_hidden, gate_to))
    sums[-1] = gate_to
    grad_out = dot(all_grads, act, HEAD_DIMS).astype(BF)
    grad_feed = stack_wide(
        jnp.einsum(
            "irf,rd->ifd", grad_hidden, all_low_two, preferred_element_type=F32
        ).astype(BF).reshape(2 * hidden, D)
    )
    grad_second = jnp.zeros((D,), F32)
    grad_middles = []
    for i, here in enumerate(parts):
        got_far = swap(sums[i], "col", 2)
        if i == chunks - 1:
            got_far, grad_feed, grad_out = lax.optimization_barrier((got_far, grad_feed, grad_out))
        grad_low_two = nears[i] + got_far.astype(F32)
        grad_norm, grad_gain = norm_back(
            grad_low_two, normed_two[here], inverse_two[here], second_gain
        )
        grad_second = grad_second + grad_gain
        grad_middles.append(grad_results[i] + grad_norm)
    result = jnp.concatenate(results, axis=0)
    grad_middle = jnp.concatenate(grad_middles, axis=0)
    grad_branch = grad_middle.astype(BF)

    branch_pair = jnp.concatenate([grad_branch, swap(grad_branch, "col", 1)], axis=0)
    grad_mixed_twin = swap(dot(branch_pair, attention_twin, PLAIN_DIMS).astype(BF), "col", 2)
    grad_mixed = jnp.concatenate(
        [dot(branch_pair, attention_rows, PLAIN_DIMS).astype(BF), grad_mixed_twin], axis=0
    )
    grad_attention_far = swap(dot(branch_pair, mixed_twin, HEAD_DIMS).astype(BF), "col", 2)
    grad_attention = dot(branch_pair, mixed_own, HEAD_DIMS) + grad_attention_far.astype(F32)
    attention_keep, attention_send = pack(index, [grad_attention.astype(BF)], [])
    near_attention = attention_keep.astype(F32) + swap(attention_send, "row", 1).astype(F32)
    held, joint_near = [], []
    grad_first = jnp.zeros((D,), F32)
    for pair in range(width // 128):
        grad_joint = attend_back_pair(
            pair,
            query_back[pair],
            grad_mixed,
            exact[pair],
            keys,
            values,
            inner,
            outer,
            held,
        )
        held = [grad_joint]
        here = slice(pair * 384, (pair + 1) * 384)
        grad_pair = grad_joint[:, here]
        if pair == width // 128 - 1:
            part = dot(grad_joint[2 * own :], joint, PLAIN_DIMS)
            far = part[:own] + swap(part[own:].astype(BF), "col", 1).astype(F32)
            grad_pair, far = lax.optimization_barrier((grad_pair, far.astype(BF)))
        weight = dot(grad_pair, all_low_one, HEAD_DIMS)
        grad_first = grad_first + jnp.sum(weight * joint[here].astype(F32), axis=0)
        keep, send = pack(index, [], [weight.astype(BF)])
        near_sum = keep.astype(F32) + swap(send, "row", 1).astype(F32)
        if pair == 0:
            held, send = lax.optimization_barrier((held, send))
        joint_near.append(near_sum)
    part = dot(grad_joint[: 2 * own], joint, PLAIN_DIMS)
    near = part[:own] + swap(part[own:].astype(BF), "col", 1).astype(F32)
    grad_low_one = near + swap(far, "col", 2).astype(F32)
    grad_first = grad_first / first_gain
    totals = add_all(
        jnp.concatenate(
            [grad_first.reshape(8, 128), grad_second.reshape(8, 128), jnp.full((8, 128), squares)]
        )
    )
    grad_input_norm, _ = norm_back(grad_low_one, normed_one, inverse_one, first_gain)
    grad_input = grad_middle + grad_input_norm
    joint_sums = [sum_far(near).reshape(3, 128, 128) for near in joint_near]
    grads = (
        jnp.concatenate(joint_sums, axis=1),
        sum_far(near_attention),
        lax.psum_scatter(grad_feed, "row", scatter_dimension=0, tiled=True)
        .astype(F32)
        .reshape(2, hidden, 128),
        lax.psum_scatter(grad_out, "row", scatter_dimension=0, tiled=True).astype(F32),
    )
    loss = totals[16, 0] / (D * valid_total)
    return (
        result.astype(BF),
        loss,
        grad_input,
        totals[:8].reshape(D),
        totals[8:16].reshape(D),
        grads[0],
        grads[1],
        grads[2],
        grads[3],
    )


def shards(hidden_in, teacher, valid_mask, first_gain, second_gain, attention_in, *rest):
    fits = (
        lax.axis_size("col") == 4
        and lax.axis_size("row") == 8
        and hidden_in.shape[0] * 4 == SEQ_LEN
        and attention_in.shape[1] % 128 == 0
    )
    body = group_shards if fits else general_shards
    return body(
        hidden_in, teacher, valid_mask, first_gain, second_gain, attention_in, *rest
    )


def solution(mesh):
    in_specs = (
        P(("row", "col"), None),
        P(("row", "col"), None),
        P(),
        P(),
        P(),
        P(None, "col", "row"),
        P("row", "col"),
        P(None, "col", "row"),
        P("row", "col"),
    )
    out_specs = (
        P(("row", "col"), None),
        P(),
        P(("row", "col"), None),
        P(),
        P(),
        P(None, "col", "row"),
        P("row", "col"),
        P(None, "col", "row"),
        P("row", "col"),
    )
    return jax.shard_map(
        shards, mesh=mesh, in_specs=in_specs, out_specs=out_specs, check_vma=False
    )
```

profile of v0, /device:TPU:0, one launch (start us, length us, event | category | flops | bytes accessed | tf_op | source)
XLA Modules:
  0.0 537.8 jit_solution(11253313715367678389)
XLA Ops:
  10.9 3.0 collective-permute-start.1
  14.0 3.6 collective-permute-start.8
  18.7 19.9 %collective-permute-done.10 = bf16[128,256]{1,0:T(8,128)(2,1)S(1)} collective-permute-done((bf16[128,256]{1,0:T(8,128)(2,1)S(1)}, bf16[128,256]{1,0:T(8,128)(2,1)S(1)}, u32[]{:S(2)}, u32[]{:S(2)}) %collective-permute-start.10) | collective-permute-done | bytes 65568 | tf_op jit(solution)/shard_map/ppermute | solution.py:303
  49.0 4.9 collective-permute-done.9.rest_7_
  53.9 7.1 %collective-permute-done.7.rest_5_ = bf16[768,128]{1,0:T(8,128)(2,1)S(1)} collective-permute-done((bf16[768,128]{1,0:T(8,128)(2,1)}, bf16[768,128]{1,0:T(8,128)(2,1)S(1)}, u32[]{:S(2)}, u32[]{:S(2)}) %collective-permute-start.7) | collective-permute-done | bytes 196640 | tf_op jit(solution)/shard_map/ppermute | solution.py:303
  61.0 3.3 collective-permute-done.5.rest_3_
  65.3 10.1 %project.1 = (bf16[2048,1024]{1,0:T(8,128)(2,1)}, bf16[768,1024]{1,0:T(8,128)(2,1)}, bf16[4,2048,128]{2,1,0:T(8,128)(2,1)}, bf16[4,2048,128]{2,1,0:T(8,128)(2,1)}, bf16[4,2048,128]{2,1,0:T(8,128)(2,1)}) custom-call(s32[1]{0:T(128)} %bitcast.row_ref, bf16[512,1024]{1,0:T(8,128)(2,1)} %copy-done.32, bf16[512,1024]{1,0:T(8,128)(2,1)} %collective-permute-done.x1, ...), custom_call_target="tpu_custom_call" | custom-call | flops 3221225472 | bytes 16777216 | tf_op jit(solution)/shard_map/project/pallas_call | solution.py:389
  75.5 17.7 %attend.2 = (bf16[2048,128]{1,0:T(8,128)(2,1)}, f32[2048,128]{1,0:T(8,128)}, bf16[2,2048,128]{2,1,0:T(8,128)(2,1)}) custom-call(bf16[4,2048,128]{2,1,0:T(8,128)(2,1)} %get-tuple-element.82.query, bf16[4,2048,128]{2,1,0:T(8,128)(2,1)} %get-tuple-element.83.keys, bf16[4,2048,128]{2,1,0:T(8,128)(2,1)} %get-tuple-element.84.values), custom_call_target="tpu_custom_call" | custom-call | flops 8589934592 | bytes 2097152 | tf_op jit(solution)/shard_map/attend/pallas_call | solution.py:455
  95.8 18.1 %attend.3 = (bf16[2048,128]{1,0:T(8,128)(2,1)}, f32[2048,128]{1,0:T(8,128)}, bf16[2,2048,128]{2,1,0:T(8,128)(2,1)}) custom-call(bf16[4,2048,128]{2,1,0:T(8,128)(2,1)} %get-tuple-element.82.query, bf16[4,2048,128]{2,1,0:T(8,128)(2,1)} %get-tuple-element.83.keys, bf16[4,2048,128]{2,1,0:T(8,128)(2,1)} %get-tuple-element.84.values), custom_call_target="tpu_custom_call" | custom-call | flops 8589934592 | bytes 2097152 | tf_op jit(solution)/shard_map/attend/pallas_call | solution.py:455
  115.6 6.6 %collective-permute-done.12 = bf16[1024,128]{1,0:T(8,128)(2,1)S(1)} collective-permute-done((bf16[1024,128]{1,0:T(8,128)(2,1)S(1)}, bf16[1024,128]{1,0:T(8,128)(2,1)S(1)}, u32[]{:S(2)}, u32[]{:S(2)}) %collective-permute-start.12) | collective-permute-done | bytes 262176 | tf_op jit(solution)/shard_map/ppermute | solution.py:303
  125.4 3.6 collective-permute-start.21
  135.0 3.1 collective-permute-done.21.refs_11_
  138.1 19.7 %collective-permute-done.19.refs_9_ = bf16[1312,128]{1,0:T(8,128)(2,1)S(1)} collective-permute-done((bf16[1312,128]{1,0:T(8,128)(2,1)S(1)}, bf16[1312,128]{1,0:T(8,128)(2,1)S(1)}, u32[]{:S(2)}, u32[]{:S(2)}) %collective-permute-start.19) | collective-permute-done | bytes 335904 | tf_op jit(solution)/shard_map/ppermute | solution.py:303
  160.3 8.2 %collective-permute-done.22.refs_12_ = bf16[1312,128]{1,0:T(8,128)(2,1)S(1)} collective-permute-done((bf16[1312,128]{1,0:T(8,128)(2,1)S(1)}, bf16[1312,128]{1,0:T(8,128)(2,1)S(1)}, u32[]{:S(2)}, u32[]{:S(2)}) %collective-permute-start.22) | collective-permute-done | bytes 335904 | tf_op jit(solution)/shard_map/ppermute | solution.py:303
  170.3 5.4 %collective-permute-done.20.refs_10_ = bf16[1312,128]{1,0:T(8,128)(2,1)S(1)} collective-permute-done((bf16[1312,128]{1,0:T(8,128)(2,1)S(1)}, bf16[1312,128]{1,0:T(8,128)(2,1)S(1)}, u32[]{:S(2)}, u32[]{:S(2)}) %collective-permute-start.20) | collective-permute-done | bytes 335904 | tf_op jit(solution)/shard_map/ppermute | solution.py:303
  175.7 5.4 %collective-permute-done.18.refs_8_ = bf16[1312,128]{1,0:T(8,128)(2,1)S(1)} collective-permute-done((bf16[1312,128]{1,0:T(8,128)(2,1)S(1)}, bf16[1312,128]{1,0:T(8,128)(2,1)S(1)}, u32[]{:S(2)}, u32[]{:S(2)}) %collective-permute-start.18) | collective-permute-done | bytes 335904 | tf_op jit(solution)/shard_map/ppermute | solution.py:303
  181.9 12.7 %feed.3 = (bf16[2048,1024]{1,0:T(8,128)(2,1)}, bf16[2048,656]{1,0:T(8,128)(2,1)}, bf16[2048,656]{1,0:T(8,128)(2,1)}, bf16[2048,656]{1,0:T(8,128)(2,1)}, f32[512,...) custom-call(s32[1]{0:T(128)} %bitcast.row_ref, bf16[256,1024]{1,0:T(8,128)(2,1)} %get-tuple-element.185.refs_0_, ...), custom_call_target="tpu_custom_call" | custom-call | flops 4127195136 | bytes 4030464 | tf_op jit(solution)/shard_map/feed/pallas_call | solution.py:612
  197.0 7.5 %feed.4 = (bf16[2048,1024]{1,0:T(8,128)(2,1)}, bf16[2048,656]{1,0:T(8,128)(2,1)}, bf16[2048,656]{1,0:T(8,128)(2,1)}, bf16[2048,656]{1,0:T(8,128)(2,1)}, f32[256,1024]{1,0:T(8,128)}, /*index=5*/bf16[256,1024]{1,0:T(8,128)(2,1)}) custom-call(s32[1]{0:T(128)} %bitcast.row_ref, ...), custom_call_target="tpu_custom_call", output_to_operand_aliasing={{0}: (5, {}), {1}: (6, {}), {2}: (7, {}), {3}: (8, {})} | custom-call | flops 2063597568 | bytes 4030464 | tf_op jit(solution)/shard_map/feed/pallas_call | solution.py:612
  208.8 10.4 %collective-permute-done.24.refs_0_ = bf16[256,1024]{1,0:T(8,128)(2,1)} collective-permute-done((bf16[256,1024]{1,0:T(8,128)(2,1)}, bf16[256,1024]{1,0:T(8,128)(2,1)}, u32[]{:S(2)}, u32[]{:S(2)}) %collective-permute-start.24) | collective-permute-done | bytes 524320 | tf_op jit(solution)/shard_map/ppermute | solution.py:303
  221.4 7.5 %feed.5 = (bf16[2048,1024]{1,0:T(8,128)(2,1)}, bf16[2048,656]{1,0:T(8,128)(2,1)}, bf16[2048,656]{1,0:T(8,128)(2,1)}, bf16[2048,656]{1,0:T(8,128)(2,1)}, f32[256,1024]{1,0:T(8,128)}, /*index=5*/bf16[256,1024]{1,0:T(8,128)(2,1)}) custom-call(s32[1]{0:T(128)} %bitcast.row_ref, ...), custom_call_target="tpu_custom_call", output_to_operand_aliasing={{0}: (5, {}), {1}: (6, {}), {2}: (7, {}), {3}: (8, {})} | custom-call | flops 2063597568 | bytes 4030464 | tf_op jit(solution)/shard_map/feed/pallas_call | solution.py:612
  229.0 5.4 %collective-permute-done.28 = bf16[256,1024]{1,0:T(8,128)(2,1)} collective-permute-done((bf16[256,1024]{1,0:T(8,128)(2,1)}, bf16[256,1024]{1,0:T(8,128)(2,1)}, u32[]{:S(2)}, u32[]{:S(2)}) %collective-permute-start.28) | collective-permute-done | bytes 524320 | tf_op jit(solution)/shard_map/ppermute | solution.py:303
  242.1 9.1 %feed_back.4 = (bf16[2048,1024]{1,0:T(8,128)(2,1)}, bf16[2,2048,656]{2,1,0:T(8,128)(2,1)}, f32[256,1024]{1,0:T(8,128)}, bf16[256,1024]{1,0:T(8,128)(2,1)}) custom-call(bf16[256,1024]{1,0:T(8,128)(2,1)} %fusion.65.refs_0_, bf16[256,1024]{1,0:T(8,128)(2,1)} %collective-permute-done.32.refs_1_, bf16[2048,656]{1,0:T(8,128)(2,1)} %get-tuple-element.110.refs_2_, ...), custom_call_target="tpu_custom_call" | custom-call | flops 2063597568 | bytes 4030464 | tf_op jit(solution)/shard_map/feed_back/pallas_call | solution.py:664
  251.2 4.0 collective-permute-done.31
  255.2 3.1 multiply_reduce_fusion.3
  260.0 6.0 %collective-permute-done.35.refs_0_ = bf16[256,1024]{1,0:T(8,128)(2,1)} collective-permute-done((bf16[256,1024]{1,0:T(8,128)(2,1)}, bf16[256,1024]{1,0:T(8,128)(2,1)}, u32[]{:S(2)}, u32[]{:S(2)}) %collective-permute-start.35) | collective-permute-done | bytes 524320 | tf_op jit(solution)/shard_map/ppermute | solution.py:303
  266.8 8.9 %feed_back.5 = (bf16[2048,1024]{1,0:T(8,128)(2,1)}, bf16[2,2048,656]{2,1,0:T(8,128)(2,1)}, f32[256,1024]{1,0:T(8,128)}, bf16[256,1024]{1,0:T(8,128)(2,1)}) custom-call(bf16[256,1024]{1,0:T(8,128)(2,1)} %copy-done.24, bf16[256,1024]{1,0:T(8,128)(2,1)} %copy-done.37, ...), custom_call_target="tpu_custom_call", output_to_operand_aliasing={{0}: (6, {}), {1}: (7, {})} | custom-call | flops 2063597568 | bytes 4030464 | tf_op jit(solution)/shard_map/feed_back/pallas_call | solution.py:664
  276.6 9.0 %feed_back.6 = (bf16[2048,1024]{1,0:T(8,128)(2,1)}, bf16[2,2048,656]{2,1,0:T(8,128)(2,1)}, f32[256,1024]{1,0:T(8,128)}, bf16[256,1024]{1,0:T(8,128)(2,1)}) custom-call(bf16[256,1024]{1,0:T(8,128)(2,1)} %collective-permute-done.35.refs_0_, bf16[256,1024]{1,0:T(8,128)(2,1)} %copy-done.36, ...), custom_call_target="tpu_custom_call", output_to_operand_aliasing={{0}: (6, {}), {1}: (7, {})} | custom-call | flops 2063597568 | bytes 4030464 | tf_op jit(solution)/shard_map/feed_back/pallas_call | solution.py:664
  290.0 10.0 %collective-permute-done.34.refs_0_ = bf16[256,1024]{1,0:T(8,128)(2,1)S(1)} collective-permute-done((bf16[256,1024]{1,0:T(8,128)(2,1)S(1)}, bf16[256,1024]{1,0:T(8,128)(2,1)S(1)}, u32[]{:S(2)}, u32[]{:S(2)}) %collective-permute-start.34) | collective-permute-done | bytes 524320 | tf_op jit(solution)/shard_map/ppermute | solution.py:303
  302.7 8.9 %feed_back.7 = (bf16[2048,1024]{1,0:T(8,128)(2,1)}, bf16[2,2048,656]{2,1,0:T(8,128)(2,1)}, f32[256,1024]{1,0:T(8,128)}, bf16[256,1024]{1,0:T(8,128)(2,1)}) custom-call(bf16[256,1024]{1,0:T(8,128)(2,1)} %copy-done.35, bf16[256,1024]{1,0:T(8,128)(2,1)} %copy-done.38, ...), custom_call_target="tpu_custom_call", output_to_operand_aliasing={{0}: (6, {}), {1}: (7, {})} | custom-call | flops 2063597568 | bytes 4030464 | tf_op jit(solution)/shard_map/feed_back/pallas_call | solution.py:664
  316.5 10.3 %fusion.7 = bf16[2,656,1024]{2,1,0:T(8,128)(2,1)} fusion(bf16[2,2048,656]{2,1,0:T(8,128)(2,1)} %get-tuple-element.134, bf16[2048,1024]{1,0:T(8,128)(2,1)} %get-tuple-element.135), kind=kOutput, calls=%fused_computation.11 | convolution fusion | flops 5504270336 | bytes 12255232 | tf_op jit(solution)/shard_map/irf,rd->ifd/dot_general | solution.py:895
  326.8 4.2 convolution_convert_fusion
  331.1 5.9 %stack.13 = bf16[8,1312,128]{2,1,0:T(8,128)(2,1)} custom-call(bf16[1312,1024]{1,0:T(8,128)(2,1)} %bitcast.81), custom_call_target="tpu_custom_call" | custom-call | tf_op jit(solution)/shard_map/stack/pallas_call | solution.py:720
  340.8 3.2 multiply_reduce_fusion.8
  360.0 8.2 %collective-permute-done.45 = bf16[1024,256]{1,0:T(8,128)(2,1)S(1)} collective-permute-done((bf16[1024,256]{1,0:T(8,128)(2,1)S(1)}, bf16[1024,256]{1,0:T(8,128)(2,1)S(1)}, u32[]{:S(2)}, u32[]{:S(2)}) %collective-permute-start.45) | collective-permute-done | bytes 524320 | tf_op jit(solution)/shard_map/ppermute | solution.py:303
  369.3 26.3 %attend_back.2.refs_0_ = bf16[2048,768]{1,0:T(8,128)(2,1)} custom-call(bf16[2,2048,128]{2,1,0:T(8,128)(2,1)} %get-tuple-element.114.query, bf16[2048,256]{1,0:T(8,128)(2,1)} %pad_maximum_fusion.3.grad, f32[2048,128]{1,0:T(8,128)} %get-tuple-element.139.exact, bf16[4,2048,128]{2,1,0:T(8,128)(2,1)} %get-tuple-element.83.keys, ...), custom_call_target="tpu_custom_call" | custom-call | flops 12884901888 | bytes 1048576 | tf_op jit(solution)/shard_map/attend_back/pallas_call | solution.py:529
  395.6 5.9 %fusion.77 = (bf16[384,1024]{1,0:T(8,128)(2,1)}, f32[384,1024]{1,0:T(8,128)}) fusion(bf16[2048,1024]{1,0:T(8,128)(2,1)} %get-tuple-element.140, bf16[2048,768]{1,0:T(8,128)(2,1)} %attend_back.2.refs_0_), kind=kOutput, calls=%fused_computation.174 | convolution fusion | flops 1611005952 | bytes 8126464 | tf_op jit(solution)/shard_map/dot_general | solution.py:315
  401.5 3.3 pack.3
  404.8 26.7 %attend_back.3 = bf16[2048,768]{1,0:T(8,128)(2,1)} custom-call(bf16[2,2048,128]{2,1,0:T(8,128)(2,1)} %get-tuple-element.142.query, bf16[2048,256]{1,0:T(8,128)(2,1)} %pad_maximum_fusion.3.grad, f32[2048,128]{1,0:T(8,128)} %get-tuple-element.143.exact, bf16[4,2048,128]{2,1,0:T(8,128)(2,1)} %get-tuple-element.83.keys, ...), custom_call_target="tpu_custom_call", output_to_operand_aliasing={{}: (7, {})} | custom-call | flops 12884901888 | bytes 1048576 | tf_op jit(solution)/shard_map/attend_back/pallas_call | solution.py:529
  431.5 3.2 fusion.22
  442.7 3.2 pack.5
  446.5 3.8 fusion.20
  451.5 9.2 %collective-permute-done.63 = bf16[4,128,256]{2,1,0:T(8,128)(2,1)S(1)} collective-permute-done((bf16[4,128,256]{2,1,0:T(8,128)(2,1)}, bf16[4,128,256]{2,1,0:T(8,128)(2,1)S(1)}, u32[]{:S(2)}, u32[]{:S(2)}) %collective-permute-start.63) | collective-permute-done | bytes 262176 | tf_op jit(solution)/shard_map/ppermute | solution.py:303
  476.7 3.3 pack.4
  489.6 3.7 collective-permute-start.51
  493.3 3.5 collective-permute-done.56
  507.8 4.5 collective-permute-done.60
  514.0 8.9 %collective-permute-done.53 = bf16[512,1024]{1,0:T(8,128)(2,1)} collective-permute-done((bf16[512,1024]{1,0:T(8,128)(2,1)}, bf16[512,1024]{1,0:T(8,128)(2,1)}, u32[]{:S(2)}, u32[]{:S(2)}) %collective-permute-start.53) | collective-permute-done | bytes 1048608 | tf_op jit(solution)/shard_map/ppermute | solution.py:303
  523.0 3.1 fusion.67
  (358 shorter events, 136.6 us)
Async XLA Ops:
  7.2 115.1 %all-gather.2.cloned.1.call-start = ((), (), s32[]{:S(2)}) async-start(), calls=%async_computation.2 | async-start | bytes 2949120 | tf_op jit(solution)/shard_map/all_gather | solution.py:790
  10.9 30.5 %collective-permute-start.1 = (bf16[512,1024]{1,0:T(8,128)(2,1)S(1)}, bf16[512,1024]{1,0:T(8,128)(2,1)}, u32[]{:S(2)}, u32[]{:S(2)}) collective-permute-start(bf16[512,1024]{1,0:T(8,128)(2,1)S(1)} %fusion.10.x0), channel_id=1, source_target_pairs={{0,2},{1,3},{2,0},{3,1},{4,6},{5,7},{6,4},{7,5},{8,10},{9,11},{10,... | collective-permute-start | bytes 3145736 | tf_op jit(solution)/shard_map/ppermute | solution.py:303
  14.0 26.3 %collective-permute-start.8 = (bf16[768,128]{1,0:T(8,128)(2,1)S(1)}, bf16[768,128]{1,0:T(8,128)(2,1)S(1)}, u32[]{:S(2)}, u32[]{:S(2)}) collective-permute-start(bf16[768,128]{1,0:T(8,128)(2,1)S(1)} %bitcast.93), channel_id=1, source_target_pairs={{0,24},{4,28},{8,16},{12,20},{16,8},{20,12},{24,0},{28,4},{1,25},{... | collective-permute-start | bytes 589832 | tf_op jit(solution)/shard_map/ppermute | solution.py:303
  17.6 22.7 %collective-permute-start.6 = (bf16[768,128]{1,0:T(8,128)(2,1)S(1)}, bf16[768,128]{1,0:T(8,128)(2,1)S(1)}, u32[]{:S(2)}, u32[]{:S(2)}) collective-permute-start(bf16[768,128]{1,0:T(8,128)(2,1)S(1)} %bitcast.94), channel_id=1, source_target_pairs={{0,16},{4,20},{8,24},{12,28},{16,0},{20,4},{24,8},{28,12},{1,17},{... | collective-permute-start | bytes 589832 | tf_op jit(solution)/shard_map/ppermute | solution.py:303
  17.6 22.8 %collective-permute-start.4 = (bf16[768,128]{1,0:T(8,128)(2,1)S(1)}, bf16[768,128]{1,0:T(8,128)(2,1)}, u32[]{:S(2)}, u32[]{:S(2)}) collective-permute-start(bf16[768,128]{1,0:T(8,128)(2,1)S(1)} %bitcast.95), channel_id=1, source_target_pairs={{0,8},{4,12},{8,0},{12,4},{16,24},{20,28},{24,16},{28,20},{1,9},{5... | collective-permute-start | bytes 589832 | tf_op jit(solution)/shard_map/ppermute | solution.py:303
  18.4 20.2 %collective-permute-start.10 = (bf16[128,256]{1,0:T(8,128)(2,1)S(1)}, bf16[128,256]{1,0:T(8,128)(2,1)S(1)}, u32[]{:S(2)}, u32[]{:S(2)}) collective-permute-start(bf16[128,256]{1,0:T(8,128)(2,1)S(1)} %copy-done.46), channel_id=1, source_target_pairs={{0,2},{1,3},{2,0},{3,1},{4,6},{5,7},{6,4},{7,5},{8,10},{9,11},{10,... | collective-permute-start | bytes 196616 | tf_op jit(solution)/shard_map/ppermute | solution.py:303
  40.3 24.0 %collective-permute-start = (bf16[512,1024]{1,0:T(8,128)(2,1)S(1)}, bf16[512,1024]{1,0:T(8,128)(2,1)}, u32[]{:S(2)}, u32[]{:S(2)}) collective-permute-start(bf16[512,1024]{1,0:T(8,128)(2,1)S(1)} %fusion.10.x0), channel_id=1, source_target_pairs={{0,1},{1,0},{2,3},{3,2},{4,5},{5,4},{6,7},{7,6},{8,9},{9,8},{10,11... | collective-permute-start | bytes 3145736 | tf_op jit(solution)/shard_map/ppermute | solution.py:303
  41.3 464.4 %reduce-scatter.7.cloned.1.call-start = ((), (), s32[]{:S(2)}) async-start(), calls=%async_computation.4 | async-start | bytes 1769472
  41.4 22.8 %collective-permute-start.2 = (bf16[512,1024]{1,0:T(8,128)(2,1)}, bf16[512,1024]{1,0:T(8,128)(2,1)S(1)}, u32[]{:S(2)}, u32[]{:S(2)}) collective-permute-start(bf16[512,1024]{1,0:T(8,128)(2,1)} %collective-permute-done.1.x2), channel_id=1, source_target_pairs={{0,1},{1,0},{2,3},{3,2},{4,5},{5,4},{6,7},{7,6},{8,9},{9,8},{10,11... | collective-permute-start | bytes 3145736 | tf_op jit(solution)/shard_map/ppermute | solution.py:303
  45.5 15.5 %collective-permute-start.7 = (bf16[768,128]{1,0:T(8,128)(2,1)}, bf16[768,128]{1,0:T(8,128)(2,1)S(1)}, u32[]{:S(2)}, u32[]{:S(2)}) collective-permute-start(bf16[768,128]{1,0:T(8,128)(2,1)} %copy-done.68), channel_id=1, source_target_pairs={{0,4},{4,0},{8,12},{12,8},{16,20},{20,16},{24,28},{28,24},{1,5},{5... | collective-permute-start | bytes 589832 | tf_op jit(solution)/shard_map/ppermute | solution.py:303
  47.3 16.9 %collective-permute-start.5 = (bf16[768,128]{1,0:T(8,128)(2,1)}, bf16[768,128]{1,0:T(8,128)(2,1)S(1)}, u32[]{:S(2)}, u32[]{:S(2)}) collective-permute-start(bf16[768,128]{1,0:T(8,128)(2,1)} %collective-permute-done.4.rest_2_), channel_id=1, source_target_pairs={{0,4},{4,0},{8,12},{12,8},{16,20},{20,16},{24,28},{28,24},{1,5},{5... | collective-permute-start | bytes 589832 | tf_op jit(solution)/shard_map/ppermute | solution.py:303
  94.2 21.3 %collective-permute-start.11 = (bf16[1024,128]{1,0:T(8,128)(2,1)S(1)}, bf16[1024,128]{1,0:T(8,128)(2,1)S(1)}, u32[]{:S(2)}, u32[]{:S(2)}) collective-permute-start(bf16[1024,128]{1,0:T(8,128)(2,1)S(1)} %get-tuple-element.195), channel_id=1, source_target_pairs={{0,2},{1,3},{2,0},{3,1},{4,6},{5,7},{6,4},{7,5},{8,10},{9,11},{10,... | collective-permute-start | bytes 786440 | tf_op jit(solution)/shard_map/ppermute | solution.py:303
  125.4 12.7 %collective-permute-start.21 = (bf16[1312,128]{1,0:T(8,128)(2,1)S(1)}, bf16[1312,128]{1,0:T(8,128)(2,1)S(1)}, u32[]{:S(2)}, u32[]{:S(2)}) collective-permute-start(bf16[1312,128]{1,0:T(8,128)(2,1)S(1)} %bitcast.88), channel_id=1, source_target_pairs={{0,24},{4,28},{8,16},{12,20},{16,8},{20,12},{24,0},{28,4},{1,25},{... | collective-permute-start | bytes 1007624 | tf_op jit(solution)/shard_map/ppermute | solution.py:303
  129.0 28.8 %collective-permute-start.19 = (bf16[1312,128]{1,0:T(8,128)(2,1)S(1)}, bf16[1312,128]{1,0:T(8,128)(2,1)S(1)}, u32[]{:S(2)}, u32[]{:S(2)}) collective-permute-start(bf16[1312,128]{1,0:T(8,128)(2,1)S(1)} %bitcast.89), channel_id=1, source_target_pairs={{0,16},{4,20},{8,24},{12,28},{16,0},{20,4},{24,8},{28,12},{1,17},{... | collective-permute-start | bytes 1007624 | tf_op jit(solution)/shard_map/ppermute | solution.py:303
  129.0 29.3 %collective-permute-start.17 = (bf16[1312,128]{1,0:T(8,128)(2,1)S(1)}, bf16[1312,128]{1,0:T(8,128)(2,1)S(1)}, u32[]{:S(2)}, u32[]{:S(2)}) collective-permute-start(bf16[1312,128]{1,0:T(8,128)(2,1)S(1)} %bitcast.90), channel_id=1, source_target_pairs={{0,8},{4,12},{8,0},{12,4},{16,24},{20,28},{24,16},{28,20},{1,9},{5... | collective-permute-start | bytes 1007624 | tf_op jit(solution)/shard_map/ppermute | solution.py:303
  129.8 30.0 %collective-permute-start.16 = (bf16[1312,128]{1,0:T(8,128)(2,1)S(1)}, bf16[1312,128]{1,0:T(8,128)(2,1)S(1)}, u32[]{:S(2)}, u32[]{:S(2)}) collective-permute-start(bf16[1312,128]{1,0:T(8,128)(2,1)S(1)} %bitcast.91), channel_id=1, source_target_pairs={{0,4},{4,0},{8,12},{12,8},{16,20},{20,16},{24,28},{28,24},{1,5},{5... | collective-permute-start | bytes 1007624 | tf_op jit(solution)/shard_map/ppermute | solution.py:303
  135.0 46.1 %collective-permute-start.14 = (bf16[256,1024]{1,0:T(8,128)(2,1)}, bf16[256,1024]{1,0:T(8,128)(2,1)}, u32[]{:S(2)}, u32[]{:S(2)}) collective-permute-start(bf16[256,1024]{1,0:T(8,128)(2,1)} %get-tuple-element.185.refs_0_), channel_id=1, source_target_pairs={{0,1},{1,0},{2,3},{3,2},{4,5},{5,4},{6,7},{7,6},{8,9},{9,8},{10,11... | collective-permute-start | bytes 1572872 | tf_op jit(solution)/shard_map/ppermute | solution.py:303
  138.1 43.8 %collective-permute-start.15 = (bf16[256,1024]{1,0:T(8,128)(2,1)S(1)}, bf16[256,1024]{1,0:T(8,128)(2,1)}, u32[]{:S(2)}, u32[]{:S(2)}) collective-permute-start(bf16[256,1024]{1,0:T(8,128)(2,1)S(1)} %get-tuple-element.186.refs_2_), channel_id=1, source_target_pairs={{0,1},{1,0},{2,3},{3,2},{4,5},{5,4},{6,7},{7,6},{8,9},{9,8},{10,11... | collective-permute-start | bytes 1572872 | tf_op jit(solution)/shard_map/ppermute | solution.py:303
  157.7 10.8 %collective-permute-start.22 = (bf16[1312,128]{1,0:T(8,128)(2,1)S(1)}, bf16[1312,128]{1,0:T(8,128)(2,1)S(1)}, u32[]{:S(2)}, u32[]{:S(2)}) collective-permute-start(bf16[1312,128]{1,0:T(8,128)(2,1)S(1)} %collective-permute-done.21.refs_11_), channel_id=1, source_target_pairs={{0,4},{4,0},{8,12},{12,8},{16,20},{20,16},{24,28},{28,24},{1,5},{5... | collective-permute-start | bytes 1007624 | tf_op jit(solution)/shard_map/ppermute | solution.py:303
  158.3 17.4 %collective-permute-start.20 = (bf16[1312,128]{1,0:T(8,128)(2,1)S(1)}, bf16[1312,128]{1,0:T(8,128)(2,1)S(1)}, u32[]{:S(2)}, u32[]{:S(2)}) collective-permute-start(bf16[1312,128]{1,0:T(8,128)(2,1)S(1)} %collective-permute-done.19.refs_9_), channel_id=1, source_target_pairs={{0,4},{4,0},{8,12},{12,8},{16,20},{20,16},{24,28},{28,24},{1,5},{5... | collective-permute-start | bytes 1007624 | tf_op jit(solution)/shard_map/ppermute | solution.py:303
  159.8 21.4 %collective-permute-start.18 = (bf16[1312,128]{1,0:T(8,128)(2,1)S(1)}, bf16[1312,128]{1,0:T(8,128)(2,1)S(1)}, u32[]{:S(2)}, u32[]{:S(2)}) collective-permute-start(bf16[1312,128]{1,0:T(8,128)(2,1)S(1)} %collective-permute-done.17.refs_7_), channel_id=1, source_target_pairs={{0,4},{4,0},{8,12},{12,8},{16,20},{20,16},{24,28},{28,24},{1,5},{5... | collective-permute-start | bytes 1007624 | tf_op jit(solution)/shard_map/ppermute | solution.py:303
  168.5 26.2 %collective-permute-start.25 = (bf16[256,1024]{1,0:T(8,128)(2,1)}, bf16[256,1024]{1,0:T(8,128)(2,1)}, u32[]{:S(2)}, u32[]{:S(2)}) collective-permute-start(bf16[256,1024]{1,0:T(8,128)(2,1)} %get-tuple-element.185.refs_0_), channel_id=1, source_target_pairs={{0,2},{1,3},{2,0},{3,1},{4,6},{5,7},{6,4},{7,5},{8,10},{9,11},{10,... | collective-permute-start | bytes 1572872 | tf_op jit(solution)/shard_map/ppermute | solution.py:303
  204.6 14.5 %collective-permute-start.24 = (bf16[256,1024]{1,0:T(8,128)(2,1)}, bf16[256,1024]{1,0:T(8,128)(2,1)}, u32[]{:S(2)}, u32[]{:S(2)}) collective-permute-start(bf16[256,1024]{1,0:T(8,128)(2,1)} %copy-done.39), channel_id=1, source_target_pairs={{0,2},{1,3},{2,0},{3,1},{4,6},{5,7},{6,4},{7,5},{8,10},{9,11},{10,... | collective-permute-start | bytes 1572872 | tf_op jit(solution)/shard_map/ppermute | solution.py:303
  205.1 23.8 %collective-permute-start.23 = (bf16[512,1024]{1,0:T(8,128)(2,1)}, bf16[512,1024]{1,0:T(8,128)(2,1)}, u32[]{:S(2)}, u32[]{:S(2)}) collective-permute-start(bf16[512,1024]{1,0:T(8,128)(2,1)} %get-tuple-element.92), channel_id=1, source_target_pairs={{0,1},{1,0},{2,3},{3,2},{4,5},{5,4},{6,7},{7,6},{8,9},{9,8},{10,11... | collective-permute-start | bytes 3145736 | tf_op jit(solution)/shard_map/ppermute | solution.py:303
  219.7 14.7 %collective-permute-start.28 = (bf16[256,1024]{1,0:T(8,128)(2,1)}, bf16[256,1024]{1,0:T(8,128)(2,1)}, u32[]{:S(2)}, u32[]{:S(2)}) collective-permute-start(bf16[256,1024]{1,0:T(8,128)(2,1)} %add_convert_fusion.3), channel_id=1, source_target_pairs={{0,2},{1,3},{2,0},{3,1},{4,6},{5,7},{6,4},{7,5},{8,10},{9,11},{10,... | collective-permute-start | bytes 1572872 | tf_op jit(solution)/shard_map/ppermute | solution.py:303
  240.1 15.1 %collective-permute-start.31 = (bf16[256,1024]{1,0:T(8,128)(2,1)}, bf16[256,1024]{1,0:T(8,128)(2,1)}, u32[]{:S(2)}, u32[]{:S(2)}) collective-permute-start(bf16[256,1024]{1,0:T(8,128)(2,1)} %add_convert_fusion.2), channel_id=1, source_target_pairs={{0,2},{1,3},{2,0},{3,1},{4,6},{5,7},{6,4},{7,5},{8,10},{9,11},{10,... | collective-permute-start | bytes 1572872 | tf_op jit(solution)/shard_map/ppermute | solution.py:303
  240.7 25.3 %collective-permute-start.35 = (bf16[256,1024]{1,0:T(8,128)(2,1)}, bf16[256,1024]{1,0:T(8,128)(2,1)}, u32[]{:S(2)}, u32[]{:S(2)}) collective-permute-start(bf16[256,1024]{1,0:T(8,128)(2,1)} %fusion.65.refs_0_), channel_id=1, source_target_pairs={{0,2},{1,3},{2,0},{3,1},{4,6},{5,7},{6,4},{7,5},{8,10},{9,11},{10,... | collective-permute-start | bytes 1572872 | tf_op jit(solution)/shard_map/ppermute | solution.py:303
  286.1 13.9 %collective-permute-start.34 = (bf16[256,1024]{1,0:T(8,128)(2,1)S(1)}, bf16[256,1024]{1,0:T(8,128)(2,1)S(1)}, u32[]{:S(2)}, u32[]{:S(2)}) collective-permute-start(bf16[256,1024]{1,0:T(8,128)(2,1)S(1)} %copy-done.25), channel_id=1, source_target_pairs={{0,2},{1,3},{2,0},{3,1},{4,6},{5,7},{6,4},{7,5},{8,10},{9,11},{10,... | collective-permute-start | bytes 1572872 | tf_op jit(solution)/shard_map/ppermute | solution.py:303
  311.8 28.9 %collective-permute-start.33 = (bf16[256,1024]{1,0:T(8,128)(2,1)}, bf16[256,1024]{1,0:T(8,128)(2,1)}, u32[]{:S(2)}, u32[]{:S(2)}) collective-permute-start(bf16[256,1024]{1,0:T(8,128)(2,1)} %get-tuple-element.116), channel_id=1, source_target_pairs={{0,1},{1,0},{2,3},{3,2},{4,5},{5,4},{6,7},{7,6},{8,9},{9,8},{10,11... | collective-permute-start | bytes 1572872 | tf_op jit(solution)/shard_map/ppermute | solution.py:303
  312.1 28.6 %collective-permute-start.40 = (bf16[256,1024]{1,0:T(8,128)(2,1)}, bf16[256,1024]{1,0:T(8,128)(2,1)}, u32[]{:S(2)}, u32[]{:S(2)}) collective-permute-start(bf16[256,1024]{1,0:T(8,128)(2,1)} %get-tuple-element.125), channel_id=1, source_target_pairs={{0,1},{1,0},{2,3},{3,2},{4,5},{5,4},{6,7},{7,6},{8,9},{9,8},{10,11... | collective-permute-start | bytes 1572872 | tf_op jit(solution)/shard_map/ppermute | solution.py:303
  312.3 28.4 %collective-permute-start.39 = (bf16[256,1024]{1,0:T(8,128)(2,1)}, bf16[256,1024]{1,0:T(8,128)(2,1)}, u32[]{:S(2)}, u32[]{:S(2)}) collective-permute-start(bf16[256,1024]{1,0:T(8,128)(2,1)} %add_convert_fusion.1), channel_id=1, source_target_pairs={{0,2},{1,3},{2,0},{3,1},{4,6},{5,7},{6,4},{7,5},{8,10},{9,11},{10,... | collective-permute-start | bytes 1572872 | tf_op jit(solution)/shard_map/ppermute | solution.py:303
  315.9 22.1 %collective-permute-start.43 = (bf16[256,1024]{1,0:T(8,128)(2,1)}, bf16[256,1024]{1,0:T(8,128)(2,1)}, u32[]{:S(2)}, u32[]{:S(2)}) collective-permute-start(bf16[256,1024]{1,0:T(8,128)(2,1)} %add_convert_fusion), channel_id=1, source_target_pairs={{0,2},{1,3},{2,0},{3,1},{4,6},{5,7},{6,4},{7,5},{8,10},{9,11},{10,... | collective-permute-start | bytes 1572872 | tf_op jit(solution)/shard_map/ppermute | solution.py:303
  340.6 187.5 %reduce-scatter.5.cloned.1.call-start = ((), (), s32[]{:S(2)}) async-start(), calls=%async_computation.3 | async-start | bytes 3022848 | tf_op jit(solution)/shard_map/reduce_scatter | solution.py:967
  353.4 14.9 %collective-permute-start.45 = (bf16[1024,256]{1,0:T(8,128)(2,1)S(1)}, bf16[1024,256]{1,0:T(8,128)(2,1)S(1)}, u32[]{:S(2)}, u32[]{:S(2)}) collective-permute-start(bf16[1024,256]{1,0:T(8,128)(2,1)S(1)} %convolution_convert_fusion.2), channel_id=1, source_target_pairs={{0,2},{1,3},{2,0},{3,1},{4,6},{5,7},{6,4},{7,5},{8,10},{9,11},{10,... | collective-permute-start | bytes 1572872 | tf_op jit(solution)/shard_map/ppermute | solution.py:303
  356.9 82.4 %collective-permute-start.62 = (bf16[1024,256]{1,0:T(8,128)(2,1)}, bf16[1024,256]{1,0:T(8,128)(2,1)}, u32[]{:S(2)}, u32[]{:S(2)}) collective-permute-start(bf16[1024,256]{1,0:T(8,128)(2,1)} %convolution_convert_fusion.1), channel_id=1, source_target_pairs={{0,2},{1,3},{2,0},{3,1},{4,6},{5,7},{6,4},{7,5},{8,10},{9,11},{10,... | collective-permute-start | bytes 1572872 | tf_op jit(solution)/shard_map/ppermute | solution.py:303
  435.9 24.9 %collective-permute-start.46 = (bf16[512,1024]{1,0:T(8,128)(2,1)}, bf16[512,1024]{1,0:T(8,128)(2,1)}, u32[]{:S(2)}, u32[]{:S(2)}) collective-permute-start(bf16[512,1024]{1,0:T(8,128)(2,1)} %slice.392), channel_id=1, source_target_pairs={{0,1},{1,0},{2,3},{3,2},{4,5},{5,4},{6,7},{7,6},{8,9},{9,8},{10,11... | collective-permute-start | bytes 3145736 | tf_op jit(solution)/shard_map/ppermute | solution.py:303
  437.9 34.0 %collective-permute-start.54 = (bf16[4,384,128]{2,1,0:T(8,128)(2,1)}, bf16[4,384,128]{2,1,0:T(8,128)(2,1)}, u32[]{:S(2)}, u32[]{:S(2)}) collective-permute-start(bf16[4,384,128]{2,1,0:T(8,128)(2,1)} %get-tuple-element.144), channel_id=1, source_target_pairs={{0,4},{4,0},{8,12},{12,8},{16,20},{20,16},{24,28},{28,24},{1,5},{5... | collective-permute-start | bytes 1179656 | tf_op jit(solution)/shard_map/ppermute | solution.py:303
  445.9 14.8 %collective-permute-start.63 = (bf16[4,128,256]{2,1,0:T(8,128)(2,1)}, bf16[4,128,256]{2,1,0:T(8,128)(2,1)S(1)}, u32[]{:S(2)}, u32[]{:S(2)}) collective-permute-start(bf16[4,128,256]{2,1,0:T(8,128)(2,1)} %get-tuple-element.152), channel_id=1, source_target_pairs={{0,4},{4,0},{8,12},{12,8},{16,20},{20,16},{24,28},{28,24},{1,5},{5... | collective-permute-start | bytes 786440 | tf_op jit(solution)/shard_map/ppermute | solution.py:303
  467.2 14.8 %collective-permute-start.64 = (bf16[128,256]{1,0:T(8,128)(2,1)}, bf16[128,256]{1,0:T(8,128)(2,1)}, u32[]{:S(2)}, u32[]{:S(2)}) collective-permute-start(bf16[128,256]{1,0:T(8,128)(2,1)} %get-tuple-element.203), channel_id=1, source_target_pairs={{0,8},{4,12},{8,0},{12,4},{16,24},{20,28},{24,16},{28,20},{1,9},{5... | collective-permute-start | bytes 196616 | tf_op jit(solution)/shard_map/ppermute | solution.py:303
  467.3 15.2 %collective-permute-start.66 = (bf16[128,256]{1,0:T(8,128)(2,1)}, bf16[128,256]{1,0:T(8,128)(2,1)}, u32[]{:S(2)}, u32[]{:S(2)}) collective-permute-start(bf16[128,256]{1,0:T(8,128)(2,1)} %get-tuple-element.204), channel_id=1, source_target_pairs={{0,24},{4,28},{8,16},{12,20},{16,8},{20,12},{24,0},{28,4},{1,25},{... | collective-permute-start | bytes 196616 | tf_op jit(solution)/shard_map/ppermute | solution.py:303
  469.3 15.4 %collective-permute-start.65 = (bf16[128,256]{1,0:T(8,128)(2,1)}, bf16[128,256]{1,0:T(8,128)(2,1)}, u32[]{:S(2)}, u32[]{:S(2)}) collective-permute-start(bf16[128,256]{1,0:T(8,128)(2,1)} %get-tuple-element.205), channel_id=1, source_target_pairs={{0,16},{4,20},{8,24},{12,28},{16,0},{20,4},{24,8},{28,12},{1,17},{... | collective-permute-start | bytes 196616 | tf_op jit(solution)/shard_map/ppermute | solution.py:303
  475.7 13.9 %collective-permute-start.55 = (bf16[384,128]{1,0:T(8,128)(2,1)}, bf16[384,128]{1,0:T(8,128)(2,1)}, u32[]{:S(2)}, u32[]{:S(2)}) collective-permute-start(bf16[384,128]{1,0:T(8,128)(2,1)} %get-tuple-element.197), channel_id=1, source_target_pairs={{0,8},{4,12},{8,0},{12,4},{16,24},{20,28},{24,16},{28,20},{1,9},{5... | collective-permute-start | bytes 294920 | tf_op jit(solution)/shard_map/ppermute | solution.py:303
  480.0 13.3 %collective-permute-start.57 = (bf16[384,128]{1,0:T(8,128)(2,1)}, bf16[384,128]{1,0:T(8,128)(2,1)S(1)}, u32[]{:S(2)}, u32[]{:S(2)}) collective-permute-start(bf16[384,128]{1,0:T(8,128)(2,1)} %get-tuple-element.198), channel_id=1, source_target_pairs={{0,24},{4,28},{8,16},{12,20},{16,8},{20,12},{24,0},{28,4},{1,25},{... | collective-permute-start | bytes 294920 | tf_op jit(solution)/shard_map/ppermute | solution.py:303
  482.0 14.9 %collective-permute-start.56 = (bf16[384,128]{1,0:T(8,128)(2,1)S(1)}, bf16[384,128]{1,0:T(8,128)(2,1)S(1)}, u32[]{:S(2)}, u32[]{:S(2)}) collective-permute-start(bf16[384,128]{1,0:T(8,128)(2,1)S(1)} %get-tuple-element.199), channel_id=1, source_target_pairs={{0,16},{4,20},{8,24},{12,28},{16,0},{20,4},{24,8},{28,12},{1,17},{... | collective-permute-start | bytes 294920 | tf_op jit(solution)/shard_map/ppermute | solution.py:303
  482.5 16.7 %collective-permute-start.58 = (bf16[4,384,128]{2,1,0:T(8,128)(2,1)}, bf16[4,384,128]{2,1,0:T(8,128)(2,1)S(1)}, u32[]{:S(2)}, u32[]{:S(2)}) collective-permute-start(bf16[4,384,128]{2,1,0:T(8,128)(2,1)} %get-tuple-element.150), channel_id=1, source_target_pairs={{0,4},{4,0},{8,12},{12,8},{16,20},{20,16},{24,28},{28,24},{1,5},{5... | collective-permute-start | bytes 1179656 | tf_op jit(solution)/shard_map/ppermute | solution.py:303
  489.6 24.5 %collective-permute-start.52 = (bf16[512,1024]{1,0:T(8,128)(2,1)S(1)}, bf16[512,1024]{1,0:T(8,128)(2,1)}, u32[]{:S(2)}, u32[]{:S(2)}) collective-permute-start(bf16[512,1024]{1,0:T(8,128)(2,1)S(1)} %copy-done.31), channel_id=1, source_target_pairs={{0,1},{1,0},{2,3},{3,2},{4,5},{5,4},{6,7},{7,6},{8,9},{9,8},{10,11... | collective-permute-start | bytes 3145736 | tf_op jit(solution)/shard_map/ppermute | solution.py:303
  497.8 25.2 %collective-permute-start.53 = (bf16[512,1024]{1,0:T(8,128)(2,1)}, bf16[512,1024]{1,0:T(8,128)(2,1)}, u32[]{:S(2)}, u32[]{:S(2)}) collective-permute-start(bf16[512,1024]{1,0:T(8,128)(2,1)} %fusion.18), channel_id=1, source_target_pairs={{0,2},{1,3},{2,0},{3,1},{4,6},{5,7},{6,4},{7,5},{8,10},{9,11},{10,... | collective-permute-start | bytes 3145736 | tf_op jit(solution)/shard_map/ppermute | solution.py:303
  501.8 10.4 %collective-permute-start.60 = (bf16[384,128]{1,0:T(8,128)(2,1)S(1)}, bf16[384,128]{1,0:T(8,128)(2,1)}, u32[]{:S(2)}, u32[]{:S(2)}) collective-permute-start(bf16[384,128]{1,0:T(8,128)(2,1)S(1)} %get-tuple-element.202), channel_id=1, source_target_pairs={{0,16},{4,20},{8,24},{12,28},{16,0},{20,4},{24,8},{28,12},{1,17},{... | collective-permute-start | bytes 294920 | tf_op jit(solution)/shard_map/ppermute | solution.py:303
  (94 other events, 830.4 us)
Sparse Core Ops, SparseCore 0:
  41.4 57.6 all-gather.1
  340.8 64.0 reduce-scatter.6
  408.4 87.4 reduce-scatter.4
where the time goes:
time: 548 us; the launch traced here: 538 us
  Pallas kernels  178 us (32%)
  waiting for transfers between devices  168 us (31%)
  starting transfers between devices  52.5 us (10%)
  other arithmetic  52.4 us (10%)
  matrix products  42.3 us (8%)
  local copies, waits for them, and re-layouts  25.4 us (5%)
  between operations  18.7 us (3%)
    ppermute x67, waiting for transfers between devices, swap(): lax.ppermute(values, axis, [(place, place ^ flip) for place in range(size)])  168 us
    pallas_call x2, Pallas kernels, attend_back_pair(): pl.pallas_call(attend_back_kernel, out_shape=jax.ShapeDtypeStruct((rows,...  53 us
    ppermute x67, starting transfers between devices, swap(): lax.ppermute(values, axis, [(place, place ^ flip) for place in range(size)])  52.4 us
    pallas_call x4, Pallas kernels, feed_back(): pl.pallas_call(functools.partial(feed_back_kernel, count=count, held=len(...  35.9 us
    pallas_call x2, Pallas kernels, attend_pair(): pl.pallas_call(attend_kernel, out_shape=(jax.ShapeDtypeStruct((rows, 128)...  35.8 us
    dot_general x13, matrix products, dot(): return lax.dot_general(left, right, dims, preferred_element_type=F32)  32 us
    pallas_call x3, Pallas kernels, feed(): pl.pallas_call(functools.partial(feed_kernel, count=count, blocks=blocks,...  27.7 us
    unnamed x149, local copies, waits for them, and re-layouts  15.2 us
  transfers between devices with their start and end apart: 70, of which 32 were waited for; matrix products, arithmetic and copies ran while one was open for 19% of the time, Pallas kernels for 28%

commit v1 on v0

--- a/solution.py
+++ b/solution.py
@@ -711,20 +711,25 @@
     )(row, *ins)
 
 
-def stack_kernel(source, target):
-    target[0] = source[...]
-
-
-def stack_wide(array):
-    rows, columns = array.shape
+def stack_kernel(*refs):
+    at = 0
+    for source in refs[:-1]:
+        rows = source.shape[0]
+        refs[-1][0, at : at + rows] = source[...]
+        at += rows
+
+
+def stack_wide(arrays):
+    rows = sum(array.shape[0] for array in arrays)
+    blocks = arrays[0].shape[1] // 128
     return pl.pallas_call(
         stack_kernel,
-        out_shape=jax.ShapeDtypeStruct((columns // 128, rows, 128), array.dtype),
-        grid=(columns // 128,),
-        in_specs=[pl.BlockSpec((rows, 128), lambda k: (0, k))],
+        out_shape=jax.ShapeDtypeStruct((blocks, rows, 128), BF),
+        grid=(blocks,),
+        in_specs=[pl.BlockSpec((array.shape[0], 128), lambda k: (0, k)) for array in arrays],
         out_specs=pl.BlockSpec((1, rows, 128), lambda k: (k, 0, 0)),
         name="stack",
-    )(array)
+    )(*arrays)
 
 
 def sum_far(near):
@@ -777,10 +782,10 @@
     inputs = hidden_in.astype(F32)
     normed_one, inverse_one, low_one = layer_norm(inputs, first_gain)
     width = attention_in.shape[1]
+    out_twin = swap(attention_out, "col", 2)
     joint_blocks, joint_parts = row_blocks(attention_in.reshape(3 * width, attention_in.shape[2]))
     far = swap(low_one, "col", 2)
     near = swap(low_one, "col", 1)
-    out_twin = swap(attention_out, "col", 2)
     hidden = feed_in.shape[1]
     index = row.reshape(1)
     feed_in, feed_out, attention_out, out_twin, *_ = lax.optimization_barrier(
@@ -890,18 +895,15 @@
     all_grads, grad_hidden = held
     all_grads, grad_hidden, gate_to = lax.optimization_barrier((all_grads, grad_hidden, gate_to))
     sums[-1] = gate_to
-    grad_out = dot(all_grads, act, HEAD_DIMS).astype(BF)
-    grad_feed = stack_wide(
-        jnp.einsum(
-            "irf,rd->ifd", grad_hidden, all_low_two, preferred_element_type=F32
-        ).astype(BF).reshape(2 * hidden, D)
-    )
+    grad_out = dot(act, all_grads, HEAD_DIMS).astype(BF)
+    grad_feed = jnp.einsum("irf,rd->ifd", grad_hidden, all_low_two, preferred_element_type=F32)
+    grad_feed = stack_wide([grad_feed.astype(BF).reshape(2 * hidden, D), grad_out])
     grad_second = jnp.zeros((D,), F32)
     grad_middles = []
     for i, here in enumerate(parts):
         got_far = swap(sums[i], "col", 2)
         if i == chunks - 1:
-            got_far, grad_feed, grad_out = lax.optimization_barrier((got_far, grad_feed, grad_out))
+            got_far, grad_feed = lax.optimization_barrier((got_far, grad_feed))
         grad_low_two = nears[i] + got_far.astype(F32)
         grad_norm, grad_gain = norm_back(
             grad_low_two, normed_two[here], inverse_two[here], second_gain
@@ -960,14 +962,14 @@
     )
     grad_input_norm, _ = norm_back(grad_low_one, normed_one, inverse_one, first_gain)
     grad_input = grad_middle + grad_input_norm
+    feed_sum = lax.psum_scatter(grad_feed, "row", scatter_dimension=0, tiled=True)
+    feed_sum = feed_sum.astype(F32).reshape(3 * hidden, 128)
     joint_sums = [sum_far(near).reshape(3, 128, 128) for near in joint_near]
     grads = (
         jnp.concatenate(joint_sums, axis=1),
         sum_far(near_attention),
-        lax.psum_scatter(grad_feed, "row", scatter_dimension=0, tiled=True)
-        .astype(F32)
-        .reshape(2, hidden, 128),
-        lax.psum_scatter(grad_out, "row", scatter_dimension=0, tiled=True).astype(F32),
+        feed_sum[: 2 * hidden].reshape(2, hidden, 128),
+        feed_sum[2 * hidden :].T,
     )
     loss = totals[16, 0] / (D * valid_total)
     return (

time: 548 us -> 534 us (0.974)
  waiting for transfers between devices: 168 us -> 157 us
    ppermute x67, waiting for transfers between devices: 168 us -> 157 us  [swap(): lax.ppermute(values, axis, [(place, place ^ flip) for place in range(size)])]
  transfers between devices with their start and end apart: 70 -> 69, of which waited for: 32 -> 30; matrix products, arithmetic and copies ran while one was open for 19% -> 18% of each run, Pallas kernels for 28% -> 29%
where the time goes in v1:
time: 534 us; the launch traced here: 524 us
  Pallas kernels  179 us (34%)
  waiting for transfers between devices  157 us (29%)
  starting transfers between devices  52.4 us (10%)
  other arithmetic  50.7 us (9%)
  matrix products  42.2 us (8%)
  local copies, waits for them, and re-layouts  23.5 us (4%)
  between operations  19.2 us (4%)
    ppermute x67, waiting for transfers between devices, swap(): lax.ppermute(values, axis, [(place, place ^ flip) for place in range(size)])  157 us
    pallas_call x2, Pallas kernels, attend_back_pair(): pl.pallas_call(attend_back_kernel, out_shape=jax.ShapeDtypeStruct((rows,...  52.8 us
    ppermute x67, starting transfers between devices, swap(): lax.ppermute(values, axis, [(place, place ^ flip) for place in range(size)])  52.3 us
    pallas_call x4, Pallas kernels, feed_back(): pl.pallas_call(functools.partial(feed_back_kernel, count=count, held=len(...  36.1 us
    pallas_call x2, Pallas kernels, attend_pair(): pl.pallas_call(attend_kernel, out_shape=(jax.ShapeDtypeStruct((rows, 128)...  35.5 us
    dot_general x13, matrix products, dot(): return lax.dot_general(left, right, dims, preferred_element_type=F32)  31.9 us
    pallas_call x3, Pallas kernels, feed(): pl.pallas_call(functools.partial(feed_kernel, count=count, blocks=blocks,...  27.7 us
    unnamed x149, local copies, waits for them, and re-layouts  11.6 us
  transfers between devices with their start and end apart: 69, of which 30 were waited for; matrix products, arithmetic and copies ran while one was open for 18% of the time, Pallas kernels for 29%

profile of v1, /device:TPU:0, one launch (start us, length us, event | category | flops | bytes accessed | tf_op | source)
XLA Modules:
  0.0 524.1 jit_solution(15346508773006701902)
XLA Ops:
  10.9 3.0 collective-permute-start.1
  14.0 3.6 collective-permute-start.8
  18.7 19.9 %collective-permute-done.10 = bf16[128,256]{1,0:T(8,128)(2,1)S(1)} collective-permute-done((bf16[128,256]{1,0:T(8,128)(2,1)S(1)}, bf16[128,256]{1,0:T(8,128)(2,1)S(1)}, u32[]{:S(2)}, u32[]{:S(2)}) %collective-permute-start.10) | collective-permute-done | bytes 65568 | tf_op jit(solution)/shard_map/ppermute | solution.py:303
  49.0 4.9 collective-permute-done.9.rest_7_
  53.9 7.1 %collective-permute-done.7.rest_5_ = bf16[768,128]{1,0:T(8,128)(2,1)S(1)} collective-permute-done((bf16[768,128]{1,0:T(8,128)(2,1)}, bf16[768,128]{1,0:T(8,128)(2,1)S(1)}, u32[]{:S(2)}, u32[]{:S(2)}) %collective-permute-start.7) | collective-permute-done | bytes 196640 | tf_op jit(solution)/shard_map/ppermute | solution.py:303
  61.0 3.3 collective-permute-done.5.rest_3_
  65.3 10.2 %project.1 = (bf16[2048,1024]{1,0:T(8,128)(2,1)}, bf16[768,1024]{1,0:T(8,128)(2,1)}, bf16[4,2048,128]{2,1,0:T(8,128)(2,1)}, bf16[4,2048,128]{2,1,0:T(8,128)(2,1)}, bf16[4,2048,128]{2,1,0:T(8,128)(2,1)}) custom-call(s32[1]{0:T(128)} %bitcast.row_ref, bf16[512,1024]{1,0:T(8,128)(2,1)} %copy-done.33, bf16[512,1024]{1,0:T(8,128)(2,1)} %collective-permute-done.x1, ...), custom_call_target="tpu_custom_call" | custom-call | flops 3221225472 | bytes 16777216 | tf_op jit(solution)/shard_map/project/pallas_call | solution.py:389
  75.5 17.7 %attend.2 = (bf16[2048,128]{1,0:T(8,128)(2,1)}, f32[2048,128]{1,0:T(8,128)}, bf16[2,2048,128]{2,1,0:T(8,128)(2,1)}) custom-call(bf16[4,2048,128]{2,1,0:T(8,128)(2,1)} %get-tuple-element.81.query, bf16[4,2048,128]{2,1,0:T(8,128)(2,1)} %get-tuple-element.82.keys, bf16[4,2048,128]{2,1,0:T(8,128)(2,1)} %get-tuple-element.83.values), custom_call_target="tpu_custom_call" | custom-call | flops 8589934592 | bytes 2097152 | tf_op jit(solution)/shard_map/attend/pallas_call | solution.py:455
  95.8 17.9 %attend.3 = (bf16[2048,128]{1,0:T(8,128)(2,1)}, f32[2048,128]{1,0:T(8,128)}, bf16[2,2048,128]{2,1,0:T(8,128)(2,1)}) custom-call(bf16[4,2048,128]{2,1,0:T(8,128)(2,1)} %get-tuple-element.81.query, bf16[4,2048,128]{2,1,0:T(8,128)(2,1)} %get-tuple-element.82.keys, bf16[4,2048,128]{2,1,0:T(8,128)(2,1)} %get-tuple-element.83.values), custom_call_target="tpu_custom_call" | custom-call | flops 8589934592 | bytes 2097152 | tf_op jit(solution)/shard_map/attend/pallas_call | solution.py:455
  115.4 6.6 %collective-permute-done.12 = bf16[1024,128]{1,0:T(8,128)(2,1)S(1)} collective-permute-done((bf16[1024,128]{1,0:T(8,128)(2,1)S(1)}, bf16[1024,128]{1,0:T(8,128)(2,1)S(1)}, u32[]{:S(2)}, u32[]{:S(2)}) %collective-permute-start.12) | collective-permute-done | bytes 262176 | tf_op jit(solution)/shard_map/ppermute | solution.py:303
  125.2 3.6 collective-permute-start.21
  134.8 3.0 collective-permute-done.21.refs_11_
  137.9 19.7 %collective-permute-done.19.refs_9_ = bf16[1312,128]{1,0:T(8,128)(2,1)S(1)} collective-permute-done((bf16[1312,128]{1,0:T(8,128)(2,1)S(1)}, bf16[1312,128]{1,0:T(8,128)(2,1)S(1)}, u32[]{:S(2)}, u32[]{:S(2)}) %collective-permute-start.19) | collective-permute-done | bytes 335904 | tf_op jit(solution)/shard_map/ppermute | solution.py:303
  160.1 8.2 %collective-permute-done.22.refs_12_ = bf16[1312,128]{1,0:T(8,128)(2,1)S(1)} collective-permute-done((bf16[1312,128]{1,0:T(8,128)(2,1)S(1)}, bf16[1312,128]{1,0:T(8,128)(2,1)S(1)}, u32[]{:S(2)}, u32[]{:S(2)}) %collective-permute-start.22) | collective-permute-done | bytes 335904 | tf_op jit(solution)/shard_map/ppermute | solution.py:303
  170.1 5.4 %collective-permute-done.20.refs_10_ = bf16[1312,128]{1,0:T(8,128)(2,1)S(1)} collective-permute-done((bf16[1312,128]{1,0:T(8,128)(2,1)S(1)}, bf16[1312,128]{1,0:T(8,128)(2,1)S(1)}, u32[]{:S(2)}, u32[]{:S(2)}) %collective-permute-start.20) | collective-permute-done | bytes 335904 | tf_op jit(solution)/shard_map/ppermute | solution.py:303
  175.5 5.4 %collective-permute-done.18.refs_8_ = bf16[1312,128]{1,0:T(8,128)(2,1)S(1)} collective-permute-done((bf16[1312,128]{1,0:T(8,128)(2,1)S(1)}, bf16[1312,128]{1,0:T(8,128)(2,1)S(1)}, u32[]{:S(2)}, u32[]{:S(2)}) %collective-permute-start.18) | collective-permute-done | bytes 335904 | tf_op jit(solution)/shard_map/ppermute | solution.py:303
  181.7 12.8 %feed.3 = (bf16[2048,1024]{1,0:T(8,128)(2,1)}, bf16[2048,656]{1,0:T(8,128)(2,1)}, bf16[2048,656]{1,0:T(8,128)(2,1)}, bf16[2048,656]{1,0:T(8,128)(2,1)}, f32[512,...) custom-call(s32[1]{0:T(128)} %bitcast.row_ref, bf16[256,1024]{1,0:T(8,128)(2,1)} %get-tuple-element.183.refs_0_, ...), custom_call_target="tpu_custom_call" | custom-call | flops 4127195136 | bytes 4030464 | tf_op jit(solution)/shard_map/feed/pallas_call | solution.py:612
  196.8 7.5 %feed.4 = (bf16[2048,1024]{1,0:T(8,128)(2,1)}, bf16[2048,656]{1,0:T(8,128)(2,1)}, bf16[2048,656]{1,0:T(8,128)(2,1)}, bf16[2048,656]{1,0:T(8,128)(2,1)}, f32[256,1024]{1,0:T(8,128)}, /*index=5*/bf16[256,1024]{1,0:T(8,128)(2,1)}) custom-call(s32[1]{0:T(128)} %bitcast.row_ref, ...), custom_call_target="tpu_custom_call", output_to_operand_aliasing={{0}: (5, {}), {1}: (6, {}), {2}: (7, {}), {3}: (8, {})} | custom-call | flops 2063597568 | bytes 4030464 | tf_op jit(solution)/shard_map/feed/pallas_call | solution.py:612
  208.6 10.4 %collective-permute-done.24.refs_0_ = bf16[256,1024]{1,0:T(8,128)(2,1)} collective-permute-done((bf16[256,1024]{1,0:T(8,128)(2,1)}, bf16[256,1024]{1,0:T(8,128)(2,1)}, u32[]{:S(2)}, u32[]{:S(2)}) %collective-permute-start.24) | collective-permute-done | bytes 524320 | tf_op jit(solution)/shard_map/ppermute | solution.py:303
  221.2 7.4 %feed.5 = (bf16[2048,1024]{1,0:T(8,128)(2,1)}, bf16[2048,656]{1,0:T(8,128)(2,1)}, bf16[2048,656]{1,0:T(8,128)(2,1)}, bf16[2048,656]{1,0:T(8,128)(2,1)}, f32[256,1024]{1,0:T(8,128)}, /*index=5*/bf16[256,1024]{1,0:T(8,128)(2,1)}) custom-call(s32[1]{0:T(128)} %bitcast.row_ref, ...), custom_call_target="tpu_custom_call", output_to_operand_aliasing={{0}: (5, {}), {1}: (6, {}), {2}: (7, {}), {3}: (8, {})} | custom-call | flops 2063597568 | bytes 4030464 | tf_op jit(solution)/shard_map/feed/pallas_call | solution.py:612
  228.8 5.4 %collective-permute-done.28 = bf16[256,1024]{1,0:T(8,128)(2,1)} collective-permute-done((bf16[256,1024]{1,0:T(8,128)(2,1)}, bf16[256,1024]{1,0:T(8,128)(2,1)}, u32[]{:S(2)}, u32[]{:S(2)}) %collective-permute-start.28) | collective-permute-done | bytes 524320 | tf_op jit(solution)/shard_map/ppermute | solution.py:303
  242.0 9.3 %feed_back.4 = (bf16[2048,1024]{1,0:T(8,128)(2,1)}, bf16[2,2048,656]{2,1,0:T(8,128)(2,1)}, f32[256,1024]{1,0:T(8,128)}, bf16[256,1024]{1,0:T(8,128)(2,1)}) custom-call(bf16[256,1024]{1,0:T(8,128)(2,1)} %fusion.65.refs_0_, bf16[256,1024]{1,0:T(8,128)(2,1)} %collective-permute-done.32.refs_1_, bf16[2048,656]{1,0:T(8,128)(2,1)} %get-tuple-element.109.refs_2_, ...), custom_call_target="tpu_custom_call" | custom-call | flops 2063597568 | bytes 4030464 | tf_op jit(solution)/shard_map/feed_back/pallas_call | solution.py:664
  251.3 3.8 collective-permute-done.31
  255.1 3.1 multiply_reduce_fusion.3
  259.8 6.0 %collective-permute-done.35.refs_0_ = bf16[256,1024]{1,0:T(8,128)(2,1)} collective-permute-done((bf16[256,1024]{1,0:T(8,128)(2,1)}, bf16[256,1024]{1,0:T(8,128)(2,1)}, u32[]{:S(2)}, u32[]{:S(2)}) %collective-permute-start.35) | collective-permute-done | bytes 524320 | tf_op jit(solution)/shard_map/ppermute | solution.py:303
  266.7 8.9 %feed_back.5 = (bf16[2048,1024]{1,0:T(8,128)(2,1)}, bf16[2,2048,656]{2,1,0:T(8,128)(2,1)}, f32[256,1024]{1,0:T(8,128)}, bf16[256,1024]{1,0:T(8,128)(2,1)}) custom-call(bf16[256,1024]{1,0:T(8,128)(2,1)} %copy-done.25, bf16[256,1024]{1,0:T(8,128)(2,1)} %copy-done.38, ...), custom_call_target="tpu_custom_call", output_to_operand_aliasing={{0}: (6, {}), {1}: (7, {})} | custom-call | flops 2063597568 | bytes 4030464 | tf_op jit(solution)/shard_map/feed_back/pallas_call | solution.py:664
  276.4 9.0 %feed_back.6 = (bf16[2048,1024]{1,0:T(8,128)(2,1)}, bf16[2,2048,656]{2,1,0:T(8,128)(2,1)}, f32[256,1024]{1,0:T(8,128)}, bf16[256,1024]{1,0:T(8,128)(2,1)}) custom-call(bf16[256,1024]{1,0:T(8,128)(2,1)} %collective-permute-done.35.refs_0_, bf16[256,1024]{1,0:T(8,128)(2,1)} %copy-done.37, ...), custom_call_target="tpu_custom_call", output_to_operand_aliasing={{0}: (6, {}), {1}: (7, {})} | custom-call | flops 2063597568 | bytes 4030464 | tf_op jit(solution)/shard_map/feed_back/pallas_call | solution.py:664
  289.8 10.0 %collective-permute-done.34.refs_0_ = bf16[256,1024]{1,0:T(8,128)(2,1)S(1)} collective-permute-done((bf16[256,1024]{1,0:T(8,128)(2,1)S(1)}, bf16[256,1024]{1,0:T(8,128)(2,1)S(1)}, u32[]{:S(2)}, u32[]{:S(2)}) %collective-permute-start.34) | collective-permute-done | bytes 524320 | tf_op jit(solution)/shard_map/ppermute | solution.py:303
  302.6 8.9 %feed_back.7 = (bf16[2048,1024]{1,0:T(8,128)(2,1)}, bf16[2,2048,656]{2,1,0:T(8,128)(2,1)}, f32[256,1024]{1,0:T(8,128)}, bf16[256,1024]{1,0:T(8,128)(2,1)}) custom-call(bf16[256,1024]{1,0:T(8,128)(2,1)} %copy-done.36, bf16[256,1024]{1,0:T(8,128)(2,1)} %copy-done.39, ...), custom_call_target="tpu_custom_call", output_to_operand_aliasing={{0}: (6, {}), {1}: (7, {})} | custom-call | flops 2063597568 | bytes 4030464 | tf_op jit(solution)/shard_map/feed_back/pallas_call | solution.py:664
  316.4 10.3 %fusion.7 = bf16[2,656,1024]{2,1,0:T(8,128)(2,1)} fusion(bf16[2,2048,656]{2,1,0:T(8,128)(2,1)} %get-tuple-element.133, bf16[2048,1024]{1,0:T(8,128)(2,1)} %get-tuple-element.134), kind=kOutput, calls=%fused_computation.11 | convolution fusion | flops 5504270336 | bytes 12255232 | tf_op jit(solution)/shard_map/irf,rd->ifd/dot_general | solution.py:899
  326.7 4.1 convolution_convert_fusion.refs_1_
  330.9 6.8 %stack.13 = bf16[8,1968,128]{2,1,0:T(8,128)(2,1)} custom-call(bf16[1312,1024]{1,0:T(8,128)(2,1)} %bitcast.83, bf16[656,1024]{1,0:T(8,128)(2,1)} %convolution_convert_fusion.refs_1_), custom_call_target="tpu_custom_call" | custom-call | tf_op jit(solution)/shard_map/stack/pallas_call | solution.py:725
  338.0 3.2 multiply_reduce_fusion.8
  357.0 8.2 %collective-permute-done.45 = bf16[1024,256]{1,0:T(8,128)(2,1)S(1)} collective-permute-done((bf16[1024,256]{1,0:T(8,128)(2,1)S(1)}, bf16[1024,256]{1,0:T(8,128)(2,1)S(1)}, u32[]{:S(2)}, u32[]{:S(2)}) %collective-permute-start.45) | collective-permute-done | bytes 524320 | tf_op jit(solution)/shard_map/ppermute | solution.py:303
  366.3 26.2 %attend_back.2.refs_0_ = bf16[2048,768]{1,0:T(8,128)(2,1)} custom-call(bf16[2,2048,128]{2,1,0:T(8,128)(2,1)} %get-tuple-element.113.query, bf16[2048,256]{1,0:T(8,128)(2,1)} %pad_maximum_fusion.3.grad, f32[2048,128]{1,0:T(8,128)} %get-tuple-element.138.exact, bf16[4,2048,128]{2,1,0:T(8,128)(2,1)} %get-tuple-element.82.keys, ...), custom_call_target="tpu_custom_call" | custom-call | flops 12884901888 | bytes 1048576 | tf_op jit(solution)/shard_map/attend_back/pallas_call | solution.py:529
  392.6 5.9 %fusion.77 = (bf16[384,1024]{1,0:T(8,128)(2,1)}, f32[384,1024]{1,0:T(8,128)}) fusion(bf16[2048,1024]{1,0:T(8,128)(2,1)} %get-tuple-element.139, bf16[2048,768]{1,0:T(8,128)(2,1)} %attend_back.2.refs_0_), kind=kOutput, calls=%fused_computation.175 | convolution fusion | flops 1611005952 | bytes 8126464 | tf_op jit(solution)/shard_map/dot_general | solution.py:315
  398.5 3.3 pack.3
  401.7 26.6 %attend_back.3 = bf16[2048,768]{1,0:T(8,128)(2,1)} custom-call(bf16[2,2048,128]{2,1,0:T(8,128)(2,1)} %get-tuple-element.141.query, bf16[2048,256]{1,0:T(8,128)(2,1)} %pad_maximum_fusion.3.grad, f32[2048,128]{1,0:T(8,128)} %get-tuple-element.142.exact, bf16[4,2048,128]{2,1,0:T(8,128)(2,1)} %get-tuple-element.82.keys, ...), custom_call_target="tpu_custom_call", output_to_operand_aliasing={{}: (7, {})} | custom-call | flops 12884901888 | bytes 1048576 | tf_op jit(solution)/shard_map/attend_back/pallas_call | solution.py:529
  428.3 3.2 fusion.22
  439.4 3.3 pack.5
  443.3 3.8 fusion.20
  448.3 2.9 collective-permute-done.63
  467.1 3.3 pack.4
  478.3 2.9 collective-permute-start.51
  490.2 3.4 collective-permute-done.61
  493.7 3.2 collective-permute-done.60
  498.6 9.2 %collective-permute-done.53 = bf16[512,1024]{1,0:T(8,128)(2,1)} collective-permute-done((bf16[512,1024]{1,0:T(8,128)(2,1)}, bf16[512,1024]{1,0:T(8,128)(2,1)}, u32[]{:S(2)}, u32[]{:S(2)}) %collective-permute-start.53) | collective-permute-done | bytes 1048608 | tf_op jit(solution)/shard_map/ppermute | solution.py:303
  507.8 3.1 fusion.67
  (356 shorter events, 130.0 us)
Async XLA Ops:
  7.2 114.9 %all-gather.2.cloned.1.call-start = ((), (), s32[]{:S(2)}) async-start(), calls=%async_computation.1 | async-start | bytes 2949120 | tf_op jit(solution)/shard_map/all_gather | solution.py:795
  10.9 30.5 %collective-permute-start.1 = (bf16[512,1024]{1,0:T(8,128)(2,1)S(1)}, bf16[512,1024]{1,0:T(8,128)(2,1)}, u32[]{:S(2)}, u32[]{:S(2)}) collective-permute-start(bf16[512,1024]{1,0:T(8,128)(2,1)S(1)} %fusion.10.x0), channel_id=1, source_target_pairs={{0,2},{1,3},{2,0},{3,1},{4,6},{5,7},{6,4},{7,5},{8,10},{9,11},{10,... | collective-permute-start | bytes 3145736 | tf_op jit(solution)/shard_map/ppermute | solution.py:303
  14.0 26.3 %collective-permute-start.8 = (bf16[768,128]{1,0:T(8,128)(2,1)S(1)}, bf16[768,128]{1,0:T(8,128)(2,1)S(1)}, u32[]{:S(2)}, u32[]{:S(2)}) collective-permute-start(bf16[768,128]{1,0:T(8,128)(2,1)S(1)} %bitcast.95), channel_id=1, source_target_pairs={{0,24},{4,28},{8,16},{12,20},{16,8},{20,12},{24,0},{28,4},{1,25},{... | collective-permute-start | bytes 589832 | tf_op jit(solution)/shard_map/ppermute | solution.py:303
  17.6 22.7 %collective-permute-start.6 = (bf16[768,128]{1,0:T(8,128)(2,1)S(1)}, bf16[768,128]{1,0:T(8,128)(2,1)S(1)}, u32[]{:S(2)}, u32[]{:S(2)}) collective-permute-start(bf16[768,128]{1,0:T(8,128)(2,1)S(1)} %bitcast.96), channel_id=1, source_target_pairs={{0,16},{4,20},{8,24},{12,28},{16,0},{20,4},{24,8},{28,12},{1,17},{... | collective-permute-start | bytes 589832 | tf_op jit(solution)/shard_map/ppermute | solution.py:303
  17.6 22.8 %collective-permute-start.4 = (bf16[768,128]{1,0:T(8,128)(2,1)S(1)}, bf16[768,128]{1,0:T(8,128)(2,1)}, u32[]{:S(2)}, u32[]{:S(2)}) collective-permute-start(bf16[768,128]{1,0:T(8,128)(2,1)S(1)} %bitcast.97), channel_id=1, source_target_pairs={{0,8},{4,12},{8,0},{12,4},{16,24},{20,28},{24,16},{28,20},{1,9},{5... | collective-permute-start | bytes 589832 | tf_op jit(solution)/shard_map/ppermute | solution.py:303
  18.4 20.2 %collective-permute-start.10 = (bf16[128,256]{1,0:T(8,128)(2,1)S(1)}, bf16[128,256]{1,0:T(8,128)(2,1)S(1)}, u32[]{:S(2)}, u32[]{:S(2)}) collective-permute-start(bf16[128,256]{1,0:T(8,128)(2,1)S(1)} %copy-done.47), channel_id=1, source_target_pairs={{0,2},{1,3},{2,0},{3,1},{4,6},{5,7},{6,4},{7,5},{8,10},{9,11},{10,... | collective-permute-start | bytes 196616 | tf_op jit(solution)/shard_map/ppermute | solution.py:303
  38.5 8.8 %collective-permute-start.3 = (bf16[768,128]{1,0:T(8,128)(2,1)S(1)}, bf16[768,128]{1,0:T(8,128)(2,1)}, u32[]{:S(2)}, u32[]{:S(2)}) collective-permute-start(bf16[768,128]{1,0:T(8,128)(2,1)S(1)} %bitcast.98), channel_id=1, source_target_pairs={{0,4},{4,0},{8,12},{12,8},{16,20},{20,16},{24,28},{28,24},{1,5},{5... | collective-permute-start | bytes 589832 | tf_op jit(solution)/shard_map/ppermute | solution.py:303
  40.3 23.9 %collective-permute-start = (bf16[512,1024]{1,0:T(8,128)(2,1)S(1)}, bf16[512,1024]{1,0:T(8,128)(2,1)}, u32[]{:S(2)}, u32[]{:S(2)}) collective-permute-start(bf16[512,1024]{1,0:T(8,128)(2,1)S(1)} %fusion.10.x0), channel_id=1, source_target_pairs={{0,1},{1,0},{2,3},{3,2},{4,5},{5,4},{6,7},{7,6},{8,9},{9,8},{10,11... | collective-permute-start | bytes 3145736 | tf_op jit(solution)/shard_map/ppermute | solution.py:303
  41.3 471.6 %reduce-scatter.2.cloned.1.call-start = ((), (), s32[]{:S(2)}) async-start(), calls=%async_computation.2 | async-start | bytes 4534272 | tf_op jit(solution)/shard_map/reduce_scatter | solution.py:965
  41.4 22.8 %collective-permute-start.2 = (bf16[512,1024]{1,0:T(8,128)(2,1)}, bf16[512,1024]{1,0:T(8,128)(2,1)S(1)}, u32[]{:S(2)}, u32[]{:S(2)}) collective-permute-start(bf16[512,1024]{1,0:T(8,128)(2,1)} %collective-permute-done.1.x2), channel_id=1, source_target_pairs={{0,1},{1,0},{2,3},{3,2},{4,5},{5,4},{6,7},{7,6},{8,9},{9,8},{10,11... | collective-permute-start | bytes 3145736 | tf_op jit(solution)/shard_map/ppermute | solution.py:303
  45.2 8.7 %collective-permute-start.9 = (bf16[768,128]{1,0:T(8,128)(2,1)}, bf16[768,128]{1,0:T(8,128)(2,1)S(1)}, u32[]{:S(2)}, u32[]{:S(2)}) collective-permute-start(bf16[768,128]{1,0:T(8,128)(2,1)} %copy-done.68), channel_id=1, source_target_pairs={{0,4},{4,0},{8,12},{12,8},{16,20},{20,16},{24,28},{28,24},{1,5},{5... | collective-permute-start | bytes 589832 | tf_op jit(solution)/shard_map/ppermute | solution.py:303
  45.5 15.5 %collective-permute-start.7 = (bf16[768,128]{1,0:T(8,128)(2,1)}, bf16[768,128]{1,0:T(8,128)(2,1)S(1)}, u32[]{:S(2)}, u32[]{:S(2)}) collective-permute-start(bf16[768,128]{1,0:T(8,128)(2,1)} %copy-done.69), channel_id=1, source_target_pairs={{0,4},{4,0},{8,12},{12,8},{16,20},{20,16},{24,28},{28,24},{1,5},{5... | collective-permute-start | bytes 589832 | tf_op jit(solution)/shard_map/ppermute | solution.py:303
  47.3 16.9 %collective-permute-start.5 = (bf16[768,128]{1,0:T(8,128)(2,1)}, bf16[768,128]{1,0:T(8,128)(2,1)S(1)}, u32[]{:S(2)}, u32[]{:S(2)}) collective-permute-start(bf16[768,128]{1,0:T(8,128)(2,1)} %collective-permute-done.4.rest_2_), channel_id=1, source_target_pairs={{0,4},{4,0},{8,12},{12,8},{16,20},{20,16},{24,28},{28,24},{1,5},{5... | collective-permute-start | bytes 589832 | tf_op jit(solution)/shard_map/ppermute | solution.py:303
  94.2 21.1 %collective-permute-start.11 = (bf16[1024,128]{1,0:T(8,128)(2,1)S(1)}, bf16[1024,128]{1,0:T(8,128)(2,1)S(1)}, u32[]{:S(2)}, u32[]{:S(2)}) collective-permute-start(bf16[1024,128]{1,0:T(8,128)(2,1)S(1)} %get-tuple-element.193), channel_id=1, source_target_pairs={{0,2},{1,3},{2,0},{3,1},{4,6},{5,7},{6,4},{7,5},{8,10},{9,11},{10,... | collective-permute-start | bytes 786440 | tf_op jit(solution)/shard_map/ppermute | solution.py:303
  125.2 12.7 %collective-permute-start.21 = (bf16[1312,128]{1,0:T(8,128)(2,1)S(1)}, bf16[1312,128]{1,0:T(8,128)(2,1)S(1)}, u32[]{:S(2)}, u32[]{:S(2)}) collective-permute-start(bf16[1312,128]{1,0:T(8,128)(2,1)S(1)} %bitcast.90), channel_id=1, source_target_pairs={{0,24},{4,28},{8,16},{12,20},{16,8},{20,12},{24,0},{28,4},{1,25},{... | collective-permute-start | bytes 1007624 | tf_op jit(solution)/shard_map/ppermute | solution.py:303
  128.8 28.8 %collective-permute-start.19 = (bf16[1312,128]{1,0:T(8,128)(2,1)S(1)}, bf16[1312,128]{1,0:T(8,128)(2,1)S(1)}, u32[]{:S(2)}, u32[]{:S(2)}) collective-permute-start(bf16[1312,128]{1,0:T(8,128)(2,1)S(1)} %bitcast.91), channel_id=1, source_target_pairs={{0,16},{4,20},{8,24},{12,28},{16,0},{20,4},{24,8},{28,12},{1,17},{... | collective-permute-start | bytes 1007624 | tf_op jit(solution)/shard_map/ppermute | solution.py:303
  128.8 29.3 %collective-permute-start.17 = (bf16[1312,128]{1,0:T(8,128)(2,1)S(1)}, bf16[1312,128]{1,0:T(8,128)(2,1)S(1)}, u32[]{:S(2)}, u32[]{:S(2)}) collective-permute-start(bf16[1312,128]{1,0:T(8,128)(2,1)S(1)} %bitcast.92), channel_id=1, source_target_pairs={{0,8},{4,12},{8,0},{12,4},{16,24},{20,28},{24,16},{28,20},{1,9},{5... | collective-permute-start | bytes 1007624 | tf_op jit(solution)/shard_map/ppermute | solution.py:303
  129.6 30.0 %collective-permute-start.16 = (bf16[1312,128]{1,0:T(8,128)(2,1)S(1)}, bf16[1312,128]{1,0:T(8,128)(2,1)S(1)}, u32[]{:S(2)}, u32[]{:S(2)}) collective-permute-start(bf16[1312,128]{1,0:T(8,128)(2,1)S(1)} %bitcast.93), channel_id=1, source_target_pairs={{0,4},{4,0},{8,12},{12,8},{16,20},{20,16},{24,28},{28,24},{1,5},{5... | collective-permute-start | bytes 1007624 | tf_op jit(solution)/shard_map/ppermute | solution.py:303
  134.8 46.1 %collective-permute-start.14 = (bf16[256,1024]{1,0:T(8,128)(2,1)}, bf16[256,1024]{1,0:T(8,128)(2,1)}, u32[]{:S(2)}, u32[]{:S(2)}) collective-permute-start(bf16[256,1024]{1,0:T(8,128)(2,1)} %get-tuple-element.183.refs_0_), channel_id=1, source_target_pairs={{0,1},{1,0},{2,3},{3,2},{4,5},{5,4},{6,7},{7,6},{8,9},{9,8},{10,11... | collective-permute-start | bytes 1572872 | tf_op jit(solution)/shard_map/ppermute | solution.py:303
  137.9 43.8 %collective-permute-start.15 = (bf16[256,1024]{1,0:T(8,128)(2,1)S(1)}, bf16[256,1024]{1,0:T(8,128)(2,1)}, u32[]{:S(2)}, u32[]{:S(2)}) collective-permute-start(bf16[256,1024]{1,0:T(8,128)(2,1)S(1)} %get-tuple-element.184.refs_2_), channel_id=1, source_target_pairs={{0,1},{1,0},{2,3},{3,2},{4,5},{5,4},{6,7},{7,6},{8,9},{9,8},{10,11... | collective-permute-start | bytes 1572872 | tf_op jit(solution)/shard_map/ppermute | solution.py:303
  157.5 10.8 %collective-permute-start.22 = (bf16[1312,128]{1,0:T(8,128)(2,1)S(1)}, bf16[1312,128]{1,0:T(8,128)(2,1)S(1)}, u32[]{:S(2)}, u32[]{:S(2)}) collective-permute-start(bf16[1312,128]{1,0:T(8,128)(2,1)S(1)} %collective-permute-done.21.refs_11_), channel_id=1, source_target_pairs={{0,4},{4,0},{8,12},{12,8},{16,20},{20,16},{24,28},{28,24},{1,5},{5... | collective-permute-start | bytes 1007624 | tf_op jit(solution)/shard_map/ppermute | solution.py:303
  158.0 17.4 %collective-permute-start.20 = (bf16[1312,128]{1,0:T(8,128)(2,1)S(1)}, bf16[1312,128]{1,0:T(8,128)(2,1)S(1)}, u32[]{:S(2)}, u32[]{:S(2)}) collective-permute-start(bf16[1312,128]{1,0:T(8,128)(2,1)S(1)} %collective-permute-done.19.refs_9_), channel_id=1, source_target_pairs={{0,4},{4,0},{8,12},{12,8},{16,20},{20,16},{24,28},{28,24},{1,5},{5... | collective-permute-start | bytes 1007624 | tf_op jit(solution)/shard_map/ppermute | solution.py:303
  159.6 21.4 %collective-permute-start.18 = (bf16[1312,128]{1,0:T(8,128)(2,1)S(1)}, bf16[1312,128]{1,0:T(8,128)(2,1)S(1)}, u32[]{:S(2)}, u32[]{:S(2)}) collective-permute-start(bf16[1312,128]{1,0:T(8,128)(2,1)S(1)} %collective-permute-done.17.refs_7_), channel_id=1, source_target_pairs={{0,4},{4,0},{8,12},{12,8},{16,20},{20,16},{24,28},{28,24},{1,5},{5... | collective-permute-start | bytes 1007624 | tf_op jit(solution)/shard_map/ppermute | solution.py:303
  168.3 26.2 %collective-permute-start.25 = (bf16[256,1024]{1,0:T(8,128)(2,1)}, bf16[256,1024]{1,0:T(8,128)(2,1)}, u32[]{:S(2)}, u32[]{:S(2)}) collective-permute-start(bf16[256,1024]{1,0:T(8,128)(2,1)} %get-tuple-element.183.refs_0_), channel_id=1, source_target_pairs={{0,2},{1,3},{2,0},{3,1},{4,6},{5,7},{6,4},{7,5},{8,10},{9,11},{10,... | collective-permute-start | bytes 1572872 | tf_op jit(solution)/shard_map/ppermute | solution.py:303
  204.5 14.5 %collective-permute-start.24 = (bf16[256,1024]{1,0:T(8,128)(2,1)}, bf16[256,1024]{1,0:T(8,128)(2,1)}, u32[]{:S(2)}, u32[]{:S(2)}) collective-permute-start(bf16[256,1024]{1,0:T(8,128)(2,1)} %copy-done.40), channel_id=1, source_target_pairs={{0,2},{1,3},{2,0},{3,1},{4,6},{5,7},{6,4},{7,5},{8,10},{9,11},{10,... | collective-permute-start | bytes 1572872 | tf_op jit(solution)/shard_map/ppermute | solution.py:303
  205.0 23.8 %collective-permute-start.23 = (bf16[512,1024]{1,0:T(8,128)(2,1)}, bf16[512,1024]{1,0:T(8,128)(2,1)}, u32[]{:S(2)}, u32[]{:S(2)}) collective-permute-start(bf16[512,1024]{1,0:T(8,128)(2,1)} %get-tuple-element.91), channel_id=1, source_target_pairs={{0,1},{1,0},{2,3},{3,2},{4,5},{5,4},{6,7},{7,6},{8,9},{9,8},{10,11... | collective-permute-start | bytes 3145736 | tf_op jit(solution)/shard_map/ppermute | solution.py:303
  219.6 14.7 %collective-permute-start.28 = (bf16[256,1024]{1,0:T(8,128)(2,1)}, bf16[256,1024]{1,0:T(8,128)(2,1)}, u32[]{:S(2)}, u32[]{:S(2)}) collective-permute-start(bf16[256,1024]{1,0:T(8,128)(2,1)} %add_convert_fusion.3), channel_id=1, source_target_pairs={{0,2},{1,3},{2,0},{3,1},{4,6},{5,7},{6,4},{7,5},{8,10},{9,11},{10,... | collective-permute-start | bytes 1572872 | tf_op jit(solution)/shard_map/ppermute | solution.py:303
  228.7 10.3 %collective-permute-start.30 = (bf16[256,1024]{1,0:T(8,128)(2,1)}, bf16[256,1024]{1,0:T(8,128)(2,1)S(1)}, u32[]{:S(2)}, u32[]{:S(2)}) collective-permute-start(bf16[256,1024]{1,0:T(8,128)(2,1)} %get-tuple-element.108), channel_id=1, source_target_pairs={{0,1},{1,0},{2,3},{3,2},{4,5},{5,4},{6,7},{7,6},{8,9},{9,8},{10,11... | collective-permute-start | bytes 1572872 | tf_op jit(solution)/shard_map/ppermute | solution.py:303
  240.0 15.1 %collective-permute-start.31 = (bf16[256,1024]{1,0:T(8,128)(2,1)}, bf16[256,1024]{1,0:T(8,128)(2,1)}, u32[]{:S(2)}, u32[]{:S(2)}) collective-permute-start(bf16[256,1024]{1,0:T(8,128)(2,1)} %add_convert_fusion.2), channel_id=1, source_target_pairs={{0,2},{1,3},{2,0},{3,1},{4,6},{5,7},{6,4},{7,5},{8,10},{9,11},{10,... | collective-permute-start | bytes 1572872 | tf_op jit(solution)/shard_map/ppermute | solution.py:303
  240.5 25.4 %collective-permute-start.35 = (bf16[256,1024]{1,0:T(8,128)(2,1)}, bf16[256,1024]{1,0:T(8,128)(2,1)}, u32[]{:S(2)}, u32[]{:S(2)}) collective-permute-start(bf16[256,1024]{1,0:T(8,128)(2,1)} %fusion.65.refs_0_), channel_id=1, source_target_pairs={{0,2},{1,3},{2,0},{3,1},{4,6},{5,7},{6,4},{7,5},{8,10},{9,11},{10,... | collective-permute-start | bytes 1572872 | tf_op jit(solution)/shard_map/ppermute | solution.py:303
  265.9 9.7 %collective-permute-start.36 = (bf16[256,1024]{1,0:T(8,128)(2,1)}, bf16[256,1024]{1,0:T(8,128)(2,1)S(1)}, u32[]{:S(2)}, u32[]{:S(2)}) collective-permute-start(bf16[256,1024]{1,0:T(8,128)(2,1)} %collective-permute-done.35.refs_0_), channel_id=1, source_target_pairs={{0,1},{1,0},{2,3},{3,2},{4,5},{5,4},{6,7},{7,6},{8,9},{9,8},{10,11... | collective-permute-start | bytes 1572872 | tf_op jit(solution)/shard_map/ppermute | solution.py:303
  285.9 13.9 %collective-permute-start.34 = (bf16[256,1024]{1,0:T(8,128)(2,1)S(1)}, bf16[256,1024]{1,0:T(8,128)(2,1)S(1)}, u32[]{:S(2)}, u32[]{:S(2)}) collective-permute-start(bf16[256,1024]{1,0:T(8,128)(2,1)S(1)} %copy-done.26), channel_id=1, source_target_pairs={{0,2},{1,3},{2,0},{3,1},{4,6},{5,7},{6,4},{7,5},{8,10},{9,11},{10,... | collective-permute-start | bytes 1572872 | tf_op jit(solution)/shard_map/ppermute | solution.py:303
  311.7 26.3 %collective-permute-start.33 = (bf16[256,1024]{1,0:T(8,128)(2,1)}, bf16[256,1024]{1,0:T(8,128)(2,1)}, u32[]{:S(2)}, u32[]{:S(2)}) collective-permute-start(bf16[256,1024]{1,0:T(8,128)(2,1)} %get-tuple-element.115), channel_id=1, source_target_pairs={{0,1},{1,0},{2,3},{3,2},{4,5},{5,4},{6,7},{7,6},{8,9},{9,8},{10,11... | collective-permute-start | bytes 1572872 | tf_op jit(solution)/shard_map/ppermute | solution.py:303
  312.0 25.9 %collective-permute-start.40 = (bf16[256,1024]{1,0:T(8,128)(2,1)}, bf16[256,1024]{1,0:T(8,128)(2,1)}, u32[]{:S(2)}, u32[]{:S(2)}) collective-permute-start(bf16[256,1024]{1,0:T(8,128)(2,1)} %get-tuple-element.124), channel_id=1, source_target_pairs={{0,1},{1,0},{2,3},{3,2},{4,5},{5,4},{6,7},{7,6},{8,9},{9,8},{10,11... | collective-permute-start | bytes 1572872 | tf_op jit(solution)/shard_map/ppermute | solution.py:303
  312.2 25.8 %collective-permute-start.39 = (bf16[256,1024]{1,0:T(8,128)(2,1)}, bf16[256,1024]{1,0:T(8,128)(2,1)}, u32[]{:S(2)}, u32[]{:S(2)}) collective-permute-start(bf16[256,1024]{1,0:T(8,128)(2,1)} %add_convert_fusion.1), channel_id=1, source_target_pairs={{0,2},{1,3},{2,0},{3,1},{4,6},{5,7},{6,4},{7,5},{8,10},{9,11},{10,... | collective-permute-start | bytes 1572872 | tf_op jit(solution)/shard_map/ppermute | solution.py:303
  315.8 22.1 %collective-permute-start.43 = (bf16[256,1024]{1,0:T(8,128)(2,1)}, bf16[256,1024]{1,0:T(8,128)(2,1)}, u32[]{:S(2)}, u32[]{:S(2)}) collective-permute-start(bf16[256,1024]{1,0:T(8,128)(2,1)} %add_convert_fusion), channel_id=1, source_target_pairs={{0,2},{1,3},{2,0},{3,1},{4,6},{5,7},{6,4},{7,5},{8,10},{9,11},{10,... | collective-permute-start | bytes 1572872 | tf_op jit(solution)/shard_map/ppermute | solution.py:303
  350.4 14.9 %collective-permute-start.45 = (bf16[1024,256]{1,0:T(8,128)(2,1)S(1)}, bf16[1024,256]{1,0:T(8,128)(2,1)S(1)}, u32[]{:S(2)}, u32[]{:S(2)}) collective-permute-start(bf16[1024,256]{1,0:T(8,128)(2,1)S(1)} %convolution_convert_fusion.2), channel_id=1, source_target_pairs={{0,2},{1,3},{2,0},{3,1},{4,6},{5,7},{6,4},{7,5},{8,10},{9,11},{10,... | collective-permute-start | bytes 1572872 | tf_op jit(solution)/shard_map/ppermute | solution.py:303
  354.5 81.7 %collective-permute-start.62 = (bf16[1024,256]{1,0:T(8,128)(2,1)}, bf16[1024,256]{1,0:T(8,128)(2,1)}, u32[]{:S(2)}, u32[]{:S(2)}) collective-permute-start(bf16[1024,256]{1,0:T(8,128)(2,1)} %convolution_convert_fusion.1), channel_id=1, source_target_pairs={{0,2},{1,3},{2,0},{3,1},{4,6},{5,7},{6,4},{7,5},{8,10},{9,11},{10,... | collective-permute-start | bytes 1572872 | tf_op jit(solution)/shard_map/ppermute | solution.py:303
  432.7 18.6 %collective-permute-start.46 = (bf16[512,1024]{1,0:T(8,128)(2,1)}, bf16[512,1024]{1,0:T(8,128)(2,1)}, u32[]{:S(2)}, u32[]{:S(2)}) collective-permute-start(bf16[512,1024]{1,0:T(8,128)(2,1)} %slice.408), channel_id=1, source_target_pairs={{0,1},{1,0},{2,3},{3,2},{4,5},{5,4},{6,7},{7,6},{8,9},{9,8},{10,11... | collective-permute-start | bytes 3145736 | tf_op jit(solution)/shard_map/ppermute | solution.py:303
  434.7 27.9 %collective-permute-start.54 = (bf16[4,384,128]{2,1,0:T(8,128)(2,1)}, bf16[4,384,128]{2,1,0:T(8,128)(2,1)}, u32[]{:S(2)}, u32[]{:S(2)}) collective-permute-start(bf16[4,384,128]{2,1,0:T(8,128)(2,1)} %get-tuple-element.143), channel_id=1, source_target_pairs={{0,4},{4,0},{8,12},{12,8},{16,20},{20,16},{24,28},{28,24},{1,5},{5... | collective-permute-start | bytes 1179656 | tf_op jit(solution)/shard_map/ppermute | solution.py:303
  457.7 15.3 %collective-permute-start.64 = (bf16[128,256]{1,0:T(8,128)(2,1)}, bf16[128,256]{1,0:T(8,128)(2,1)}, u32[]{:S(2)}, u32[]{:S(2)}) collective-permute-start(bf16[128,256]{1,0:T(8,128)(2,1)} %get-tuple-element.201), channel_id=1, source_target_pairs={{0,8},{4,12},{8,0},{12,4},{16,24},{20,28},{24,16},{28,20},{1,9},{5... | collective-permute-start | bytes 196616 | tf_op jit(solution)/shard_map/ppermute | solution.py:303
  457.7 15.3 %collective-permute-start.66 = (bf16[128,256]{1,0:T(8,128)(2,1)}, bf16[128,256]{1,0:T(8,128)(2,1)}, u32[]{:S(2)}, u32[]{:S(2)}) collective-permute-start(bf16[128,256]{1,0:T(8,128)(2,1)} %get-tuple-element.202), channel_id=1, source_target_pairs={{0,24},{4,28},{8,16},{12,20},{16,8},{20,12},{24,0},{28,4},{1,25},{... | collective-permute-start | bytes 196616 | tf_op jit(solution)/shard_map/ppermute | solution.py:303
  460.3 14.3 %collective-permute-start.65 = (bf16[128,256]{1,0:T(8,128)(2,1)}, bf16[128,256]{1,0:T(8,128)(2,1)}, u32[]{:S(2)}, u32[]{:S(2)}) collective-permute-start(bf16[128,256]{1,0:T(8,128)(2,1)} %get-tuple-element.203), channel_id=1, source_target_pairs={{0,16},{4,20},{8,24},{12,28},{16,0},{20,4},{24,8},{28,12},{1,17},{... | collective-permute-start | bytes 196616 | tf_op jit(solution)/shard_map/ppermute | solution.py:303
  466.2 12.1 %collective-permute-start.55 = (bf16[384,128]{1,0:T(8,128)(2,1)}, bf16[384,128]{1,0:T(8,128)(2,1)}, u32[]{:S(2)}, u32[]{:S(2)}) collective-permute-start(bf16[384,128]{1,0:T(8,128)(2,1)} %get-tuple-element.195), channel_id=1, source_target_pairs={{0,8},{4,12},{8,0},{12,4},{16,24},{20,28},{24,16},{28,20},{1,9},{5... | collective-permute-start | bytes 294920 | tf_op jit(solution)/shard_map/ppermute | solution.py:303
  470.4 10.8 %collective-permute-start.57 = (bf16[384,128]{1,0:T(8,128)(2,1)}, bf16[384,128]{1,0:T(8,128)(2,1)S(1)}, u32[]{:S(2)}, u32[]{:S(2)}) collective-permute-start(bf16[384,128]{1,0:T(8,128)(2,1)} %get-tuple-element.196), channel_id=1, source_target_pairs={{0,24},{4,28},{8,16},{12,20},{16,8},{20,12},{24,0},{28,4},{1,25},{... | collective-permute-start | bytes 294920 | tf_op jit(solution)/shard_map/ppermute | solution.py:303
  473.0 10.4 %collective-permute-start.58 = (bf16[4,384,128]{2,1,0:T(8,128)(2,1)}, bf16[4,384,128]{2,1,0:T(8,128)(2,1)S(1)}, u32[]{:S(2)}, u32[]{:S(2)}) collective-permute-start(bf16[4,384,128]{2,1,0:T(8,128)(2,1)} %get-tuple-element.149), channel_id=1, source_target_pairs={{0,4},{4,0},{8,12},{12,8},{16,20},{20,16},{24,28},{28,24},{1,5},{5... | collective-permute-start | bytes 1179656 | tf_op jit(solution)/shard_map/ppermute | solution.py:303
  478.3 20.3 %collective-permute-start.52 = (bf16[512,1024]{1,0:T(8,128)(2,1)S(1)}, bf16[512,1024]{1,0:T(8,128)(2,1)}, u32[]{:S(2)}, u32[]{:S(2)}) collective-permute-start(bf16[512,1024]{1,0:T(8,128)(2,1)S(1)} %copy-done.32), channel_id=1, source_target_pairs={{0,1},{1,0},{2,3},{3,2},{4,5},{5,4},{6,7},{7,6},{8,9},{9,8},{10,11... | collective-permute-start | bytes 3145736 | tf_op jit(solution)/shard_map/ppermute | solution.py:303
  482.2 25.6 %collective-permute-start.53 = (bf16[512,1024]{1,0:T(8,128)(2,1)}, bf16[512,1024]{1,0:T(8,128)(2,1)}, u32[]{:S(2)}, u32[]{:S(2)}) collective-permute-start(bf16[512,1024]{1,0:T(8,128)(2,1)} %fusion.18), channel_id=1, source_target_pairs={{0,2},{1,3},{2,0},{3,1},{4,6},{5,7},{6,4},{7,5},{8,10},{9,11},{10,... | collective-permute-start | bytes 3145736 | tf_op jit(solution)/shard_map/ppermute | solution.py:303
  (94 other events, 787.6 us)
Sparse Core Ops, SparseCore 0:
  41.4 57.6 all-gather.1
  347.2 84.2 reduce-scatter.1

commit v2 on v1

--- a/solution.py
+++ b/solution.py
@@ -290,6 +290,7 @@
     )
 
 
+ROW, COL = "row", "col"
 BF = jnp.bfloat16
 F32 = jnp.float32
 MASKED = -1e30
@@ -304,10 +305,10 @@
 
 
 def row_blocks(block):
-    parts = [block] + [swap(block, "row", 2 * step) for step in range(1, 4)]
+    parts = [block] + [swap(block, ROW, 2 * step) for step in range(1, 4)]
     blocks = []
     for part in parts:
-        blocks += [part, swap(part, "row", 1)]
+        blocks += [part, swap(part, ROW, 1)]
     return blocks, parts
 
 
@@ -412,7 +413,6 @@
         cost_estimate=pl.CostEstimate(
             flops=2 * total * width * D, transcendentals=0, bytes_accessed=8 * total * D
         ),
-        name="project",
     )(row, *tokens, *weights, inner, outer, bias)
 
 
@@ -465,7 +465,6 @@
         cost_estimate=pl.CostEstimate(
             flops=16 * rows * rows * 128, transcendentals=0, bytes_accessed=8 * rows * 128
         ),
-        name="attend",
     )(query, keys, values)
 
 
@@ -546,7 +545,6 @@
         cost_estimate=pl.CostEstimate(
             flops=48 * rows * rows * HD, transcendentals=0, bytes_accessed=8 * rows * HD
         ),
-        name="attend_back",
     )(query, grad, exact, keys, values, inner, outer, *held)
 
 
@@ -633,7 +631,6 @@
         cost_estimate=pl.CostEstimate(
             flops=6 * size * hidden * D, transcendentals=0, bytes_accessed=6 * hidden * D
         ),
-        name="feed",
     )(row, *tokens, second, *firsts, *held)
 
 
@@ -678,7 +675,6 @@
         cost_estimate=pl.CostEstimate(
             flops=6 * size * hidden * D, transcendentals=0, bytes_accessed=6 * hidden * D
         ),
-        name="feed_back",
     )(*grads, slope, gelu, first, second, *held)
 
 
@@ -707,7 +703,6 @@
         grid_spec=pltpu.PrefetchScalarGridSpec(
             num_scalar_prefetch=1, grid=(4,), in_specs=in_specs, out_specs=out_specs
         ),
-        name="pack",
     )(row, *ins)
 
 
@@ -728,23 +723,19 @@
         grid=(blocks,),
         in_specs=[pl.BlockSpec((array.shape[0], 128), lambda k: (0, k)) for array in arrays],
         out_specs=pl.BlockSpec((1, rows, 128), lambda k: (k, 0, 0)),
-        name="stack",
     )(*arrays)
 
 
 def sum_far(near):
     total = near[0]
     for step in range(1, 4):
-        total = total + swap(near[step].astype(BF), "row", 2 * step).astype(F32)
+        total = total + swap(near[step].astype(BF), ROW, 2 * step).astype(F32)
     return total
 
 
 def add_all(values):
-    for axis in ("col", "row"):
-        flip = 1
-        while flip < lax.axis_size(axis):
-            values = values + swap(values, axis, flip)
-            flip *= 2
+    for axis, flip in ((ROW, 2), (ROW, 4), (COL, 1), (ROW, 1), (COL, 2)):
+        values = values + swap(values, axis, flip)
     return values
 
 
@@ -760,11 +751,11 @@
     feed_out,
 ):
     own = hidden_in.shape[0]
-    column = lax.axis_index("col")
-    row = lax.axis_index("row")
+    column = lax.axis_index(COL)
+    row = lax.axis_index(ROW)
     group = own * 4
     group_start = row * group
-    total_tokens = group * lax.axis_size("row")
+    total_tokens = group * lax.axis_size(ROW)
     valid_total = jnp.sum(valid_mask.astype(F32))
     live_group = lax.dynamic_slice_in_dim(valid_mask, group_start, group, 0)
     live_own = lax.dynamic_slice_in_dim(live_group, column * own, own, 0).astype(F32)
@@ -782,18 +773,18 @@
     inputs = hidden_in.astype(F32)
     normed_one, inverse_one, low_one = layer_norm(inputs, first_gain)
     width = attention_in.shape[1]
-    out_twin = swap(attention_out, "col", 2)
+    out_twin = swap(attention_out, COL, 2)
     joint_blocks, joint_parts = row_blocks(attention_in.reshape(3 * width, attention_in.shape[2]))
-    far = swap(low_one, "col", 2)
-    near = swap(low_one, "col", 1)
+    far = swap(low_one, COL, 2)
+    near = swap(low_one, COL, 1)
     hidden = feed_in.shape[1]
     index = row.reshape(1)
     feed_in, feed_out, attention_out, out_twin, *_ = lax.optimization_barrier(
         (feed_in, feed_out, attention_out, out_twin, *joint_parts)
     )
-    tokens = [low_one, near, far, swap(far, "col", 1)]
+    tokens = [low_one, near, far, swap(far, COL, 1)]
     out_rows = lax.all_gather(
-        jnp.concatenate([attention_out, out_twin, feed_out], axis=1), "row", axis=0, tiled=True
+        jnp.concatenate([attention_out, out_twin, feed_out], axis=1), ROW, axis=0, tiled=True
     )
     feed_in_blocks, _ = row_blocks(feed_in.reshape(2 * hidden, 128))
     all_low_one, joint, query, keys, values = project(
@@ -805,7 +796,7 @@
         mixed.append(pair_mixed)
         exact.append(pair_exact)
         query_back.append(pair_query)
-        mixed_twin.append(swap(pair_mixed[2 * own :], "col", 2))
+        mixed_twin.append(swap(pair_mixed[2 * own :], COL, 2))
     mixed = jnp.concatenate([m[: 2 * own] for m in mixed], axis=1)
     mixed_twin = jnp.concatenate(mixed_twin, axis=1)
     attention_rows = out_rows[:, :width]
@@ -815,7 +806,7 @@
     near = dot(mixed_own[own:], attention_rows, ROW_DIMS) + dot(
         mixed_twin[own:], attention_twin, ROW_DIMS
     )
-    near = swap(near, "col", 1)
+    near = swap(near, COL, 1)
     branch = (
         dot(mixed_own[:own], attention_rows, ROW_DIMS)
         + dot(mixed_twin[:own], attention_twin, ROW_DIMS)
@@ -827,15 +818,15 @@
     chunks = 2
     size = own // chunks
     parts = [slice(i * size, (i + 1) * size) for i in range(chunks)]
-    far = [swap(low_two[here], "col", 2) for here in parts]
+    far = [swap(low_two[here], COL, 2) for here in parts]
     near = []
     for here in parts:
-        near += [low_two[here], swap(low_two[here], "col", 1)]
+        near += [low_two[here], swap(low_two[here], COL, 1)]
     *kept, keep_near, send_near, feed_in_rows = feed(
         index, near, feed_in_blocks, feed_out_rows, group, 0, []
     )
     far[0], kept[0] = lax.optimization_barrier((far[0], kept[0]))
-    got_near = swap(send_near, "col", 1)
+    got_near = swap(send_near, COL, 1)
     sums = []
     gate_to = None
     for i in range(chunks):
@@ -843,17 +834,17 @@
         if gate_to is not None:
             there, gate_to = lax.optimization_barrier((there, gate_to))
             sums[-1] = gate_to
-        there = [there, swap(there, "col", 1)]
+        there = [there, swap(there, COL, 1)]
         *kept, keep, send = feed(
             index, there, [feed_in_rows], feed_out_rows, group, 2 * chunks + 2 * i, kept
         )
-        gate_to = (keep + swap(send, "col", 1).astype(F32)).astype(BF)
+        gate_to = (keep + swap(send, COL, 1).astype(F32)).astype(BF)
         sums.append(gate_to)
     all_low_two, act, slope, gelu = kept
     squares = jnp.float32(0.0)
     results, grad_results, far, held, nears = [], [], [], [], []
     for i, here in enumerate(parts):
-        got_far = swap(sums[i], "col", 2)
+        got_far = swap(sums[i], COL, 2)
         if held:
             got_far, held[0] = lax.optimization_barrier((got_far, held[0]))
         result = (
@@ -869,10 +860,10 @@
         grad_result = (total_tokens * live_here)[:, None] * error_term / valid_total
         grad_results.append(grad_result)
         low = grad_result.astype(BF)
-        far.append(swap(low, "col", 2))
-        low = [low, swap(low, "col", 1)]
+        far.append(swap(low, COL, 2))
+        low = [low, swap(low, COL, 1)]
         *held, keep, send = feed_back(low, slope, gelu, feed_in_rows, feed_out_rows, 2 * i, held)
-        nears.append(keep + swap(send, "col", 1).astype(F32))
+        nears.append(keep + swap(send, COL, 1).astype(F32))
     sums = []
     gate_to = None
     for i in range(chunks):
@@ -880,7 +871,7 @@
         if gate_to is not None:
             there, gate_to = lax.optimization_barrier((there, gate_to))
             sums[-1] = gate_to
-        there = [there, swap(there, "col", 1)]
+        there = [there, swap(there, COL, 1)]
         *held, keep, send = feed_back(
             there,
             slope,
@@ -890,18 +881,17 @@
             2 * chunks + 2 * i,
             held,
         )
-        gate_to = (keep + swap(send, "col", 1).astype(F32)).astype(BF)
+        gate_to = (keep + swap(send, COL, 1).astype(F32)).astype(BF)
         sums.append(gate_to)
     all_grads, grad_hidden = held
     all_grads, grad_hidden, gate_to = lax.optimization_barrier((all_grads, grad_hidden, gate_to))
     sums[-1] = gate_to
-    grad_out = dot(act, all_grads, HEAD_DIMS).astype(BF)
     grad_feed = jnp.einsum("irf,rd->ifd", grad_hidden, all_low_two, preferred_element_type=F32)
-    grad_feed = stack_wide([grad_feed.astype(BF).reshape(2 * hidden, D), grad_out])
+    grad_feed = grad_feed.astype(BF).reshape(2 * hidden, D)
     grad_second = jnp.zeros((D,), F32)
     grad_middles = []
     for i, here in enumerate(parts):
-        got_far = swap(sums[i], "col", 2)
+        got_far = swap(sums[i], COL, 2)
         if i == chunks - 1:
             got_far, grad_feed = lax.optimization_barrier((got_far, grad_feed))
         grad_low_two = nears[i] + got_far.astype(F32)
@@ -914,15 +904,18 @@
     grad_middle = jnp.concatenate(grad_middles, axis=0)
     grad_branch = grad_middle.astype(BF)
 
-    branch_pair = jnp.concatenate([grad_branch, swap(grad_branch, "col", 1)], axis=0)
-    grad_mixed_twin = swap(dot(branch_pair, attention_twin, PLAIN_DIMS).astype(BF), "col", 2)
+    grad_branch, all_grads = lax.optimization_barrier((grad_branch, all_grads))
+    grad_out = dot(act, all_grads, HEAD_DIMS).astype(BF)
+    branch_pair = jnp.concatenate([grad_branch, swap(grad_branch, COL, 1)], axis=0)
+    grad_mixed_twin = swap(dot(branch_pair, attention_twin, PLAIN_DIMS).astype(BF), COL, 2)
+    grad_feed = stack_wide([grad_feed, grad_out])
     grad_mixed = jnp.concatenate(
         [dot(branch_pair, attention_rows, PLAIN_DIMS).astype(BF), grad_mixed_twin], axis=0
     )
-    grad_attention_far = swap(dot(branch_pair, mixed_twin, HEAD_DIMS).astype(BF), "col", 2)
+    grad_attention_far = swap(dot(branch_pair, mixed_twin, HEAD_DIMS).astype(BF), COL, 2)
     grad_attention = dot(branch_pair, mixed_own, HEAD_DIMS) + grad_attention_far.astype(F32)
     attention_keep, attention_send = pack(index, [grad_attention.astype(BF)], [])
-    near_attention = attention_keep.astype(F32) + swap(attention_send, "row", 1).astype(F32)
+    near_attention = attention_keep.astype(F32) + swap(attention_send, ROW, 1).astype(F32)
     held, joint_near = [], []
     grad_first = jnp.zeros((D,), F32)
     for pair in range(width // 128):
@@ -940,20 +933,26 @@
         held = [grad_joint]
         here = slice(pair * 384, (pair + 1) * 384)
         grad_pair = grad_joint[:, here]
-        if pair == width // 128 - 1:
-            part = dot(grad_joint[2 * own :], joint, PLAIN_DIMS)
-            far = part[:own] + swap(part[own:].astype(BF), "col", 1).astype(F32)
+        last = pair == width // 128 - 1
+        if last:
+            far = swap(dot(grad_joint[3 * own :], joint, PLAIN_DIMS).astype(BF), COL, 1)
+            far = dot(grad_joint[2 * own : 3 * own], joint, PLAIN_DIMS) + far.astype(F32)
             grad_pair, far = lax.optimization_barrier((grad_pair, far.astype(BF)))
         weight = dot(grad_pair, all_low_one, HEAD_DIMS)
         grad_first = grad_first + jnp.sum(weight * joint[here].astype(F32), axis=0)
-        keep, send = pack(index, [], [weight.astype(BF)])
-        near_sum = keep.astype(F32) + swap(send, "row", 1).astype(F32)
+        weight = weight.astype(BF)
+        keep, send = pack(index, [], [weight])
+        if last:
+            send, grad_joint, grad_first, joint_near[0] = lax.optimization_barrier(
+                (send, grad_joint, grad_first, joint_near[0])
+            )
+        near_sum = keep.astype(F32) + swap(send, ROW, 1).astype(F32)
         if pair == 0:
             held, send = lax.optimization_barrier((held, send))
         joint_near.append(near_sum)
-    part = dot(grad_joint[: 2 * own], joint, PLAIN_DIMS)
-    near = part[:own] + swap(part[own:].astype(BF), "col", 1).astype(F32)
-    grad_low_one = near + swap(far, "col", 2).astype(F32)
+    near = swap(dot(grad_joint[own : 2 * own], joint, PLAIN_DIMS).astype(BF), COL, 1)
+    near = dot(grad_joint[:own], joint, PLAIN_DIMS) + near.astype(F32)
+    grad_low_one = near + swap(far, COL, 2).astype(F32)
     grad_first = grad_first / first_gain
     totals = add_all(
         jnp.concatenate(
@@ -962,7 +961,7 @@
     )
     grad_input_norm, _ = norm_back(grad_low_one, normed_one, inverse_one, first_gain)
     grad_input = grad_middle + grad_input_norm
-    feed_sum = lax.psum_scatter(grad_feed, "row", scatter_dimension=0, tiled=True)
+    feed_sum = lax.psum_scatter(grad_feed, ROW, scatter_dimension=0, tiled=True)
     feed_sum = feed_sum.astype(F32).reshape(3 * hidden, 128)
     joint_sums = [sum_far(near).reshape(3, 128, 128) for near in joint_near]
     grads = (
@@ -987,8 +986,8 @@
 
 def shards(hidden_in, teacher, valid_mask, first_gain, second_gain, attention_in, *rest):
     fits = (
-        lax.axis_size("col") == 4
-        and lax.axis_size("row") == 8
+        lax.axis_size(COL) == 4
+        and lax.axis_size(ROW) == 8
         and hidden_in.shape[0] * 4 == SEQ_LEN
         and attention_in.shape[1] % 128 == 0
     )

time: 534 us -> 553 us (1.036)
  waiting for transfers between devices: 157 us -> 179 us
  other arithmetic: 50.7 us -> 44.5 us
  matrix products: 42.2 us -> 47.9 us
    ppermute x67, waiting for transfers between devices: 157 us -> 179 us  [swap(): lax.ppermute(values, axis, [(place, place ^ flip) for place in range(size)])]
    dot_general x13 -> x15, matrix products: 31.9 us -> 37.5 us  [dot(): return lax.dot_general(left, right, dims, preferred_element_type=F32)]
    unnamed x149 -> x132, local copies, waits for them, and re-layouts: 11.6 us -> 11 us
  transfers between devices with their start and end apart: 69 -> 69, of which waited for: 30 -> 31; matrix products, arithmetic and copies ran while one was open for 18% -> 17% of each run, Pallas kernels for 29% -> 28%
where the time goes in v2:
time: 553 us; the launch traced here: 543 us
  waiting for transfers between devices  179 us (32%)
  Pallas kernels  178 us (32%)
  starting transfers between devices  51.7 us (9%)
  matrix products  47.9 us (9%)
  other arithmetic  44.5 us (8%)
  local copies, waits for them, and re-layouts  22.6 us (4%)
  between operations  19.1 us (3%)
    ppermute x67, waiting for transfers between devices, swap(): lax.ppermute(values, axis, [(place, place ^ flip) for place in range(size)])  179 us
    pallas_call x2, Pallas kernels, attend_back_pair(): pl.pallas_call(attend_back_kernel, out_shape=jax.ShapeDtypeStruct((rows,...  52.7 us
    ppermute x67, starting transfers between devices, swap(): lax.ppermute(values, axis, [(place, place ^ flip) for place in range(size)])  51.6 us
    dot_general x15, matrix products, dot(): return lax.dot_general(left, right, dims, preferred_element_type=F32)  37.5 us
    pallas_call x4, Pallas kernels, feed_back(): pl.pallas_call(functools.partial(feed_back_kernel, count=count, held=len(...  35.9 us
    pallas_call x2, Pallas kernels, attend_pair(): pl.pallas_call(attend_kernel, out_shape=(jax.ShapeDtypeStruct((rows, 128)...  35.5 us
    pallas_call x3, Pallas kernels, feed(): pl.pallas_call(functools.partial(feed_kernel, count=count, blocks=blocks,...  27.5 us
  transfers between devices with their start and end apart: 69, of which 31 were waited for; matrix products, arithmetic and copies ran while one was open for 17% of the time, Pallas kernels for 28%

profile of v2, /device:TPU:0, one launch (start us, length us, event | category | flops | bytes accessed | tf_op | source)
XLA Modules:
  0.0 542.9 jit_solution(3288045036005165283)
XLA Ops:
  10.9 3.0 collective-permute-start.1
  14.0 3.6 collective-permute-start.8
  18.7 19.9 %collective-permute-done.10 = bf16[128,256]{1,0:T(8,128)(2,1)S(1)} collective-permute-done((bf16[128,256]{1,0:T(8,128)(2,1)S(1)}, bf16[128,256]{1,0:T(8,128)(2,1)S(1)}, u32[]{:S(2)}, u32[]{:S(2)}) %collective-permute-start.10) | collective-permute-done | bytes 65568 | tf_op jit(solution)/shard_map/ppermute | solution.py:304
  49.0 4.9 collective-permute-done.9.rest_7_
  53.9 7.1 %collective-permute-done.7.rest_5_ = bf16[768,128]{1,0:T(8,128)(2,1)S(1)} collective-permute-done((bf16[768,128]{1,0:T(8,128)(2,1)}, bf16[768,128]{1,0:T(8,128)(2,1)S(1)}, u32[]{:S(2)}, u32[]{:S(2)}) %collective-permute-start.7) | collective-permute-done | bytes 196640 | tf_op jit(solution)/shard_map/ppermute | solution.py:304
  61.0 3.3 collective-permute-done.5.rest_3_
  65.3 10.2 %shard_map.160 = (bf16[2048,1024]{1,0:T(8,128)(2,1)}, bf16[768,1024]{1,0:T(8,128)(2,1)}, bf16[4,2048,128]{2,1,0:T(8,128)(2,1)}, bf16[4,2048,128]{2,1,0:T(8,128)(2,1)}, bf16[4,2048,128]{2,1,0:T(8,128)(2,1)}) custom-call(s32[1]{0:T(128)} %bitcast.row_ref, bf16[512,1024]{1,0:T(8,128)(2,1)} %copy-done.22, bf16[512,1024]{1,0:T(8,128)(2,1)} %collective-permute-done.x1, ...), custom_call_target="tpu_custom_call" | custom-call | flops 3221225472 | bytes 16777216 | tf_op jit(solution)/shard_map/pallas_call | solution.py:390
  75.5 17.7 %shard_map.161 = (bf16[2048,128]{1,0:T(8,128)(2,1)}, f32[2048,128]{1,0:T(8,128)}, bf16[2,2048,128]{2,1,0:T(8,128)(2,1)}) custom-call(bf16[4,2048,128]{2,1,0:T(8,128)(2,1)} %get-tuple-element.87.query, bf16[4,2048,128]{2,1,0:T(8,128)(2,1)} %get-tuple-element.88.keys, bf16[4,2048,128]{2,1,0:T(8,128)(2,1)} %get-tuple-element.89.values), custom_call_target="tpu_custom_call" | custom-call | flops 8589934592 | bytes 2097152 | tf_op jit(solution)/shard_map/pallas_call | solution.py:455
  95.7 17.9 %shard_map.162 = (bf16[2048,128]{1,0:T(8,128)(2,1)}, f32[2048,128]{1,0:T(8,128)}, bf16[2,2048,128]{2,1,0:T(8,128)(2,1)}) custom-call(bf16[4,2048,128]{2,1,0:T(8,128)(2,1)} %get-tuple-element.87.query, bf16[4,2048,128]{2,1,0:T(8,128)(2,1)} %get-tuple-element.88.keys, bf16[4,2048,128]{2,1,0:T(8,128)(2,1)} %get-tuple-element.89.values), custom_call_target="tpu_custom_call" | custom-call | flops 8589934592 | bytes 2097152 | tf_op jit(solution)/shard_map/pallas_call | solution.py:455
  115.3 6.6 %collective-permute-done.12 = bf16[1024,128]{1,0:T(8,128)(2,1)S(1)} collective-permute-done((bf16[1024,128]{1,0:T(8,128)(2,1)S(1)}, bf16[1024,128]{1,0:T(8,128)(2,1)S(1)}, u32[]{:S(2)}, u32[]{:S(2)}) %collective-permute-start.12) | collective-permute-done | bytes 262176 | tf_op jit(solution)/shard_map/ppermute | solution.py:304
  125.1 3.6 collective-permute-start.21
  134.7 3.1 collective-permute-done.21.refs_11_
  137.8 19.7 %collective-permute-done.19.refs_9_ = bf16[1312,128]{1,0:T(8,128)(2,1)S(1)} collective-permute-done((bf16[1312,128]{1,0:T(8,128)(2,1)S(1)}, bf16[1312,128]{1,0:T(8,128)(2,1)S(1)}, u32[]{:S(2)}, u32[]{:S(2)}) %collective-permute-start.19) | collective-permute-done | bytes 335904 | tf_op jit(solution)/shard_map/ppermute | solution.py:304
  160.0 8.2 %collective-permute-done.22.refs_12_ = bf16[1312,128]{1,0:T(8,128)(2,1)S(1)} collective-permute-done((bf16[1312,128]{1,0:T(8,128)(2,1)S(1)}, bf16[1312,128]{1,0:T(8,128)(2,1)S(1)}, u32[]{:S(2)}, u32[]{:S(2)}) %collective-permute-start.22) | collective-permute-done | bytes 335904 | tf_op jit(solution)/shard_map/ppermute | solution.py:304
  170.0 5.4 collective-permute-done.20.refs_10_
  175.4 5.4 %collective-permute-done.18.refs_8_ = bf16[1312,128]{1,0:T(8,128)(2,1)S(1)} collective-permute-done((bf16[1312,128]{1,0:T(8,128)(2,1)S(1)}, bf16[1312,128]{1,0:T(8,128)(2,1)S(1)}, u32[]{:S(2)}, u32[]{:S(2)}) %collective-permute-start.18) | collective-permute-done | bytes 335904 | tf_op jit(solution)/shard_map/ppermute | solution.py:304
  181.6 12.7 %shard_map.163 = (bf16[2048,1024]{1,0:T(8,128)(2,1)}, bf16[2048,656]{1,0:T(8,128)(2,1)}, bf16[2048,656]{1,0:T(8,128)(2,1)}, bf16[2048,656]{1,0:T(8,128)(2,1)}, f...) custom-call(s32[1]{0:T(128)} %bitcast.row_ref, ...), custom_call_target="tpu_custom_call" | custom-call | flops 4127195136 | bytes 4030464 | tf_op jit(solution)/shard_map/pallas_call | solution.py:610
  196.6 7.4 %shard_map.164 = (bf16[2048,1024]{1,0:T(8,128)(2,1)}, bf16[2048,656]{1,0:T(8,128)(2,1)}, bf16[2048,656]{1,0:T(8,128)(2,1)}, bf16[2048,656]{1,0:T(8,128)(2,1)}, f...) custom-call(s32[1]{0:T(128)} %bitcast.row_ref, ...), custom_call_target="tpu_custom_call", output_to_operand_aliasing={{0}: (5, {}), {1}: (6, {}), {2}: (7, {}), {3}: (8, {})} | custom-call | flops 2063597568 | bytes 4030464 | tf_op jit(solution)/shard_map/pallas_call | solution.py:610
  208.4 10.3 %collective-permute-done.24.refs_0_ = bf16[256,1024]{1,0:T(8,128)(2,1)} collective-permute-done((bf16[256,1024]{1,0:T(8,128)(2,1)}, bf16[256,1024]{1,0:T(8,128)(2,1)}, u32[]{:S(2)}, u32[]{:S(2)}) %collective-permute-start.24) | collective-permute-done | bytes 524320 | tf_op jit(solution)/shard_map/ppermute | solution.py:304
  221.0 7.4 %shard_map.165 = (bf16[2048,1024]{1,0:T(8,128)(2,1)}, bf16[2048,656]{1,0:T(8,128)(2,1)}, bf16[2048,656]{1,0:T(8,128)(2,1)}, bf16[2048,656]{1,0:T(8,128)(2,1)}, f...) custom-call(s32[1]{0:T(128)} %bitcast.row_ref, ...), custom_call_target="tpu_custom_call", output_to_operand_aliasing={{0}: (5, {}), {1}: (6, {}), {2}: (7, {}), {3}: (8, {})} | custom-call | flops 2063597568 | bytes 4030464 | tf_op jit(solution)/shard_map/pallas_call | solution.py:610
  228.5 5.5 %collective-permute-done.28 = bf16[256,1024]{1,0:T(8,128)(2,1)} collective-permute-done((bf16[256,1024]{1,0:T(8,128)(2,1)}, bf16[256,1024]{1,0:T(8,128)(2,1)}, u32[]{:S(2)}, u32[]{:S(2)}) %collective-permute-start.28) | collective-permute-done | bytes 524320 | tf_op jit(solution)/shard_map/ppermute | solution.py:304
  241.7 9.3 %shard_map.166 = (bf16[2048,1024]{1,0:T(8,128)(2,1)}, bf16[2,2048,656]{2,1,0:T(8,128)(2,1)}, f32[256,1024]{1,0:T(8,128)}, bf16[256,1024]{1,0:T(8,128)(2,1)}) custom-call(bf16[256,1024]{1,0:T(8,128)(2,1)} %fusion.60.refs_0_, bf16[256,1024]{1,0:T(8,128)(2,1)} %collective-permute-done.32.refs_1_, bf16[2048,656]{1,0:T(8,128)(2,1)} %get-tuple-element.115.refs_2_, ...), custom_call_target="tpu_custom_call" | custom-call | flops 2063597568 | bytes 4030464 | tf_op jit(solution)/shard_map/pallas_call | solution.py:661
  251.0 3.8 collective-permute-done.31
  254.8 3.1 multiply_reduce_fusion.3
  259.6 5.9 %collective-permute-done.35.refs_0_ = bf16[256,1024]{1,0:T(8,128)(2,1)} collective-permute-done((bf16[256,1024]{1,0:T(8,128)(2,1)}, bf16[256,1024]{1,0:T(8,128)(2,1)}, u32[]{:S(2)}, u32[]{:S(2)}) %collective-permute-start.35) | collective-permute-done | bytes 524320 | tf_op jit(solution)/shard_map/ppermute | solution.py:304
  266.3 8.9 %shard_map.167 = (bf16[2048,1024]{1,0:T(8,128)(2,1)}, bf16[2,2048,656]{2,1,0:T(8,128)(2,1)}, f32[256,1024]{1,0:T(8,128)}, bf16[256,1024]{1,0:T(8,128)(2,1)}) custom-call(bf16[256,1024]{1,0:T(8,128)(2,1)} %copy-done.17, bf16[256,1024]{1,0:T(8,128)(2,1)} %copy-done.28, ...), custom_call_target="tpu_custom_call", output_to_operand_aliasing={{0}: (6, {}), {1}: (7, {})} | custom-call | flops 2063597568 | bytes 4030464 | tf_op jit(solution)/shard_map/pallas_call | solution.py:661
  276.0 8.9 %shard_map.168 = (bf16[2048,1024]{1,0:T(8,128)(2,1)}, bf16[2,2048,656]{2,1,0:T(8,128)(2,1)}, f32[256,1024]{1,0:T(8,128)}, bf16[256,1024]{1,0:T(8,128)(2,1)}) custom-call(bf16[256,1024]{1,0:T(8,128)(2,1)} %collective-permute-done.35.refs_0_, bf16[256,1024]{1,0:T(8,128)(2,1)} %copy-done.27, ...), custom_call_target="tpu_custom_call", output_to_operand_aliasing={{0}: (6, {}), {1}: (7, {})} | custom-call | flops 2063597568 | bytes 4030464 | tf_op jit(solution)/shard_map/pallas_call | solution.py:661
  288.6 10.8 %collective-permute-done.34.refs_0_ = bf16[256,1024]{1,0:T(8,128)(2,1)S(1)} collective-permute-done((bf16[256,1024]{1,0:T(8,128)(2,1)S(1)}, bf16[256,1024]{1,0:T(8,128)(2,1)S(1)}, u32[]{:S(2)}, u32[]{:S(2)}) %collective-permute-start.34) | collective-permute-done | bytes 524320 | tf_op jit(solution)/shard_map/ppermute | solution.py:304
  302.1 8.9 %shard_map.169 = (bf16[2048,1024]{1,0:T(8,128)(2,1)}, bf16[2,2048,656]{2,1,0:T(8,128)(2,1)}, f32[256,1024]{1,0:T(8,128)}, bf16[256,1024]{1,0:T(8,128)(2,1)}) custom-call(bf16[256,1024]{1,0:T(8,128)(2,1)} %copy-done.26, bf16[256,1024]{1,0:T(8,128)(2,1)} %copy-done.29, ...), custom_call_target="tpu_custom_call", output_to_operand_aliasing={{0}: (6, {}), {1}: (7, {})} | custom-call | flops 2063597568 | bytes 4030464 | tf_op jit(solution)/shard_map/pallas_call | solution.py:661
  315.1 10.4 %fusion.7 = bf16[2,656,1024]{2,1,0:T(8,128)(2,1)} fusion(bf16[2,2048,656]{2,1,0:T(8,128)(2,1)} %get-tuple-element.139, bf16[2048,1024]{1,0:T(8,128)(2,1)} %get-tuple-element.140), kind=kOutput, calls=%fused_computation.11 | convolution fusion | flops 5504270336 | bytes 12255232 | tf_op jit(solution)/shard_map/irf,rd->ifd/dot_general | solution.py:889
  325.5 11.5 %collective-permute-done.43 = bf16[256,1024]{1,0:T(8,128)(2,1)S(1)} collective-permute-done((bf16[256,1024]{1,0:T(8,128)(2,1)S(1)}, bf16[256,1024]{1,0:T(8,128)(2,1)S(1)}, u32[]{:S(2)}, u32[]{:S(2)}) %collective-permute-start.43) | collective-permute-done | bytes 524320 | tf_op jit(solution)/shard_map/ppermute | solution.py:304
  344.1 4.0 convolution_convert_fusion.refs_1_
  348.1 6.5 %shard_map.175 = bf16[8,1968,128]{2,1,0:T(8,128)(2,1)} custom-call(bf16[1312,1024]{1,0:T(8,128)(2,1)} %bitcast.87, bf16[656,1024]{1,0:T(8,128)(2,1)} %convolution_convert_fusion.refs_1_), custom_call_target="tpu_custom_call" | custom-call | tf_op jit(solution)/shard_map/pallas_call | solution.py:720
  364.9 9.4 %collective-permute-done.45 = bf16[1024,256]{1,0:T(8,128)(2,1)S(1)} collective-permute-done((bf16[1024,256]{1,0:T(8,128)(2,1)S(1)}, bf16[1024,256]{1,0:T(8,128)(2,1)S(1)}, u32[]{:S(2)}, u32[]{:S(2)}) %collective-permute-start.45) | collective-permute-done | bytes 524320 | tf_op jit(solution)/shard_map/ppermute | solution.py:304
  375.5 26.2 %shard_map.170.refs_0_ = bf16[2048,768]{1,0:T(8,128)(2,1)} custom-call(bf16[2,2048,128]{2,1,0:T(8,128)(2,1)} %get-tuple-element.145.query, bf16[2048,256]{1,0:T(8,128)(2,1)} %pad_maximum_fusion.2.grad, f32[2048,128]{1,0:T(8,128)} %get-tuple-element.146.exact, bf16[4,2048,128]{2,1,0:T(8,128)(2,1)} %get-tuple-element.88.keys, ...), custom_call_target="tpu_custom_call" | custom-call | flops 12884901888 | bytes 1048576 | tf_op jit(solution)/shard_map/pallas_call | solution.py:528
  401.7 6.0 %fusion.71 = (bf16[384,1024]{1,0:T(8,128)(2,1)}, f32[384,1024]{1,0:T(8,128)}) fusion(bf16[2048,1024]{1,0:T(8,128)(2,1)} %get-tuple-element.147, bf16[2048,768]{1,0:T(8,128)(2,1)} %shard_map.170.refs_0_), kind=kOutput, calls=%fused_computation.171 | convolution fusion | flops 1611005952 | bytes 8126464 | tf_op jit(solution)/shard_map/dot_general | solution.py:316
  407.6 3.3 shard_map.171
  410.9 26.5 %shard_map.172 = bf16[2048,768]{1,0:T(8,128)(2,1)} custom-call(bf16[2,2048,128]{2,1,0:T(8,128)(2,1)} %get-tuple-element.119.query, bf16[2048,256]{1,0:T(8,128)(2,1)} %pad_maximum_fusion.2.grad, f32[2048,128]{1,0:T(8,128)} %get-tuple-element.144.exact, bf16[4,2048,128]{2,1,0:T(8,128)(2,1)} %get-tuple-element.88.keys, ...), custom_call_target="tpu_custom_call", output_to_operand_aliasing={{}: (7, {})} | custom-call | flops 12884901888 | bytes 1048576 | tf_op jit(solution)/shard_map/pallas_call | solution.py:528
  437.4 3.8 convolution_convert_fusion.2
  443.8 3.1 shard_map.174
  452.5 3.7 collective-permute-done.63
  458.8 5.4 %collective-permute-done.47 = bf16[4,384,128]{2,1,0:T(8,128)(2,1)S(1)} collective-permute-done((bf16[4,384,128]{2,1,0:T(8,128)(2,1)}, bf16[4,384,128]{2,1,0:T(8,128)(2,1)S(1)}, u32[]{:S(2)}, u32[]{:S(2)}) %collective-permute-start.47) | collective-permute-done | bytes 393248 | tf_op jit(solution)/shard_map/ppermute | solution.py:304
  465.2 3.6 add_convert_fusion
  471.5 3.5 shard_map.173
  494.4 3.1 convolution_convert_fusion.1
  499.3 3.6 collective-permute-done.58
  513.1 3.1 collective-permute-done.60
  517.0 9.7 %collective-permute-done.54 = bf16[512,1024]{1,0:T(8,128)(2,1)S(1)} collective-permute-done((bf16[512,1024]{1,0:T(8,128)(2,1)}, bf16[512,1024]{1,0:T(8,128)(2,1)S(1)}, u32[]{:S(2)}, u32[]{:S(2)}) %collective-permute-start.54) | collective-permute-done | bytes 1048608 | tf_op jit(solution)/shard_map/ppermute | solution.py:304
  (340 shorter events, 135.0 us)
Async XLA Ops:
  7.2 114.8 %all-gather.2.cloned.1.call-start = ((), (), s32[]{:S(2)}) async-start(), calls=%async_computation.1 | async-start | bytes 2949120 | tf_op jit(solution)/shard_map/all_gather | solution.py:786
  10.9 30.5 %collective-permute-start.1 = (bf16[512,1024]{1,0:T(8,128)(2,1)S(1)}, bf16[512,1024]{1,0:T(8,128)(2,1)}, u32[]{:S(2)}, u32[]{:S(2)}) collective-permute-start(bf16[512,1024]{1,0:T(8,128)(2,1)S(1)} %fusion.10.x0), channel_id=1, source_target_pairs={{0,2},{1,3},{2,0},{3,1},{4,6},{5,7},{6,4},{7,5},{8,10},{9,11},{10,... | collective-permute-start | bytes 3145736 | tf_op jit(solution)/shard_map/ppermute | solution.py:304
  14.0 26.3 %collective-permute-start.8 = (bf16[768,128]{1,0:T(8,128)(2,1)S(1)}, bf16[768,128]{1,0:T(8,128)(2,1)S(1)}, u32[]{:S(2)}, u32[]{:S(2)}) collective-permute-start(bf16[768,128]{1,0:T(8,128)(2,1)S(1)} %bitcast.99), channel_id=1, source_target_pairs={{0,24},{4,28},{8,16},{12,20},{16,8},{20,12},{24,0},{28,4},{1,25},{... | collective-permute-start | bytes 589832 | tf_op jit(solution)/shard_map/ppermute | solution.py:304
  17.6 22.7 %collective-permute-start.6 = (bf16[768,128]{1,0:T(8,128)(2,1)S(1)}, bf16[768,128]{1,0:T(8,128)(2,1)S(1)}, u32[]{:S(2)}, u32[]{:S(2)}) collective-permute-start(bf16[768,128]{1,0:T(8,128)(2,1)S(1)} %bitcast.100), channel_id=1, source_target_pairs={{0,16},{4,20},{8,24},{12,28},{16,0},{20,4},{24,8},{28,12},{1,17},{... | collective-permute-start | bytes 589832 | tf_op jit(solution)/shard_map/ppermute | solution.py:304
  17.6 22.8 %collective-permute-start.4 = (bf16[768,128]{1,0:T(8,128)(2,1)S(1)}, bf16[768,128]{1,0:T(8,128)(2,1)}, u32[]{:S(2)}, u32[]{:S(2)}) collective-permute-start(bf16[768,128]{1,0:T(8,128)(2,1)S(1)} %bitcast.101), channel_id=1, source_target_pairs={{0,8},{4,12},{8,0},{12,4},{16,24},{20,28},{24,16},{28,20},{1,9},{5... | collective-permute-start | bytes 589832 | tf_op jit(solution)/shard_map/ppermute | solution.py:304
  18.4 20.2 %collective-permute-start.10 = (bf16[128,256]{1,0:T(8,128)(2,1)S(1)}, bf16[128,256]{1,0:T(8,128)(2,1)S(1)}, u32[]{:S(2)}, u32[]{:S(2)}) collective-permute-start(bf16[128,256]{1,0:T(8,128)(2,1)S(1)} %copy-done.42), channel_id=1, source_target_pairs={{0,2},{1,3},{2,0},{3,1},{4,6},{5,7},{6,4},{7,5},{8,10},{9,11},{10,... | collective-permute-start | bytes 196616 | tf_op jit(solution)/shard_map/ppermute | solution.py:304
  38.5 8.8 %collective-permute-start.3 = (bf16[768,128]{1,0:T(8,128)(2,1)S(1)}, bf16[768,128]{1,0:T(8,128)(2,1)}, u32[]{:S(2)}, u32[]{:S(2)}) collective-permute-start(bf16[768,128]{1,0:T(8,128)(2,1)S(1)} %bitcast.102), channel_id=1, source_target_pairs={{0,4},{4,0},{8,12},{12,8},{16,20},{20,16},{24,28},{28,24},{1,5},{5... | collective-permute-start | bytes 589832 | tf_op jit(solution)/shard_map/ppermute | solution.py:304
  40.3 23.9 %collective-permute-start = (bf16[512,1024]{1,0:T(8,128)(2,1)S(1)}, bf16[512,1024]{1,0:T(8,128)(2,1)}, u32[]{:S(2)}, u32[]{:S(2)}) collective-permute-start(bf16[512,1024]{1,0:T(8,128)(2,1)S(1)} %fusion.10.x0), channel_id=1, source_target_pairs={{0,1},{1,0},{2,3},{3,2},{4,5},{5,4},{6,7},{7,6},{8,9},{9,8},{10,11... | collective-permute-start | bytes 3145736 | tf_op jit(solution)/shard_map/ppermute | solution.py:304
  41.3 490.4 %reduce-scatter.2.cloned.1.call-start = ((), (), s32[]{:S(2)}) async-start(), calls=%async_computation.2 | async-start | bytes 4534272 | tf_op jit(solution)/shard_map/reduce_scatter | solution.py:964
  41.4 22.8 %collective-permute-start.2 = (bf16[512,1024]{1,0:T(8,128)(2,1)}, bf16[512,1024]{1,0:T(8,128)(2,1)S(1)}, u32[]{:S(2)}, u32[]{:S(2)}) collective-permute-start(bf16[512,1024]{1,0:T(8,128)(2,1)} %collective-permute-done.1.x2), channel_id=1, source_target_pairs={{0,1},{1,0},{2,3},{3,2},{4,5},{5,4},{6,7},{7,6},{8,9},{9,8},{10,11... | collective-permute-start | bytes 3145736 | tf_op jit(solution)/shard_map/ppermute | solution.py:304
  45.5 15.5 %collective-permute-start.7 = (bf16[768,128]{1,0:T(8,128)(2,1)}, bf16[768,128]{1,0:T(8,128)(2,1)S(1)}, u32[]{:S(2)}, u32[]{:S(2)}) collective-permute-start(bf16[768,128]{1,0:T(8,128)(2,1)} %copy-done.60), channel_id=1, source_target_pairs={{0,4},{4,0},{8,12},{12,8},{16,20},{20,16},{24,28},{28,24},{1,5},{5... | collective-permute-start | bytes 589832 | tf_op jit(solution)/shard_map/ppermute | solution.py:304
  47.3 16.9 %collective-permute-start.5 = (bf16[768,128]{1,0:T(8,128)(2,1)}, bf16[768,128]{1,0:T(8,128)(2,1)S(1)}, u32[]{:S(2)}, u32[]{:S(2)}) collective-permute-start(bf16[768,128]{1,0:T(8,128)(2,1)} %collective-permute-done.4.rest_2_), channel_id=1, source_target_pairs={{0,4},{4,0},{8,12},{12,8},{16,20},{20,16},{24,28},{28,24},{1,5},{5... | collective-permute-start | bytes 589832 | tf_op jit(solution)/shard_map/ppermute | solution.py:304
  94.2 21.1 %collective-permute-start.11 = (bf16[1024,128]{1,0:T(8,128)(2,1)S(1)}, bf16[1024,128]{1,0:T(8,128)(2,1)S(1)}, u32[]{:S(2)}, u32[]{:S(2)}) collective-permute-start(bf16[1024,128]{1,0:T(8,128)(2,1)S(1)} %get-tuple-element.202), channel_id=1, source_target_pairs={{0,2},{1,3},{2,0},{3,1},{4,6},{5,7},{6,4},{7,5},{8,10},{9,11},{10,... | collective-permute-start | bytes 786440 | tf_op jit(solution)/shard_map/ppermute | solution.py:304
  125.1 12.7 %collective-permute-start.21 = (bf16[1312,128]{1,0:T(8,128)(2,1)S(1)}, bf16[1312,128]{1,0:T(8,128)(2,1)S(1)}, u32[]{:S(2)}, u32[]{:S(2)}) collective-permute-start(bf16[1312,128]{1,0:T(8,128)(2,1)S(1)} %bitcast.94), channel_id=1, source_target_pairs={{0,24},{4,28},{8,16},{12,20},{16,8},{20,12},{24,0},{28,4},{1,25},{... | collective-permute-start | bytes 1007624 | tf_op jit(solution)/shard_map/ppermute | solution.py:304
  128.7 28.8 %collective-permute-start.19 = (bf16[1312,128]{1,0:T(8,128)(2,1)S(1)}, bf16[1312,128]{1,0:T(8,128)(2,1)S(1)}, u32[]{:S(2)}, u32[]{:S(2)}) collective-permute-start(bf16[1312,128]{1,0:T(8,128)(2,1)S(1)} %bitcast.95), channel_id=1, source_target_pairs={{0,16},{4,20},{8,24},{12,28},{16,0},{20,4},{24,8},{28,12},{1,17},{... | collective-permute-start | bytes 1007624 | tf_op jit(solution)/shard_map/ppermute | solution.py:304
  128.7 29.3 %collective-permute-start.17 = (bf16[1312,128]{1,0:T(8,128)(2,1)S(1)}, bf16[1312,128]{1,0:T(8,128)(2,1)S(1)}, u32[]{:S(2)}, u32[]{:S(2)}) collective-permute-start(bf16[1312,128]{1,0:T(8,128)(2,1)S(1)} %bitcast.96), channel_id=1, source_target_pairs={{0,8},{4,12},{8,0},{12,4},{16,24},{20,28},{24,16},{28,20},{1,9},{5... | collective-permute-start | bytes 1007624 | tf_op jit(solution)/shard_map/ppermute | solution.py:304
  129.5 30.0 %collective-permute-start.16 = (bf16[1312,128]{1,0:T(8,128)(2,1)S(1)}, bf16[1312,128]{1,0:T(8,128)(2,1)S(1)}, u32[]{:S(2)}, u32[]{:S(2)}) collective-permute-start(bf16[1312,128]{1,0:T(8,128)(2,1)S(1)} %bitcast.97), channel_id=1, source_target_pairs={{0,4},{4,0},{8,12},{12,8},{16,20},{20,16},{24,28},{28,24},{1,5},{5... | collective-permute-start | bytes 1007624 | tf_op jit(solution)/shard_map/ppermute | solution.py:304
  134.7 46.2 %collective-permute-start.14 = (bf16[256,1024]{1,0:T(8,128)(2,1)}, bf16[256,1024]{1,0:T(8,128)(2,1)}, u32[]{:S(2)}, u32[]{:S(2)}) collective-permute-start(bf16[256,1024]{1,0:T(8,128)(2,1)} %get-tuple-element.194.refs_0_), channel_id=1, source_target_pairs={{0,1},{1,0},{2,3},{3,2},{4,5},{5,4},{6,7},{7,6},{8,9},{9,8},{10,11... | collective-permute-start | bytes 1572872 | tf_op jit(solution)/shard_map/ppermute | solution.py:304
  137.8 43.8 %collective-permute-start.15 = (bf16[256,1024]{1,0:T(8,128)(2,1)S(1)}, bf16[256,1024]{1,0:T(8,128)(2,1)}, u32[]{:S(2)}, u32[]{:S(2)}) collective-permute-start(bf16[256,1024]{1,0:T(8,128)(2,1)S(1)} %get-tuple-element.195.refs_2_), channel_id=1, source_target_pairs={{0,1},{1,0},{2,3},{3,2},{4,5},{5,4},{6,7},{7,6},{8,9},{9,8},{10,11... | collective-permute-start | bytes 1572872 | tf_op jit(solution)/shard_map/ppermute | solution.py:304
  157.5 10.8 %collective-permute-start.22 = (bf16[1312,128]{1,0:T(8,128)(2,1)S(1)}, bf16[1312,128]{1,0:T(8,128)(2,1)S(1)}, u32[]{:S(2)}, u32[]{:S(2)}) collective-permute-start(bf16[1312,128]{1,0:T(8,128)(2,1)S(1)} %collective-permute-done.21.refs_11_), channel_id=1, source_target_pairs={{0,4},{4,0},{8,12},{12,8},{16,20},{20,16},{24,28},{28,24},{1,5},{5... | collective-permute-start | bytes 1007624 | tf_op jit(solution)/shard_map/ppermute | solution.py:304
  158.0 17.4 %collective-permute-start.20 = (bf16[1312,128]{1,0:T(8,128)(2,1)S(1)}, bf16[1312,128]{1,0:T(8,128)(2,1)S(1)}, u32[]{:S(2)}, u32[]{:S(2)}) collective-permute-start(bf16[1312,128]{1,0:T(8,128)(2,1)S(1)} %collective-permute-done.19.refs_9_), channel_id=1, source_target_pairs={{0,4},{4,0},{8,12},{12,8},{16,20},{20,16},{24,28},{28,24},{1,5},{5... | collective-permute-start | bytes 1007624 | tf_op jit(solution)/shard_map/ppermute | solution.py:304
  159.5 21.4 %collective-permute-start.18 = (bf16[1312,128]{1,0:T(8,128)(2,1)S(1)}, bf16[1312,128]{1,0:T(8,128)(2,1)S(1)}, u32[]{:S(2)}, u32[]{:S(2)}) collective-permute-start(bf16[1312,128]{1,0:T(8,128)(2,1)S(1)} %collective-permute-done.17.refs_7_), channel_id=1, source_target_pairs={{0,4},{4,0},{8,12},{12,8},{16,20},{20,16},{24,28},{28,24},{1,5},{5... | collective-permute-start | bytes 1007624 | tf_op jit(solution)/shard_map/ppermute | solution.py:304
  168.2 26.1 %collective-permute-start.25 = (bf16[256,1024]{1,0:T(8,128)(2,1)}, bf16[256,1024]{1,0:T(8,128)(2,1)}, u32[]{:S(2)}, u32[]{:S(2)}) collective-permute-start(bf16[256,1024]{1,0:T(8,128)(2,1)} %get-tuple-element.194.refs_0_), channel_id=1, source_target_pairs={{0,2},{1,3},{2,0},{3,1},{4,6},{5,7},{6,4},{7,5},{8,10},{9,11},{10,... | collective-permute-start | bytes 1572872 | tf_op jit(solution)/shard_map/ppermute | solution.py:304
  204.2 14.5 %collective-permute-start.24 = (bf16[256,1024]{1,0:T(8,128)(2,1)}, bf16[256,1024]{1,0:T(8,128)(2,1)}, u32[]{:S(2)}, u32[]{:S(2)}) collective-permute-start(bf16[256,1024]{1,0:T(8,128)(2,1)} %copy-done.32), channel_id=1, source_target_pairs={{0,2},{1,3},{2,0},{3,1},{4,6},{5,7},{6,4},{7,5},{8,10},{9,11},{10,... | collective-permute-start | bytes 1572872 | tf_op jit(solution)/shard_map/ppermute | solution.py:304
  204.7 23.8 %collective-permute-start.23 = (bf16[512,1024]{1,0:T(8,128)(2,1)}, bf16[512,1024]{1,0:T(8,128)(2,1)}, u32[]{:S(2)}, u32[]{:S(2)}) collective-permute-start(bf16[512,1024]{1,0:T(8,128)(2,1)} %get-tuple-element.97), channel_id=1, source_target_pairs={{0,1},{1,0},{2,3},{3,2},{4,5},{5,4},{6,7},{7,6},{8,9},{9,8},{10,11... | collective-permute-start | bytes 3145736 | tf_op jit(solution)/shard_map/ppermute | solution.py:304
  219.3 14.7 %collective-permute-start.28 = (bf16[256,1024]{1,0:T(8,128)(2,1)}, bf16[256,1024]{1,0:T(8,128)(2,1)}, u32[]{:S(2)}, u32[]{:S(2)}) collective-permute-start(bf16[256,1024]{1,0:T(8,128)(2,1)} %add_convert_fusion.4), channel_id=1, source_target_pairs={{0,2},{1,3},{2,0},{3,1},{4,6},{5,7},{6,4},{7,5},{8,10},{9,11},{10,... | collective-permute-start | bytes 1572872 | tf_op jit(solution)/shard_map/ppermute | solution.py:304
  228.4 10.3 %collective-permute-start.30 = (bf16[256,1024]{1,0:T(8,128)(2,1)}, bf16[256,1024]{1,0:T(8,128)(2,1)S(1)}, u32[]{:S(2)}, u32[]{:S(2)}) collective-permute-start(bf16[256,1024]{1,0:T(8,128)(2,1)} %get-tuple-element.114), channel_id=1, source_target_pairs={{0,1},{1,0},{2,3},{3,2},{4,5},{5,4},{6,7},{7,6},{8,9},{9,8},{10,11... | collective-permute-start | bytes 1572872 | tf_op jit(solution)/shard_map/ppermute | solution.py:304
  239.6 15.1 %collective-permute-start.31 = (bf16[256,1024]{1,0:T(8,128)(2,1)}, bf16[256,1024]{1,0:T(8,128)(2,1)}, u32[]{:S(2)}, u32[]{:S(2)}) collective-permute-start(bf16[256,1024]{1,0:T(8,128)(2,1)} %add_convert_fusion.3), channel_id=1, source_target_pairs={{0,2},{1,3},{2,0},{3,1},{4,6},{5,7},{6,4},{7,5},{8,10},{9,11},{10,... | collective-permute-start | bytes 1572872 | tf_op jit(solution)/shard_map/ppermute | solution.py:304
  240.2 25.3 %collective-permute-start.35 = (bf16[256,1024]{1,0:T(8,128)(2,1)}, bf16[256,1024]{1,0:T(8,128)(2,1)}, u32[]{:S(2)}, u32[]{:S(2)}) collective-permute-start(bf16[256,1024]{1,0:T(8,128)(2,1)} %fusion.60.refs_0_), channel_id=1, source_target_pairs={{0,2},{1,3},{2,0},{3,1},{4,6},{5,7},{6,4},{7,5},{8,10},{9,11},{10,... | collective-permute-start | bytes 1572872 | tf_op jit(solution)/shard_map/ppermute | solution.py:304
  265.5 9.7 %collective-permute-start.36 = (bf16[256,1024]{1,0:T(8,128)(2,1)}, bf16[256,1024]{1,0:T(8,128)(2,1)S(1)}, u32[]{:S(2)}, u32[]{:S(2)}) collective-permute-start(bf16[256,1024]{1,0:T(8,128)(2,1)} %collective-permute-done.35.refs_0_), channel_id=1, source_target_pairs={{0,1},{1,0},{2,3},{3,2},{4,5},{5,4},{6,7},{7,6},{8,9},{9,8},{10,11... | collective-permute-start | bytes 1572872 | tf_op jit(solution)/shard_map/ppermute | solution.py:304
  285.4 13.9 %collective-permute-start.34 = (bf16[256,1024]{1,0:T(8,128)(2,1)S(1)}, bf16[256,1024]{1,0:T(8,128)(2,1)S(1)}, u32[]{:S(2)}, u32[]{:S(2)}) collective-permute-start(bf16[256,1024]{1,0:T(8,128)(2,1)S(1)} %copy-done.18), channel_id=1, source_target_pairs={{0,2},{1,3},{2,0},{3,1},{4,6},{5,7},{6,4},{7,5},{8,10},{9,11},{10,... | collective-permute-start | bytes 1572872 | tf_op jit(solution)/shard_map/ppermute | solution.py:304
  311.1 26.0 %collective-permute-start.33 = (bf16[256,1024]{1,0:T(8,128)(2,1)}, bf16[256,1024]{1,0:T(8,128)(2,1)S(1)}, u32[]{:S(2)}, u32[]{:S(2)}) collective-permute-start(bf16[256,1024]{1,0:T(8,128)(2,1)} %get-tuple-element.121), channel_id=1, source_target_pairs={{0,1},{1,0},{2,3},{3,2},{4,5},{5,4},{6,7},{7,6},{8,9},{9,8},{10,11... | collective-permute-start | bytes 1572872 | tf_op jit(solution)/shard_map/ppermute | solution.py:304
  311.4 25.6 %collective-permute-start.40 = (bf16[256,1024]{1,0:T(8,128)(2,1)}, bf16[256,1024]{1,0:T(8,128)(2,1)S(1)}, u32[]{:S(2)}, u32[]{:S(2)}) collective-permute-start(bf16[256,1024]{1,0:T(8,128)(2,1)} %get-tuple-element.130), channel_id=1, source_target_pairs={{0,1},{1,0},{2,3},{3,2},{4,5},{5,4},{6,7},{7,6},{8,9},{9,8},{10,11... | collective-permute-start | bytes 1572872 | tf_op jit(solution)/shard_map/ppermute | solution.py:304
  311.6 25.4 %collective-permute-start.39 = (bf16[256,1024]{1,0:T(8,128)(2,1)S(1)}, bf16[256,1024]{1,0:T(8,128)(2,1)S(1)}, u32[]{:S(2)}, u32[]{:S(2)}) collective-permute-start(bf16[256,1024]{1,0:T(8,128)(2,1)S(1)} %add_convert_fusion.2), channel_id=1, source_target_pairs={{0,2},{1,3},{2,0},{3,1},{4,6},{5,7},{6,4},{7,5},{8,10},{9,11},{10,... | collective-permute-start | bytes 1572872 | tf_op jit(solution)/shard_map/ppermute | solution.py:304
  314.4 22.6 %collective-permute-start.43 = (bf16[256,1024]{1,0:T(8,128)(2,1)S(1)}, bf16[256,1024]{1,0:T(8,128)(2,1)S(1)}, u32[]{:S(2)}, u32[]{:S(2)}) collective-permute-start(bf16[256,1024]{1,0:T(8,128)(2,1)S(1)} %add_convert_fusion.1), channel_id=1, source_target_pairs={{0,2},{1,3},{2,0},{3,1},{4,6},{5,7},{6,4},{7,5},{8,10},{9,11},{10,... | collective-permute-start | bytes 1572872 | tf_op jit(solution)/shard_map/ppermute | solution.py:304
  343.0 13.0 %collective-permute-start.44 = (bf16[512,1024]{1,0:T(8,128)(2,1)}, bf16[512,1024]{1,0:T(8,128)(2,1)}, u32[]{:S(2)}, u32[]{:S(2)}) collective-permute-start(bf16[512,1024]{1,0:T(8,128)(2,1)} %fusion.16), channel_id=1, source_target_pairs={{0,1},{1,0},{2,3},{3,2},{4,5},{5,4},{6,7},{7,6},{8,9},{9,8},{10,11... | collective-permute-start | bytes 3145736 | tf_op jit(solution)/shard_map/ppermute | solution.py:304
  359.5 14.9 %collective-permute-start.45 = (bf16[1024,256]{1,0:T(8,128)(2,1)S(1)}, bf16[1024,256]{1,0:T(8,128)(2,1)S(1)}, u32[]{:S(2)}, u32[]{:S(2)}) collective-permute-start(bf16[1024,256]{1,0:T(8,128)(2,1)S(1)} %convolution_convert_fusion.4), channel_id=1, source_target_pairs={{0,2},{1,3},{2,0},{3,1},{4,6},{5,7},{6,4},{7,5},{8,10},{9,11},{10,... | collective-permute-start | bytes 1572872 | tf_op jit(solution)/shard_map/ppermute | solution.py:304
  361.7 79.4 %collective-permute-start.62 = (bf16[1024,256]{1,0:T(8,128)(2,1)}, bf16[1024,256]{1,0:T(8,128)(2,1)}, u32[]{:S(2)}, u32[]{:S(2)}) collective-permute-start(bf16[1024,256]{1,0:T(8,128)(2,1)} %convolution_convert_fusion.3), channel_id=1, source_target_pairs={{0,2},{1,3},{2,0},{3,1},{4,6},{5,7},{6,4},{7,5},{8,10},{9,11},{10,... | collective-permute-start | bytes 1572872 | tf_op jit(solution)/shard_map/ppermute | solution.py:304
  441.1 24.0 %collective-permute-start.46 = (bf16[512,1024]{1,0:T(8,128)(2,1)}, bf16[512,1024]{1,0:T(8,128)(2,1)}, u32[]{:S(2)}, u32[]{:S(2)}) collective-permute-start(bf16[512,1024]{1,0:T(8,128)(2,1)} %convolution_convert_fusion.2), channel_id=1, source_target_pairs={{0,1},{1,0},{2,3},{3,2},{4,5},{5,4},{6,7},{7,6},{8,9},{9,8},{10,11... | collective-permute-start | bytes 3145736 | tf_op jit(solution)/shard_map/ppermute | solution.py:304
  446.8 9.4 %collective-permute-start.63 = (bf16[4,128,256]{2,1,0:T(8,128)(2,1)}, bf16[4,128,256]{2,1,0:T(8,128)(2,1)S(1)}, u32[]{:S(2)}, u32[]{:S(2)}) collective-permute-start(bf16[4,128,256]{2,1,0:T(8,128)(2,1)} %get-tuple-element.161), channel_id=1, source_target_pairs={{0,4},{4,0},{8,12},{12,8},{16,20},{20,16},{24,28},{28,24},{1,5},{5... | collective-permute-start | bytes 786440 | tf_op jit(solution)/shard_map/ppermute | solution.py:304
  449.4 14.8 %collective-permute-start.47 = (bf16[4,384,128]{2,1,0:T(8,128)(2,1)}, bf16[4,384,128]{2,1,0:T(8,128)(2,1)S(1)}, u32[]{:S(2)}, u32[]{:S(2)}) collective-permute-start(bf16[4,384,128]{2,1,0:T(8,128)(2,1)} %get-tuple-element.148), channel_id=1, source_target_pairs={{0,4},{4,0},{8,12},{12,8},{16,20},{20,16},{24,28},{28,24},{1,5},{5... | collective-permute-start | bytes 1179656 | tf_op jit(solution)/shard_map/ppermute | solution.py:304
  475.2 10.6 %collective-permute-start.64 = (bf16[128,256]{1,0:T(8,128)(2,1)S(1)}, bf16[128,256]{1,0:T(8,128)(2,1)S(1)}, u32[]{:S(2)}, u32[]{:S(2)}) collective-permute-start(bf16[128,256]{1,0:T(8,128)(2,1)S(1)} %get-tuple-element.210), channel_id=1, source_target_pairs={{0,8},{4,12},{8,0},{12,4},{16,24},{20,28},{24,16},{28,20},{1,9},{5... | collective-permute-start | bytes 196616 | tf_op jit(solution)/shard_map/ppermute | solution.py:304
  488.8 16.0 %collective-permute-start.55 = (bf16[384,128]{1,0:T(8,128)(2,1)}, bf16[384,128]{1,0:T(8,128)(2,1)}, u32[]{:S(2)}, u32[]{:S(2)}) collective-permute-start(bf16[384,128]{1,0:T(8,128)(2,1)} %get-tuple-element.204), channel_id=1, source_target_pairs={{0,8},{4,12},{8,0},{12,4},{16,24},{20,28},{24,16},{28,20},{1,9},{5... | collective-permute-start | bytes 294920 | tf_op jit(solution)/shard_map/ppermute | solution.py:304
  489.4 17.0 %collective-permute-start.57 = (bf16[384,128]{1,0:T(8,128)(2,1)}, bf16[384,128]{1,0:T(8,128)(2,1)}, u32[]{:S(2)}, u32[]{:S(2)}) collective-permute-start(bf16[384,128]{1,0:T(8,128)(2,1)} %get-tuple-element.205), channel_id=1, source_target_pairs={{0,24},{4,28},{8,16},{12,20},{16,8},{20,12},{24,0},{28,4},{1,25},{... | collective-permute-start | bytes 294920 | tf_op jit(solution)/shard_map/ppermute | solution.py:304
  491.9 17.0 %collective-permute-start.56 = (bf16[384,128]{1,0:T(8,128)(2,1)}, bf16[384,128]{1,0:T(8,128)(2,1)}, u32[]{:S(2)}, u32[]{:S(2)}) collective-permute-start(bf16[384,128]{1,0:T(8,128)(2,1)} %get-tuple-element.206), channel_id=1, source_target_pairs={{0,16},{4,20},{8,24},{12,28},{16,0},{20,4},{24,8},{28,12},{1,17},{... | collective-permute-start | bytes 294920 | tf_op jit(solution)/shard_map/ppermute | solution.py:304
  492.2 10.7 %collective-permute-start.58 = (bf16[4,384,128]{2,1,0:T(8,128)(2,1)}, bf16[4,384,128]{2,1,0:T(8,128)(2,1)}, u32[]{:S(2)}, u32[]{:S(2)}) collective-permute-start(bf16[4,384,128]{2,1,0:T(8,128)(2,1)} %get-tuple-element.159), channel_id=1, source_target_pairs={{0,4},{4,0},{8,12},{12,8},{16,20},{20,16},{24,28},{28,24},{1,5},{5... | collective-permute-start | bytes 1179656 | tf_op jit(solution)/shard_map/ppermute | solution.py:304
  497.5 19.5 %collective-permute-start.53 = (bf16[512,1024]{1,0:T(8,128)(2,1)}, bf16[512,1024]{1,0:T(8,128)(2,1)}, u32[]{:S(2)}, u32[]{:S(2)}) collective-permute-start(bf16[512,1024]{1,0:T(8,128)(2,1)} %convolution_convert_fusion.1), channel_id=1, source_target_pairs={{0,1},{1,0},{2,3},{3,2},{4,5},{5,4},{6,7},{7,6},{8,9},{9,8},{10,11... | collective-permute-start | bytes 3145736 | tf_op jit(solution)/shard_map/ppermute | solution.py:304
  502.9 23.8 %collective-permute-start.54 = (bf16[512,1024]{1,0:T(8,128)(2,1)}, bf16[512,1024]{1,0:T(8,128)(2,1)S(1)}, u32[]{:S(2)}, u32[]{:S(2)}) collective-permute-start(bf16[512,1024]{1,0:T(8,128)(2,1)} %add_convert_fusion), channel_id=1, source_target_pairs={{0,2},{1,3},{2,0},{3,1},{4,6},{5,7},{6,4},{7,5},{8,10},{9,11},{10,... | collective-permute-start | bytes 3145736 | tf_op jit(solution)/shard_map/ppermute | solution.py:304
  (85 other events, 784.6 us)
Sparse Core Ops, SparseCore 0:
  41.4 57.6 all-gather.1
  354.8 83.3 reduce-scatter.1
